TPU v7x, 32 devices: a whole 2x2x4 slice. The times are simulated.
32 devices in a mesh: dp: 2 (over x), seq: 16 (over z, y, core).
Axes of the slice: x: 2, y: 2, z: 4, core: 2. Of those that a mesh axis runs over, the one named last changes fastest.
Arguments:
- frames: bfloat16 [4, 1024, 1024], P('dp', 'seq'), may hold values from -6 to 6
- out_grad: bfloat16 [4, 1024, 1024], P('dp', 'seq'), may hold values from -6 to 6
- order: int32 [4], P('dp'), may hold values from 0 to 3, each once
- lengths: int32 [4], replicated, may hold values from 1 to 1024, 2560 in all
- first_gain: bfloat16 [1024], P(('dp', 'seq')), may hold values from 0.25 to 1.75
- first_shift: bfloat16 [1024], P(('dp', 'seq')), may hold values from -3 to 3
- query_weight: bfloat16 [1024, 1024], P(('dp', 'seq')), may hold values from -0.1875 to 0.1875
- query_bias: bfloat16 [1024], P(('dp', 'seq')), may hold values from -3 to 3
- key_weight: bfloat16 [1024, 1024], P(('dp', 'seq')), may hold values from -0.1875 to 0.1875
- value_weight: bfloat16 [1024, 1024], P(('dp', 'seq')), may hold values from -0.1875 to 0.1875
- value_bias: bfloat16 [1024], P(('dp', 'seq')), may hold values from -3 to 3
- output_weight: bfloat16 [1024, 1024], P(('dp', 'seq')), may hold values from -3 to 3
- output_bias: bfloat16 [1024], P(('dp', 'seq')), may hold values from -3 to 3
- second_gain: bfloat16 [1024], P(('dp', 'seq')), may hold values from 0.25 to 1.75
- second_shift: bfloat16 [1024], P(('dp', 'seq')), may hold values from -3 to 3
- up_weight: bfloat16 [1024, 4096], P(('dp', 'seq')), may hold values from -0.1875 to 0.1875
- up_bias: bfloat16 [4096], P(('dp', 'seq')), may hold values from -3 to 3
- down_weight: bfloat16 [4096, 1024], P(('dp', 'seq')), may hold values from -0.09375 to 0.09375
- down_bias: bfloat16 [1024], P(('dp', 'seq')), may hold values from -3 to 3
Outputs:
- output: bfloat16 [4, 1024, 1024], P('dp', 'seq')
- frames_grad: bfloat16 [4, 1024, 1024], P('dp', 'seq')
- first_gain_grad: float32 [1024], P(('dp', 'seq'))
- first_shift_grad: float32 [1024], P(('dp', 'seq'))
- query_weight_grad: float32 [1024, 1024], P(('dp', 'seq'))
- query_bias_grad: float32 [1024], P(('dp', 'seq'))
- key_weight_grad: float32 [1024, 1024], P(('dp', 'seq'))
- value_weight_grad: float32 [1024, 1024], P(('dp', 'seq'))
- value_bias_grad: float32 [1024], P(('dp', 'seq'))
- output_weight_grad: float32 [1024, 1024], P(('dp', 'seq'))
- output_bias_grad: float32 [1024], P(('dp', 'seq'))
- second_gain_grad: float32 [1024], P(('dp', 'seq'))
- second_shift_grad: float32 [1024], P(('dp', 'seq'))
- up_weight_grad: float32 [1024, 4096], P(('dp', 'seq'))
- up_bias_grad: float32 [4096], P(('dp', 'seq'))
- down_weight_grad: float32 [4096, 1024], P(('dp', 'seq'))
- down_bias_grad: float32 [1024], P(('dp', 'seq'))
Inputs may be any that keep to these rules, and one draw needn't show every extreme that they name: order[s] is the utterance held in slot s; each utterance is held by exactly one slot. lengths[u] counts the true frames of utterance u; frames from lengths[u] on are padding and are masked as keys; the longest utterance fills all 1024 frames.
All inputs are finite; a program needn't handle non-finite values.
Results may differ from a plain program's by a relative error of at most 0.012.
Values may be sent and summed in bfloat16 or wider, within the bound.
No kernel may reach another device: no remote copies, remote signals or barrier semaphores. Data moves between devices by JAX's collectives and lax.ppermute only.
A program may use at most 256 MiB of HBM per device.

v0:
```python
import jax
import jax.numpy as jnp
from jax import lax
from jax.sharding import PartitionSpec as P

HEADS = 16
HEAD = 64


norm_eps = 1e-05
inv_root_two = 0.7071067811865476
inv_root_tau = 0.3989422804014327


def normalize(rows):
    average = jnp.mean(rows, axis=-1, keepdims=True)
    centered = rows - average
    inv_std = lax.rsqrt(jnp.mean(centered * centered, axis=-1, keepdims=True) + norm_eps)
    return (centered * inv_std, inv_std)


def norm_back(grad_rows, scaled, inv_std, gain):
    grad_hat = grad_rows * gain
    return inv_std * (
        grad_hat
        - jnp.mean(grad_hat, axis=-1, keepdims=True)
        - scaled * jnp.mean(grad_hat * scaled, axis=-1, keepdims=True)
    )


def project(rows, weight):
    return jnp.einsum("ufd,de->ufe", rows, weight, preferred_element_type=jnp.float32)


def project_back(grads, weight):
    return jnp.einsum("ufe,de->ufd", grads, weight, preferred_element_type=jnp.float32)


def outer_sum(rows, grads):
    return jnp.einsum("ufd,ufe->de", rows, grads, preferred_element_type=jnp.float32)


def row_total(grads):
    return jnp.sum(grads.astype(jnp.float32), axis=(0, 1))


def gelu_slope(pre_act):
    cdf_part = 0.5 * (1.0 + lax.erf(pre_act * inv_root_two))
    return cdf_part + pre_act * jnp.exp(-0.5 * pre_act * pre_act) * inv_root_tau


def attend_forward(queries, keys_full, values_full, key_valid):
    slots, rows, width_all = queries.shape
    key_count = keys_full.shape[1]
    per_group = 4
    width = per_group * HEAD
    groups = HEADS // per_group

    def group_step(index, carry):
        mixed, log_sums = carry
        start = index * width
        q_group = lax.dynamic_slice_in_dim(queries, start, width, 2).reshape(
            slots, rows, per_group, HEAD
        )
        k_group = lax.dynamic_slice_in_dim(keys_full, start, width, 2).reshape(
            slots, key_count, per_group, HEAD
        )
        v_group = lax.dynamic_slice_in_dim(values_full, start, width, 2).reshape(
            slots, key_count, per_group, HEAD
        )
        scores = jnp.einsum("ufhe,ukhe->uhfk", q_group, k_group, preferred_element_type=jnp.float32)
        scores = jnp.where(key_valid[:, None, None, :], scores, jnp.float32(-1e30))
        row_max = jnp.max(scores, axis=-1, keepdims=True)
        exp_scores = jnp.exp(scores - row_max)
        row_sum = jnp.sum(exp_scores, axis=-1, keepdims=True)
        p_low = (exp_scores / row_sum).astype(jnp.bfloat16)
        o_group = jnp.einsum("uhfk,ukhe->ufhe", p_low, v_group, preferred_element_type=jnp.float32)
        mixed = lax.dynamic_update_slice_in_dim(
            mixed, o_group.reshape(slots, rows, width), start, 2
        )
        log_group = (row_max + jnp.log(row_sum))[..., 0]
        log_sums = lax.dynamic_update_slice_in_dim(log_sums, log_group, index * per_group, 1)
        return (mixed, log_sums)

    init = (
        jnp.zeros((slots, rows, width_all), jnp.float32),
        jnp.zeros((slots, HEADS, rows), jnp.float32),
    )
    mixed, log_sums = lax.fori_loop(0, groups, group_step, init)
    return (mixed.astype(jnp.bfloat16), log_sums)


def attend_backward(queries, keys_full, values_full, key_valid, log_sums, mixed_grad):
    slots, rows, width_all = queries.shape
    key_count = keys_full.shape[1]
    per_group = 4
    width = per_group * HEAD
    groups = HEADS // per_group

    def group_step(index, carry):
        q_grad, centres = carry
        start = index * width
        q_group = lax.dynamic_slice_in_dim(queries, start, width, 2).reshape(
            slots, rows, per_group, HEAD
        )
        k_group = lax.dynamic_slice_in_dim(keys_full, start, width, 2).reshape(
            slots, key_count, per_group, HEAD
        )
        v_group = lax.dynamic_slice_in_dim(values_full, start, width, 2).reshape(
            slots, key_count, per_group, HEAD
        )
        o_grad = lax.dynamic_slice_in_dim(mixed_grad, start, width, 2).reshape(
            slots, rows, per_group, HEAD
        )
        log_group = lax.dynamic_slice_in_dim(log_sums, index * per_group, per_group, 1)
        scores = jnp.einsum("ufhe,ukhe->uhfk", q_group, k_group, preferred_element_type=jnp.float32)
        probs = jnp.where(key_valid[:, None, None, :], jnp.exp(scores - log_group[..., None]), 0.0)
        p_grad = jnp.einsum("ufhe,ukhe->uhfk", o_grad, v_group, preferred_element_type=jnp.float32)
        centre = jnp.sum(probs * p_grad, axis=-1, keepdims=True)
        s_grad = (probs * (p_grad - centre)).astype(jnp.bfloat16)
        q_part = jnp.einsum("uhfk,ukhe->ufhe", s_grad, k_group, preferred_element_type=jnp.float32)
        q_grad = lax.dynamic_update_slice_in_dim(
            q_grad, q_part.reshape(slots, rows, width), start, 2
        )
        centres = lax.dynamic_update_slice_in_dim(centres, centre[..., 0], index * per_group, 1)
        return (q_grad, centres)

    init = (
        jnp.zeros((slots, rows, width_all), jnp.float32),
        jnp.zeros((slots, HEADS, rows), jnp.float32),
    )
    return lax.fori_loop(0, groups, group_step, init)


def key_side(queries_all, grads_all, log_all, centre_all, keys_local, values_local, valid_local):
    slots, rows, width_all = keys_local.shape
    query_count = queries_all.shape[1]
    per_group = 4
    width = per_group * HEAD
    groups = HEADS // per_group

    def group_step(index, carry):
        k_grad, v_grad = carry
        start = index * width
        q_group = lax.dynamic_slice_in_dim(queries_all, start, width, 2).reshape(
            slots, query_count, per_group, HEAD
        )
        o_grad = lax.dynamic_slice_in_dim(grads_all, start, width, 2).reshape(
            slots, query_count, per_group, HEAD
        )
        k_group = lax.dynamic_slice_in_dim(keys_local, start, width, 2).reshape(
            slots, rows, per_group, HEAD
        )
        v_group = lax.dynamic_slice_in_dim(values_local, start, width, 2).reshape(
            slots, rows, per_group, HEAD
        )
        log_group = lax.dynamic_slice_in_dim(log_all, index * per_group, per_group, 1)
        centre = lax.dynamic_slice_in_dim(centre_all, index * per_group, per_group, 1)
        scores = jnp.einsum("ufhe,ukhe->uhfk", q_group, k_group, preferred_element_type=jnp.float32)
        probs = jnp.where(
            valid_local[:, None, None, :], jnp.exp(scores - log_group[..., None]), 0.0
        )
        p_grad = jnp.einsum("ufhe,ukhe->uhfk", o_grad, v_group, preferred_element_type=jnp.float32)
        s_grad = (probs * (p_grad - centre[..., None])).astype(jnp.bfloat16)
        v_part = jnp.einsum(
            "uhfk,ufhe->ukhe",
            probs.astype(jnp.bfloat16),
            o_grad,
            preferred_element_type=jnp.float32,
        )
        k_part = jnp.einsum("uhfk,ufhe->ukhe", s_grad, q_group, preferred_element_type=jnp.float32)
        k_grad = lax.dynamic_update_slice_in_dim(
            k_grad, k_part.reshape(slots, rows, width), start, 2
        )
        v_grad = lax.dynamic_update_slice_in_dim(
            v_grad, v_part.reshape(slots, rows, width), start, 2
        )
        return (k_grad, v_grad)

    init = (
        jnp.zeros((slots, rows, width_all), jnp.float32),
        jnp.zeros((slots, rows, width_all), jnp.float32),
    )
    return lax.fori_loop(0, groups, group_step, init)


def on_device(
    frames,
    out_grad,
    order,
    lengths,
    first_gain,
    first_shift,
    query_weight,
    query_bias,
    key_weight,
    value_weight,
    value_bias,
    output_weight,
    output_bias,
    second_gain,
    second_shift,
    up_weight,
    up_bias,
    down_weight,
    down_bias,
):
    f32 = jnp.float32
    bf16 = jnp.bfloat16
    attn_params = (
        lax.all_gather(first_gain, ("dp", "seq"), axis=0, tiled=True),
        lax.all_gather(first_shift, ("dp", "seq"), axis=0, tiled=True),
        lax.all_gather(query_weight, ("dp", "seq"), axis=0, tiled=True),
        lax.all_gather(query_bias, ("dp", "seq"), axis=0, tiled=True),
        lax.all_gather(key_weight, ("dp", "seq"), axis=0, tiled=True),
        lax.all_gather(value_weight, ("dp", "seq"), axis=0, tiled=True),
        lax.all_gather(value_bias, ("dp", "seq"), axis=0, tiled=True),
        lax.all_gather(output_weight, ("dp", "seq"), axis=0, tiled=True),
        lax.all_gather(output_bias, ("dp", "seq"), axis=0, tiled=True),
    )
    gain_one, shift_one, w_query, b_query, w_key, w_value, b_value, w_output, b_output = attn_params
    rows_in = frames.astype(f32)
    scaled_one, inv_one = normalize(rows_in)
    h_first = (scaled_one * gain_one.astype(f32) + shift_one.astype(f32)).astype(bf16)
    queries = ((project(h_first, w_query) + b_query.astype(f32)) * 0.125).astype(bf16)
    keys_local = project(h_first, w_key).astype(bf16)
    values_local = (project(h_first, w_value) + b_value.astype(f32)).astype(bf16)
    keys_full, values_full = (
        lax.all_gather(keys_local, "seq", axis=1, tiled=True),
        lax.all_gather(values_local, "seq", axis=1, tiled=True),
    )
    slot_ids = jnp.arange(lengths.shape[0], dtype=jnp.int32)
    slot_lengths = jnp.sum(
        jnp.where(order[:, None] == slot_ids[None, :], lengths[None, :], 0), axis=1
    )
    key_valid = jnp.arange(keys_full.shape[1], dtype=jnp.int32)[None, :] < slot_lengths[:, None]
    mixed, log_sums = attend_forward(queries, keys_full, values_full, key_valid)
    middle = rows_in + project(mixed, w_output) + b_output.astype(f32)
    ffn_params = (
        lax.all_gather(second_gain, ("dp", "seq"), axis=0, tiled=True),
        lax.all_gather(second_shift, ("dp", "seq"), axis=0, tiled=True),
        lax.all_gather(up_weight, ("dp", "seq"), axis=0, tiled=True),
        lax.all_gather(up_bias, ("dp", "seq"), axis=0, tiled=True),
        lax.all_gather(down_weight, ("dp", "seq"), axis=0, tiled=True),
        lax.all_gather(down_bias, ("dp", "seq"), axis=0, tiled=True),
    )
    gain_two, shift_two, w_up, b_up, w_down, b_down = ffn_params
    scaled_two, inv_two = normalize(middle)
    h_second = (scaled_two * gain_two.astype(f32) + shift_two.astype(f32)).astype(bf16)
    pre_act = project(h_second, w_up) + b_up.astype(f32)
    act_low = jax.nn.gelu(pre_act, approximate=False).astype(bf16)
    output = (middle + project(act_low, w_down) + b_down.astype(f32)).astype(bf16)
    gain_two, shift_two, w_up, b_up, w_down, b_down = (
        lax.all_gather(second_gain, ("dp", "seq"), axis=0, tiled=True),
        lax.all_gather(second_shift, ("dp", "seq"), axis=0, tiled=True),
        lax.all_gather(up_weight, ("dp", "seq"), axis=0, tiled=True),
        lax.all_gather(up_bias, ("dp", "seq"), axis=0, tiled=True),
        lax.all_gather(down_weight, ("dp", "seq"), axis=0, tiled=True),
        lax.all_gather(down_bias, ("dp", "seq"), axis=0, tiled=True),
    )
    grad_rows = out_grad.astype(f32)
    down_bias_part = jnp.sum(grad_rows, axis=(0, 1))
    down_weight_part = outer_sum(act_low, out_grad)
    pre_grad = (project_back(out_grad, w_down) * gelu_slope(pre_act)).astype(bf16)
    up_bias_part = row_total(pre_grad)
    up_weight_part = outer_sum(h_second, pre_grad)
    h_second_grad = project_back(pre_grad, w_up)
    gain_two_part = jnp.sum(h_second_grad * scaled_two, axis=(0, 1))
    shift_two_part = jnp.sum(h_second_grad, axis=(0, 1))
    ffn_grads = (
        lax.psum_scatter(gain_two_part, ("dp", "seq"), scatter_dimension=0, tiled=True),
        lax.psum_scatter(shift_two_part, ("dp", "seq"), scatter_dimension=0, tiled=True),
        lax.psum_scatter(up_weight_part, ("dp", "seq"), scatter_dimension=0, tiled=True),
        lax.psum_scatter(up_bias_part, ("dp", "seq"), scatter_dimension=0, tiled=True),
        lax.psum_scatter(down_weight_part, ("dp", "seq"), scatter_dimension=0, tiled=True),
        lax.psum_scatter(down_bias_part, ("dp", "seq"), scatter_dimension=0, tiled=True),
    )
    middle_grad = grad_rows + norm_back(h_second_grad, scaled_two, inv_two, gain_two.astype(f32))
    gain_one, shift_one, w_query, b_query, w_key, w_value, b_value, w_output, b_output = (
        lax.all_gather(first_gain, ("dp", "seq"), axis=0, tiled=True),
        lax.all_gather(first_shift, ("dp", "seq"), axis=0, tiled=True),
        lax.all_gather(query_weight, ("dp", "seq"), axis=0, tiled=True),
        lax.all_gather(query_bias, ("dp", "seq"), axis=0, tiled=True),
        lax.all_gather(key_weight, ("dp", "seq"), axis=0, tiled=True),
        lax.all_gather(value_weight, ("dp", "seq"), axis=0, tiled=True),
        lax.all_gather(value_bias, ("dp", "seq"), axis=0, tiled=True),
        lax.all_gather(output_weight, ("dp", "seq"), axis=0, tiled=True),
        lax.all_gather(output_bias, ("dp", "seq"), axis=0, tiled=True),
    )
    branch_grad = middle_grad.astype(bf16)
    output_bias_part = row_total(branch_grad)
    output_weight_part = outer_sum(mixed, branch_grad)
    mixed_grad = project_back(branch_grad, w_output).astype(bf16)
    keys_full, values_full = (
        lax.all_gather(keys_local, "seq", axis=1, tiled=True),
        lax.all_gather(values_local, "seq", axis=1, tiled=True),
    )
    q_grad, centres = attend_backward(
        queries, keys_full, values_full, key_valid, log_sums, mixed_grad
    )
    queries_all, grads_all = (
        lax.all_gather(queries, "seq", axis=1, tiled=True),
        lax.all_gather(mixed_grad, "seq", axis=1, tiled=True),
    )
    log_all, centre_all = (
        lax.all_gather(log_sums, "seq", axis=2, tiled=True),
        lax.all_gather(centres, "seq", axis=2, tiled=True),
    )
    rows_here = keys_local.shape[1]
    positions = lax.axis_index("seq") * rows_here + jnp.arange(rows_here, dtype=jnp.int32)
    valid_local = positions[None, :] < slot_lengths[:, None]
    k_grad_own, v_grad_own = key_side(
        queries_all, grads_all, log_all, centre_all, keys_local, values_local, valid_local
    )
    k_grad = k_grad_own.astype(bf16)
    v_grad = v_grad_own.astype(bf16)
    q_pre_grad = q_grad.astype(bf16) * jnp.asarray(0.125, bf16)
    query_weight_part = outer_sum(h_first, q_pre_grad)
    query_bias_part = row_total(q_pre_grad)
    key_weight_part = outer_sum(h_first, k_grad)
    value_weight_part = outer_sum(h_first, v_grad)
    value_bias_part = row_total(v_grad)
    h_first_grad = (
        project_back(q_pre_grad, w_query)
        + project_back(k_grad, w_key)
        + project_back(v_grad, w_value)
    )
    gain_one_part = jnp.sum(h_first_grad * scaled_one, axis=(0, 1))
    shift_one_part = jnp.sum(h_first_grad, axis=(0, 1))
    attn_grads = (
        lax.psum_scatter(gain_one_part, ("dp", "seq"), scatter_dimension=0, tiled=True),
        lax.psum_scatter(shift_one_part, ("dp", "seq"), scatter_dimension=0, tiled=True),
        lax.psum_scatter(query_weight_part, ("dp", "seq"), scatter_dimension=0, tiled=True),
        lax.psum_scatter(query_bias_part, ("dp", "seq"), scatter_dimension=0, tiled=True),
        lax.psum_scatter(key_weight_part, ("dp", "seq"), scatter_dimension=0, tiled=True),
        lax.psum_scatter(value_weight_part, ("dp", "seq"), scatter_dimension=0, tiled=True),
        lax.psum_scatter(value_bias_part, ("dp", "seq"), scatter_dimension=0, tiled=True),
        lax.psum_scatter(output_weight_part, ("dp", "seq"), scatter_dimension=0, tiled=True),
        lax.psum_scatter(output_bias_part, ("dp", "seq"), scatter_dimension=0, tiled=True),
    )
    frames_grad = (
        middle_grad + norm_back(h_first_grad, scaled_one, inv_one, gain_one.astype(f32))
    ).astype(bf16)
    return (
        output,
        frames_grad,
        attn_grads[0],
        attn_grads[1],
        attn_grads[2],
        attn_grads[3],
        attn_grads[4],
        attn_grads[5],
        attn_grads[6],
        attn_grads[7],
        attn_grads[8],
        ffn_grads[0],
        ffn_grads[1],
        ffn_grads[2],
        ffn_grads[3],
        ffn_grads[4],
        ffn_grads[5],
    )


def solution(mesh):
    return jax.shard_map(
        on_device,
        mesh=mesh,
        in_specs=(
            P("dp", "seq", None),
            P("dp", "seq", None),
            P("dp"),
            P(),
            P(("dp", "seq")),
            P(("dp", "seq")),
            P(("dp", "seq"), None),
            P(("dp", "seq")),
            P(("dp", "seq"), None),
            P(("dp", "seq"), None),
            P(("dp", "seq")),
            P(("dp", "seq"), None),
            P(("dp", "seq")),
            P(("dp", "seq")),
            P(("dp", "seq")),
            P(("dp", "seq"), None),
            P(("dp", "seq")),
            P(("dp", "seq"), None),
            P(("dp", "seq")),
        ),
        out_specs=(
            P("dp", "seq", None),
            P("dp", "seq", None),
            P(("dp", "seq")),
            P(("dp", "seq")),
            P(("dp", "seq"), None),
            P(("dp", "seq")),
            P(("dp", "seq"), None),
            P(("dp", "seq"), None),
            P(("dp", "seq")),
            P(("dp", "seq"), None),
            P(("dp", "seq")),
            P(("dp", "seq")),
            P(("dp", "seq")),
            P(("dp", "seq"), None),
            P(("dp", "seq")),
            P(("dp", "seq"), None),
            P(("dp", "seq")),
        ),
        check_vma=False,
    )
```

profile of v0, /device:TPU:0, one launch (start us, length us, event | category | flops | bytes accessed | tf_op | source)
XLA Modules:
  0.0 1555.2 jit_solution(17484564946680763287)
XLA Ops:
  16.2 42.3 %all-reduce.18 = (bf16[1024]{0:T(1024)(128)(2,1)S(1)}, bf16[1024]{0:T(1024)(128)(2,1)S(1)}, bf16[1024]{0:T(1024)(128)(2,1)S(1)}, bf16[1024]{0:T(1024)(128)(2,1)S...) all-reduce(bf16[1024]{0:T(1024)(128)(2,1)S(1)} %dynamic-update-slic, ...), channel_id=1, replica_groups=mesh['dp'=2,'seq'=16] {'dp','seq'}, use_global_device_ids=true, to_apply=%add.4 | all-reduce | flops 8192 | bytes 32768
  60.8 9.4 all-gather.12.cloned.1.call-done
  70.1 2.9 fusion.123
  73.1 55.3 %all-gather.18.cloned.1.call-done = bf16[1024,1024]{1,0:T(8,128)(2,1)} async-done(((bf16[32,1024]{1,0:T(8,128)(2,1)}), bf16[1024,1024]{1,0:T(8,128)(2,1)}) %all-gather.18.cloned.1.call-update) | async-done | bytes 2097168 | tf_op jit(solution)/shard_map/all_gather | solution.py:215
  128.4 2.8 fusion.117
  133.4 39.2 %all-gather = bf16[32,1,128]{2,1,0:T(2,128)(2,1)S(1)} all-gather(bf16[1,1,128]{2,1,0:T(2,128)(2,1)S(1)} %bitcast.177), channel_id=1, replica_groups=mesh['dp'=2,'seq'=16] {'dp','seq'}, dimensions={0}, use_global_device_ids=true | all-gather | bytes 8448 | tf_op jit(solution)/shard_map/all_gather | solution.py:243
  172.9 13.7 all-gather.16.cloned.1.call-done
  186.6 2.8 fusion.114
  189.6 49.0 %all-gather.14.cloned.1.call-done = bf16[2,1024,1024]{2,1,0:T(8,128)(2,1)} async-done(((bf16[2,64,1024]{2,1,0:T(8,128)(2,1)}), bf16[2,1024,1024]{2,1,0:T(8,128)(2,1)}) %all-gather.14.cloned.1.call-update) | async-done | bytes 4194320 | tf_op jit(solution)/shard_map/all_gather | solution.py:230
  238.7 6.3 copy.118
  244.9 44.9 %all-gather.20.cloned.1.call-done = bf16[2,1024,1024]{2,1,0:T(8,128)(2,1)} async-done(((bf16[2,64,1024]{2,1,0:T(8,128)(2,1)}), bf16[2,1024,1024]{2,1,0:T(8,128)(2,1)}) %all-gather.20.cloned.1.call-update) | async-done | bytes 4194320 | tf_op jit(solution)/shard_map/all_gather | solution.py:229
  289.8 6.2 copy.119
  296.0 18.6 %while.48 = (s32[]{:T(128)}, bf16[2,64,1024]{1,2,0:T(8,128)(2,1)S(1)}, f32[2,16,64]{2,1,0:T(8,128)S(1)}, bf16[2,1024,1024]{1,2,0:T(8,128)(2,1)}, bf16[2,64,1024]...) while((s32[]{:T(128)}, ...), condition=%wide.region_6.7_spmd.clone, body=%wide.region_3.6_spmd.clone.sunk | while | flops 138937856 | bytes 13269241 | solution.py:89
  296.0 1.7 constant_dynamic-slice_fusion.25
  300.7 1.7 constant_dynamic-slice_fusion.25
  305.4 1.7 constant_dynamic-slice_fusion.25
  310.0 1.7 constant_dynamic-slice_fusion.25
  314.7 32.8 %all-gather.22.cloned.1.call-done = bf16[1024,1024]{1,0:T(8,128)(2,1)} async-done(((bf16[32,1024]{1,0:T(8,128)(2,1)}), bf16[1024,1024]{1,0:T(8,128)(2,1)}) %all-gather.22.cloned.1.call-update) | async-done | bytes 2097168 | tf_op jit(solution)/shard_map/all_gather | solution.py:218
  347.5 2.1 fusion.160
  349.9 76.9 %all-gather.24.cloned.1.call-done = bf16[1024,4096]{1,0:T(8,128)(2,1)} async-done(((bf16[32,4096]{1,0:T(8,128)(2,1)}), bf16[1024,4096]{1,0:T(8,128)(2,1)}) %all-gather.24.cloned.1.call-update) | async-done | bytes 8388624 | tf_op jit(solution)/shard_map/all_gather | solution.py:242
  426.8 7.8 fusion.142
  434.6 71.3 %all-gather.26.cloned.1.call-done = bf16[4096,1024]{1,0:T(8,128)(2,1)} async-done(((bf16[128,1024]{1,0:T(8,128)(2,1)}), bf16[4096,1024]{1,0:T(8,128)(2,1)}) %all-gather.26.cloned.1.call-update) | async-done | bytes 8388624 | tf_op jit(solution)/shard_map/all_gather | solution.py:244
  505.9 7.8 convert_reduce_fusion
  513.7 3.5 multiply_reduce_fusion.1
  518.2 1.5 fusion.120
  521.4 45.7 %while.49 = (s32[]{:T(128)}, bf16[2,64,1024]{1,2,0:T(8,128)(2,1)}, f32[2,16,64]{2,1,0:T(8,128)}, bf16[2,1024,1024]{1,2,0:T(8,128)(2,1)}, bf16[2,64,1024]{2,1,0:T...) while((s32[]{:T(128)}, bf16[2,64,1024]{1,2,0:T(8,128)(2,1)}, ...), condition=%wide.region_13.14_spmd.clone, body=%wide.region_11.13_spmd.clone.sunk | while | flops 206046720 | bytes 18833732 | solution.py:132
  521.5 2.8 constant_dynamic-slice_fusion.27
  524.3 1.5 constant_dynamic-slice_fusion.28
  528.7 2.0 multiply_reduce_fusion.7
  532.8 3.1 constant_dynamic-slice_fusion.27
  536.0 1.5 constant_dynamic-slice_fusion.28
  540.4 2.0 multiply_reduce_fusion.7
  544.5 2.8 constant_dynamic-slice_fusion.27
  551.8 2.0 multiply_reduce_fusion.7
  555.8 2.8 constant_dynamic-slice_fusion.27
  563.1 2.0 multiply_reduce_fusion.7
  567.2 3.9 convolution_bitcast_fusion.5
  571.8 26.9 %all_gather.91 = f32[2,16,1024]{1,0,2:T(2,128)S(1)} all-gather(f32[2,16,64]{1,0,2:T(2,128)S(1)} %copy.124), channel_id=1, replica_groups=mesh['dp'=2,'seq'=16] {'seq'}, dimensions={2}, use_global_device_ids=true | all-gather | bytes 139264 | tf_op jit(solution)/shard_map/all_gather | solution.py:306
  599.8 24.5 %all_gather.93 = f32[2,16,1024]{1,0,2:T(2,128)S(1)} all-gather(f32[2,16,64]{1,0,2:T(2,128)S(1)} %copy.125), channel_id=1, replica_groups=mesh['dp'=2,'seq'=16] {'seq'}, dimensions={2}, use_global_device_ids=true | all-gather | bytes 139264 | tf_op jit(solution)/shard_map/all_gather | solution.py:307
  625.4 2.7 convolution_bitcast_fusion.2
  629.9 69.9 %while.50 = (s32[]{:T(128)}, bf16[2,64,1024]{1,2,0:T(8,128)(2,1)}, bf16[2,64,1024]{1,2,0:T(8,128)(2,1)}, bf16[2,1024,1024]{2,1,0:T(8,128)(2,1)}, bf16[2,64,1024]...) while((s32[]{:T(128)}, bf16[2,64,1024]{1,2,0:T(8,128)(2,1)}, ...), condition=%wide.region_15.16_spmd.clone, body=%wide.region_14.15_spmd.clone.sunk | while | flops 272629888 | bytes 20743672 | solution.py:184
  637.4 2.4 fusion.218
  642.9 2.9 fusion.219
  645.8 1.6 constant_dynamic-update-slice_fusion.12
  654.9 2.4 fusion.218
  660.4 2.9 fusion.219
  663.2 1.6 constant_dynamic-update-slice_fusion.12
  672.4 2.4 fusion.218
  677.8 2.9 fusion.219
  680.7 1.7 constant_dynamic-update-slice_fusion.12
  689.8 2.4 fusion.218
  695.3 2.9 fusion.219
  698.2 1.6 constant_dynamic-update-slice_fusion.12
  699.9 4.0 convolution_bitcast_fusion.4
  704.9 2.9 convolution_bitcast_fusion.3
  709.2 8.2 convolution_bitcast_fusion.1
  718.5 11.2 convolution_bitcast_fusion
  730.9 9.3 fusion.111
  744.5 38.8 %all-reduce.17 = (f32[1024]{0:T(1024)S(1)}, f32[1024]{0:T(1024)S(1)}, f32[1024]{0:T(1024)S(1)}, f32[1024]{0:T(1024)S(1)}, f32[1024]{0:T(1024)S(1)}, /*index=5*/f...) all-reduce(f32[1024]{0:T(1024)S(1)} %get-tuple-element.676, ...), channel_id=2, replica_groups=mesh['dp'=2,'seq'=16] {'dp','seq'}, use_global_device_ids=true, to_apply=%region_19.20.clone | all-reduce | flops 12288 | bytes 98304
  789.5 107.0 %reduce-scatter.13.cloned.1.call-done = f32[32,1024]{1,0:T(8,128)} async-done(((f32[1024,1024]{1,0:T(8,128)}), f32[32,1024]{1,0:T(8,128)}) %reduce-scatter.13.cloned.1.call-update) | async-done | bytes 131088 | tf_op jit(solution)/shard_map/reduce_scatter | solution.py:338
  896.5 140.3 %reduce-scatter.9.cloned.1.call-done = f32[32,1024]{1,0:T(8,128)} async-done(((f32[1024,1024]{1,0:T(8,128)}), f32[32,1024]{1,0:T(8,128)}) %reduce-scatter.9.cloned.1.call-update) | async-done | bytes 131088 | tf_op jit(solution)/shard_map/reduce_scatter | solution.py:335
  1036.8 140.5 %reduce-scatter.11.cloned.1.call-done = f32[32,1024]{1,0:T(8,128)} async-done(((f32[1024,1024]{1,0:T(8,128)}), f32[32,1024]{1,0:T(8,128)}) %reduce-scatter.11.cloned.1.call-update) | async-done | bytes 131088 | tf_op jit(solution)/shard_map/reduce_scatter | solution.py:336
  1177.3 183.3 %reduce-scatter.15.cloned.1.call-done = f32[32,4096]{1,0:T(8,128)} async-done(((f32[1024,4096]{1,0:T(8,128)}), f32[32,4096]{1,0:T(8,128)}) %reduce-scatter.15.cloned.1.call-update) | async-done | bytes 524304 | tf_op jit(solution)/shard_map/reduce_scatter | solution.py:273
  1360.7 187.6 %reduce-scatter.17.cloned.1.call-done = f32[128,1024]{1,0:T(8,128)} async-done(((f32[4096,1024]{1,0:T(8,128)}), f32[128,1024]{1,0:T(8,128)}) %reduce-scatter.17.cloned.1.call-update) | async-done | bytes 524304 | tf_op jit(solution)/shard_map/reduce_scatter | solution.py:275
  (346 shorter events, 113.1 us)
Async XLA Ops:
  7.2 121.2 %copy-start = (bf16[2,64,1024]{2,1,0:T(8,128)(2,1)S(1)}, bf16[2,64,1024]{2,1,0:T(8,128)(2,1)}, u32[]{:S(2)}) copy-start(bf16[2,64,1024]{2,1,0:T(8,128)(2,1)} %param.25) | copy-start | bytes 786436
  7.2 62.9 %all-gather.12.cloned.1.call-start = ((), (), s32[]{:S(2)}) async-start(), calls=%async_computation.6 | async-start | bytes 2162688 | tf_op jit(solution)/shard_map/all_gather | solution.py:216
  7.9 120.5 %all-gather.18.cloned.1.call-start = ((), (), s32[]{:S(2)}) async-start(), calls=%async_computation.9 | async-start | bytes 2162688 | tf_op jit(solution)/shard_map/all_gather | solution.py:215
  8.7 177.9 %all-gather.16.cloned.1.call-start = ((), (), s32[]{:S(2)}) async-start(), calls=%async_computation.8 | async-start | bytes 2162688 | tf_op jit(solution)/shard_map/all_gather | solution.py:213
  9.4 229.2 %all-gather.14.cloned.1.call-start = ((), (), s32[]{:S(2)}) async-start(), calls=%async_computation.7 | async-start | bytes 4456448 | tf_op jit(solution)/shard_map/all_gather | solution.py:230
  58.5 128.1 %copy-start.27 = (f32[1024]{0:T(1024)}, f32[1024]{0:T(1024)S(1)}, u32[]{:S(2)}) copy-start(f32[1024]{0:T(1024)S(1)} %convert_element_type.122) | copy-start | bytes 12292
  59.6 127.0 %copy-start.32 = (f32[2,64]{1,0:T(2,128)}, f32[2,64]{1,0:T(2,128)S(1)}, u32[]{:S(2)}) copy-start(f32[2,64]{1,0:T(2,128)S(1)} %broadcast_multiply_fusion.5) | copy-start | bytes 1540
  60.8 125.8 %copy-start.34 = (f32[2,64]{1,0:T(2,128)}, f32[2,64]{1,0:T(2,128)S(1)}, u32[]{:S(2)}) copy-start(f32[2,64]{1,0:T(2,128)S(1)} %add_rsqrt_fusion.1) | copy-start | bytes 1540
  73.0 60.3 %copy-start.46 = (bf16[128]{0:T(256)(128)(2,1)S(1)}, bf16[128]{0:T(256)(128)(2,1)}, u32[]{:S(2)}) copy-start(bf16[128]{0:T(256)(128)(2,1)} %param.41) | copy-start | bytes 772
  73.0 99.6 %copy-start.47 = (s32[4]{0:T(128)S(1)}, s32[4]{0:T(128)}, u32[]{:S(2)}) copy-start(s32[4]{0:T(128)} %param.28) | copy-start | bytes 52
  73.0 99.6 %copy-start.48 = (s32[2]{0:T(128)S(1)}, s32[2]{0:T(128)}, u32[]{:S(2)}) copy-start(s32[2]{0:T(128)} %param.27) | copy-start | bytes 28
  73.1 216.7 %all-gather.20.cloned.1.call-start = ((), (), s32[]{:S(2)}) async-start(), calls=%async_computation.10 | async-start | bytes 4456448 | tf_op jit(solution)/shard_map/all_gather | solution.py:229
  131.2 216.2 %all-gather.22.cloned.1.call-start = ((), (), s32[]{:S(2)}) async-start(), calls=%async_computation.11 | async-start | bytes 2162688 | tf_op jit(solution)/shard_map/all_gather | solution.py:218
  131.8 295.0 %all-gather.24.cloned.1.call-start = ((), (), s32[]{:S(2)}) async-start(), calls=%async_computation.12 | async-start | bytes 8650752 | tf_op jit(solution)/shard_map/all_gather | solution.py:242
  132.6 373.3 %all-gather.26.cloned.1.call-start = ((), (), s32[]{:S(2)}) async-start(), calls=%async_computation.13 | async-start | bytes 8650752 | tf_op jit(solution)/shard_map/all_gather | solution.py:244
  133.3 494.9 %all-gather.28.cloned.1.call-start = ((), (), s32[]{:S(2)}) async-start(), calls=%async_computation.14 | async-start | bytes 4456448 | tf_op jit(solution)/shard_map/all_gather | solution.py:302
  172.7 254.2 %copy-start.25 = (f32[1024]{0:T(1024)}, f32[1024]{0:T(1024)S(1)}, u32[]{:S(2)}) copy-start(f32[1024]{0:T(1024)S(1)} %convert_element_type.132) | copy-start | bytes 12292
  189.4 438.8 %all-gather.30.cloned.1.call-start = ((), (), s32[]{:S(2)}) async-start(), calls=%async_computation.15 | async-start | bytes 4456448 | tf_op jit(solution)/shard_map/all_gather | solution.py:303
  314.7 119.9 %copy-start.12 = (bf16[2,64,1024]{1,2,0:T(8,128)(2,1)}, bf16[2,64,1024]{1,2,0:T(8,128)(2,1)S(1)}, u32[]{:S(2)}) copy-start(bf16[2,64,1024]{1,2,0:T(8,128)(2,1)S(1)} %get-tuple-element.467) | copy-start | bytes 786436
  314.7 119.9 %copy-start.30 = (s32[2]{0:T(128)}, s32[2]{0:T(128)S(1)}, u32[]{:S(2)}) copy-start(s32[2]{0:T(128)S(1)} %get-tuple-element.1157) | copy-start | bytes 28
  349.6 167.6 %copy-start.2 = (f32[2,64,1024]{2,1,0:T(8,128)}, f32[2,64,1024]{2,1,0:T(8,128)S(1)}, u32[]{:S(2)}) copy-start(f32[2,64,1024]{2,1,0:T(8,128)S(1)} %get-tuple-element.769) | copy-start | bytes 1572868
  349.7 167.6 %copy-start.36 = (f32[2,64]{1,0:T(2,128)}, f32[2,64]{1,0:T(2,128)S(1)}, u32[]{:S(2)}) copy-start(f32[2,64]{1,0:T(2,128)S(1)} %broadcast_multiply_fusion.4) | copy-start | bytes 1540
  349.9 167.4 %copy-start.38 = (f32[2,64]{1,0:T(2,128)}, f32[2,64]{1,0:T(2,128)S(1)}, u32[]{:S(2)}) copy-start(f32[2,64]{1,0:T(2,128)S(1)} %add_rsqrt_fusion) | copy-start | bytes 1540
  426.8 79.1 %copy-start.20 = (bf16[2,64,1024]{2,1,0:T(8,128)(2,1)S(1)}, bf16[2,64,1024]{2,1,0:T(8,128)(2,1)}, u32[]{:S(2)}) copy-start(bf16[2,64,1024]{2,1,0:T(8,128)(2,1)} %param.26) | copy-start | bytes 786436
  505.9 7.8 copy-start.1
  513.7 3.5 copy-start.10
  513.7 3.6 copy-start.21
  513.7 4.5 copy-start.9
  518.2 3.3 copy-start.4
  519.7 269.7 %reduce-scatter.7.cloned.1.call-start = ((), (), s32[]{:S(2)}) async-start(), calls=%async_computation.16 | async-start | bytes 4325376 | tf_op jit(solution)/shard_map/reduce_scatter | solution.py:333
  521.5 2.8 copy-start.23
  530.7 2.1 copy-start.24
  532.8 3.2 copy-start.23
  542.4 2.1 copy-start.24
  544.5 2.8 copy-start.23
  553.7 2.1 copy-start.24
  555.8 2.8 copy-start.23
  565.1 2.1 copy-start.24
  571.1 28.7 %copy-start.29 = (f32[2,16,64]{2,1,0:T(8,128)S(1)}, f32[2,16,64]{2,1,0:T(8,128)}, u32[]{:S(2)}) copy-start(f32[2,16,64]{2,1,0:T(8,128)} %get-tuple-element.470) | copy-start | bytes 24580
  571.1 325.4 %reduce-scatter.13.cloned.1.call-start = ((), (), s32[]{:S(2)}) async-start(), calls=%async_computation.19 | async-start | bytes 4325376 | tf_op jit(solution)/shard_map/reduce_scatter | solution.py:338
  571.8 53.7 %copy-start.5 = (f32[2,64,1024]{2,1,0:T(8,128)S(1)}, f32[2,64,1024]{2,1,0:T(8,128)}, u32[]{:S(2)}) copy-start(f32[2,64,1024]{2,1,0:T(8,128)} %copy-done.4) | copy-start | bytes 1572868
  571.8 53.7 %copy-start.13 = (bf16[2,64,1024]{1,2,0:T(8,128)(2,1)S(1)}, bf16[2,64,1024]{1,2,0:T(8,128)(2,1)}, u32[]{:S(2)}) copy-start(bf16[2,64,1024]{1,2,0:T(8,128)(2,1)} %copy-done.12) | copy-start | bytes 786436
  628.1 1.8 copy-start.31
  628.2 408.7 %reduce-scatter.9.cloned.1.call-start = ((), (), s32[]{:S(2)}) async-start(), calls=%async_computation.17 | async-start | bytes 4325376 | tf_op jit(solution)/shard_map/reduce_scatter | solution.py:335
  629.9 69.9 %copy-start.28 = (f32[1024]{0:T(1024)S(1)}, f32[1024]{0:T(1024)}, u32[]{:S(2)}) copy-start(f32[1024]{0:T(1024)} %copy-done.27) | copy-start | bytes 12292
  636.7 4.6 copy-start.19
  637.4 3.9 copy-start.49
  642.9 2.9 copy-start.15
  654.1 4.6 copy-start.19
  654.9 3.9 copy-start.49
  660.4 2.9 copy-start.15
  671.6 4.6 copy-start.19
  672.4 3.9 copy-start.49
  677.8 2.9 copy-start.15
  689.1 4.6 copy-start.19
  689.8 3.9 copy-start.49
  695.3 2.9 copy-start.15
  703.9 473.5 %reduce-scatter.11.cloned.1.call-start = ((), (), s32[]{:S(2)}) async-start(), calls=%async_computation.18 | async-start | bytes 4325376 | tf_op jit(solution)/shard_map/reduce_scatter | solution.py:336
  707.8 652.8 %reduce-scatter.15.cloned.1.call-start = ((), (), s32[]{:S(2)}) async-start(), calls=%async_computation.20 | async-start | bytes 17301504 | tf_op jit(solution)/shard_map/reduce_scatter | solution.py:273
  717.4 830.8 %reduce-scatter.17.cloned.1.call-start = ((), (), s32[]{:S(2)}) async-start(), calls=%async_computation.21 | async-start | bytes 17301504 | tf_op jit(solution)/shard_map/reduce_scatter | solution.py:275
  730.9 9.5 copy-start.14
  730.9 9.5 copy-start.17
  740.2 1.6 copy-start.16
  743.5 45.1 %copy-start.6 = (f32[2,64,1024]{2,1,0:T(8,128)S(1)}, f32[2,64,1024]{2,1,0:T(8,128)}, u32[]{:S(2)}) copy-start(f32[2,64,1024]{2,1,0:T(8,128)} %copy-done.4) | copy-start | bytes 1572868
  (19 other events, 21.2 us)
Sparse Core Ops, SparseCore 0:
  10.9 59.1 all-gather.11
  73.0 55.3 all-gather.17
  131.3 55.2 all-gather.15
  189.2 49.4 all-gather.13
  240.7 49.0 all-gather.19
  292.5 54.9 all-gather.21
  350.4 76.4 all-gather.23
  429.7 76.1 all-gather.25
  508.6 49.1 all-gather.27
  559.9 53.3 all-gather.29
  616.1 140.3 reduce-scatter.6
  759.3 137.1 reduce-scatter.12
  899.3 137.4 reduce-scatter.8
  1039.5 137.7 reduce-scatter.10
  1180.1 180.5 reduce-scatter.14
  1363.4 184.7 reduce-scatter.16
where the time goes:
time: 1560 us
  waiting for transfers between devices  1120 us (72%)
  blocking collectives  172 us (11%)
  local copies, waits for them, and re-layouts  120 us (8%)
  matrix products  117 us (8%)
    reduce_scatter x1, waiting for transfers between devices, on_device(): lax.psum_scatter(down_weight_part, ('dp', 'seq'), scatter_dimension=0, ti...  188 us
    reduce_scatter x1, waiting for transfers between devices, on_device(): lax.psum_scatter(up_weight_part, ('dp', 'seq'), scatter_dimension=0, tile...  183 us
    reduce_scatter x1, waiting for transfers between devices, on_device(): lax.psum_scatter(value_weight_part, ('dp', 'seq'), scatter_dimension=0, t...  141 us
    reduce_scatter x1, waiting for transfers between devices, on_device(): lax.psum_scatter(key_weight_part, ('dp', 'seq'), scatter_dimension=0, til...  140 us
    reduce_scatter x1, waiting for transfers between devices, on_device(): lax.psum_scatter(output_weight_part, ('dp', 'seq'), scatter_dimension=0,...  107 us
    unnamed x2, blocking collectives  81.1 us
    all_gather x1, waiting for transfers between devices, on_device(): lax.all_gather(up_weight, ('dp', 'seq'), axis=0, tiled=True)  76.9 us
    all_gather x1, waiting for transfers between devices, on_device(): lax.all_gather(down_weight, ('dp', 'seq'), axis=0, tiled=True)  71.3 us
  transfers between devices with their start and end apart: 16, of which 13 were waited for; matrix products, arithmetic and copies ran while one was open for 16% of the time, Pallas kernels for 0%

commit v1 on v0

v1 whole, which is shorter than its diff:
```python
import functools

import jax
import jax.numpy as jnp
from jax import lax
from jax.experimental import pallas as pl
from jax.experimental.pallas import tpu as pltpu
from jax.sharding import PartitionSpec as P

HEAD = 64
f32 = jnp.float32
bf16 = jnp.bfloat16
norm_eps = 1e-05
inv_root_two = 0.7071067811865476
inv_root_tau = 0.3989422804014327
NT = (((1,), (1,)), ((), ()))
NN = (((1,), (0,)), ((), ()))
MIB = 1024 * 1024


def dot(a, b, dims=NN):
    return lax.dot_general(a, b, dims, preferred_element_type=f32)


def normalize(rows):
    average = jnp.mean(rows, axis=-1, keepdims=True)
    centered = rows - average
    inv_std = lax.rsqrt(jnp.mean(centered * centered, axis=-1, keepdims=True) + norm_eps)
    return centered * inv_std, inv_std


def norm_back(grad_rows, scaled, inv_std, gain):
    grad_hat = grad_rows * gain
    return inv_std * (
        grad_hat
        - jnp.mean(grad_hat, axis=-1, keepdims=True)
        - scaled * jnp.mean(grad_hat * scaled, axis=-1, keepdims=True)
    )


def vmem_call(kernel, meta, args, outs, name, flops, scratch=(), limit=40):
    spec = pl.BlockSpec(memory_space=pltpu.VMEM)
    nbytes = sum(a.size * a.dtype.itemsize for a in list(args) + list(outs))
    return pl.pallas_call(
        kernel,
        out_shape=tuple(outs),
        in_specs=[pl.BlockSpec(memory_space=pltpu.SMEM)] + [spec] * len(args),
        out_specs=tuple([spec] * len(outs)),
        scratch_shapes=list(scratch),
        compiler_params=pltpu.CompilerParams(vmem_limit_bytes=limit * MIB),
        cost_estimate=pl.CostEstimate(flops=int(flops), bytes_accessed=int(nbytes), transcendentals=0),
        name=name,
    )(meta, *args)


def sds(shape, dtype):
    return jax.ShapeDtypeStruct(shape, dtype)


def qkv_kernel(n, meta, *refs):
    xs = refs[: 2 * n]
    w, vec, bq, bv, x_out, h_out, q_out, k_out, v_out = refs[2 * n :]
    j = meta[0]
    half = xs[0].shape[0]
    hd = bq.shape[1]
    for r in range(n):
        m = j ^ r
        base = pl.multiple_of(m * (2 * half), 2 * half)
        for part in range(2):
            rows = xs[2 * r + part][...]
            at = pl.ds(base + part * half, half)
            x_out[at, :] = rows
            scaled, _ = normalize(rows.astype(f32))
            h_out[at, :] = (scaled * vec[0:1, :] + vec[1:2, :]).astype(bf16)
        at = pl.ds(base, 2 * half)
        qkv = dot(h_out[at, :], w[...])
        q_out[at, :] = ((qkv[:, :hd] + bq[...]) * 0.125).astype(bf16)
        k_out[at, :] = qkv[:, hd : 2 * hd].astype(bf16)
        v_out[at, :] = (qkv[:, 2 * hd :] + bv[...]).astype(bf16)


def key_mask(meta, rows, n, half, width):
    row = lax.broadcasted_iota(jnp.int32, (rows, width), 0)
    member = row // (2 * half)
    inside = row % (2 * half)
    own = (inside < half).astype(jnp.int32)
    h = meta[1]
    block_half = own * h + (1 - own) * (1 - h)
    frame = (block_half * n + member) * half + inside % half
    return frame < meta[2]


def attend_kernel(n, half, qb, meta, q, k, v, o_out, lse_out, bias):
    total = k.shape[0]
    heads = k.shape[1] // HEAD
    bias[...] = jnp.where(key_mask(meta, total, n, half, 128), 0.0, -1.0).astype(f32)
    for head in range(heads):
        cols = slice(head * HEAD, (head + 1) * HEAD)
        kh = k[:, cols]
        vt = v[:, cols].astype(f32).T.astype(bf16)

        def step(i, _, cols=cols, kh=kh, vt=vt, head=head):
            at = pl.ds(pl.multiple_of(i * qb, qb), qb)
            scores = dot(kh, q[at, cols], NT)
            valid = bias[:, 0:1] >= 0.0
            scores = jnp.where(valid, scores, -1e30)
            row_max = jnp.max(scores, axis=0, keepdims=True)
            e = jnp.exp(scores - row_max)
            row_sum = jnp.sum(e, axis=0, keepdims=True)
            ot = dot(vt, e.astype(bf16)) / row_sum
            o_out[at, cols] = ot.T.astype(bf16)
            lse_out[pl.ds(head, 1), at] = row_max + jnp.log(row_sum)
            return 0

        lax.fori_loop(0, total // qb, step, 0)


def mid_kernel(n, meta, o_in, w_out, x_own, x_recv, vec, y_out, h_out, cat):
    hd = o_in.shape[2]
    half = x_own.shape[0]
    for m in range(n):
        cat[:, m * hd : (m + 1) * hd] = o_in[m]
    y = dot(cat[...], w_out[...]) + vec[4:5, :]
    y_out[:half, :] = y[:half] + x_own[...].astype(f32)
    y_out[half:, :] = y[half:] + x_recv[...].astype(f32)
    scaled, _ = normalize(y_out[...])
    h_out[...] = (scaled * vec[5:6, :] + vec[6:7, :]).astype(bf16)


def down_back_kernel(n, meta, *refs):
    dys = refs[:n]
    w_down, dy_out, dg_out = refs[n:]
    j = meta[0]
    rows = dys[0].shape[0]
    for r in range(n):
        at = pl.ds(pl.multiple_of((j ^ r) * rows, rows), rows)
        dy = dys[r][...]
        dy_out[at, :] = dy
        dg_out[at, :] = dot(dy, w_down[...], NT)


def ffn_kernel(n, meta, *refs):
    hs = refs[:n]
    w_up, b_up, dg, h_out, g_out, du_out, keep, send, db_out = refs[n:]
    j = meta[0]
    rows = hs[0].shape[0]
    db_out[...] = jnp.zeros_like(db_out)
    for r in range(n):
        at = pl.ds(pl.multiple_of((j ^ r) * rows, rows), rows)
        h = hs[r][...]
        h_out[at, :] = h
        u = dot(h, w_up[...]) + b_up[...]
        cdf = 0.5 * (1.0 + lax.erf(u * inv_root_two))
        g_out[at, :] = (u * cdf).astype(bf16)
        slope = cdf + u * jnp.exp(-0.5 * u * u) * inv_root_tau
        du = (dg[at, :] * slope).astype(bf16)
        du_out[at, :] = du
        db_out[...] += jnp.sum(du.astype(f32), axis=0, keepdims=True)
        dh = dot(du, w_up[...], NT)
        here = slice((r // 2) * rows, (r // 2 + 1) * rows)
        if r % 2 == 0:
            keep[here, :] = dh
        else:
            send[here, :] = dh.astype(bf16)


def down_kernel(n, meta, g, w_down, keep, send):
    j = meta[0]
    rows = g.shape[0] // n
    for r in range(n):
        at = pl.ds(pl.multiple_of((j ^ r) * rows, rows), rows)
        out = dot(g[at, :], w_down[...])
        here = slice((r // 2) * rows, (r // 2 + 1) * rows)
        if r % 2 == 0:
            keep[here, :] = out
        else:
            send[here, :] = out.astype(bf16)


def pair_kernel(meta, keep, recv, *outs):
    rows = outs[0].shape[0]
    for i, out in enumerate(outs):
        here = slice(i * rows, (i + 1) * rows)
        out[...] = (keep[here, :] + recv[here, :].astype(f32)).astype(out.dtype)


def out_kernel(count, meta, *refs):
    own, y = refs[0], refs[count]
    vec, kept, sent = refs[count + 1 :]
    total = own[...]
    for i in range(1, count):
        total = total + refs[i][...].astype(f32)
    out = (y[...] + total + vec[7:8, :]).astype(bf16)
    half = kept.shape[0]
    kept[...] = out[:half]
    sent[...] = out[half:]


def mid_back_kernel(n, count, meta, *refs):
    own = refs[0]
    y, dy, vec, w_out = refs[count : count + 4]
    dy1_out, da_out, do_out, small = refs[count + 4 :]
    dh = own[...]
    for i in range(1, count):
        dh = dh + refs[i][...].astype(f32)
    scaled, inv_std = normalize(y[...])
    dyf = dy[...].astype(f32)
    dy1 = dyf + norm_back(dh, scaled, inv_std, vec[5:6, :])
    dy1_out[...] = dy1
    da = dy1.astype(bf16)
    da_out[...] = da
    small[0:1, :] = jnp.sum(dh * scaled, axis=0, keepdims=True)
    small[1:2, :] = jnp.sum(dh, axis=0, keepdims=True)
    small[2:3, :] = jnp.sum(da.astype(f32), axis=0, keepdims=True)
    small[3:4, :] = jnp.sum(dyf, axis=0, keepdims=True)
    hd = do_out.shape[2]
    for m in range(n):
        do_out[m] = dot(da, w_out[m * hd : (m + 1) * hd, :], NT).astype(bf16)


def attend_back_kernel(n, half, qb, meta, q, k, v, do, lse, w, dqkv, keep, send, db, bias, acc_k, acc_v):
    total = k.shape[0]
    hd = k.shape[1]
    heads = hd // HEAD
    bias[...] = jnp.where(key_mask(meta, total, n, half, 128), 0.0, -1.0).astype(f32)
    for head in range(heads):
        cols = slice(head * HEAD, (head + 1) * HEAD)
        kh = k[:, cols]
        vh = v[:, cols]
        kt = kh.astype(f32).T.astype(bf16)
        acc_k[...] = jnp.zeros_like(acc_k)
        acc_v[...] = jnp.zeros_like(acc_v)

        def step(i, _, cols=cols, kh=kh, vh=vh, kt=kt, head=head):
            at = pl.ds(pl.multiple_of(i * qb, qb), qb)
            qh = q[at, cols]
            doh = do[at, cols]
            scores = dot(kh, qh, NT)
            valid = bias[:, 0:1] >= 0.0
            probs = jnp.where(valid, jnp.exp(scores - lse[pl.ds(head, 1), at]), 0.0)
            dp = dot(vh, doh, NT)
            centre = jnp.sum(probs * dp, axis=0, keepdims=True)
            ds = (probs * (dp - centre)).astype(bf16)
            acc_v[...] += dot(probs.astype(bf16), doh)
            acc_k[...] += dot(ds, qh)
            dq = dot(kt, ds)
            dqkv[at, cols] = (dq.T.astype(bf16).astype(f32) * 0.125).astype(bf16)
            return 0

        lax.fori_loop(0, total // qb, step, 0)
        dqkv[:, hd + head * HEAD : hd + (head + 1) * HEAD] = acc_k[...].astype(bf16)
        dqkv[:, 2 * hd + head * HEAD : 2 * hd + (head + 1) * HEAD] = acc_v[...].astype(bf16)
    j = meta[0]
    rows = 2 * half
    db[...] = jnp.zeros_like(db)
    for r in range(n):
        at = pl.ds(pl.multiple_of((j ^ r) * rows, rows), rows)
        grads = dqkv[at, :]
        db[...] += jnp.sum(grads.astype(f32), axis=0, keepdims=True)
        dh = dot(grads, w[...], NT)
        here = slice((r // 2) * rows, (r // 2 + 1) * rows)
        if r % 2 == 0:
            keep[here, :] = dh
        else:
            send[here, :] = dh.astype(bf16)


def first_small_kernel(meta, x, dqkv, w, small):
    rows = 128
    small[...] = jnp.zeros_like(small)

    def step(i, _):
        at = pl.ds(pl.multiple_of(i * rows, rows), rows)
        dh = dot(dqkv[at, :], w[...], NT)
        scaled, _ = normalize(x[at, :].astype(f32))
        small[0:1, :] += jnp.sum(dh * scaled, axis=0, keepdims=True)
        small[1:2, :] += jnp.sum(dh, axis=0, keepdims=True)
        return 0

    lax.fori_loop(0, x.shape[0] // rows, step, 0)


def place_kernel(meta, *refs):
    out = refs[-1]
    for r, piece in enumerate(refs[:-1]):
        m = meta[0] ^ r
        for i in range(out.shape[0]):
            out[i, m] = piece[i]


def last_kernel(count, meta, *refs):
    own = refs[0]
    x_own, x_recv, dy1, vec, kept, sent = refs[count:]
    half = kept.shape[0]
    for part, (x, out) in enumerate(((x_own, kept), (x_recv, sent))):
        at = slice(part * half, (part + 1) * half)
        dh = own[at, :]
        for i in range(1, count):
            dh = dh + refs[i][at, :].astype(f32)
        scaled, inv_std = normalize(x[...].astype(f32))
        out[...] = (dy1[at, :] + norm_back(dh, scaled, inv_std, vec[0:1, :])).astype(bf16)


def on_device(
    dp_size,
    seq_size,
    frames,
    out_grad,
    order,
    lengths,
    first_gain,
    first_shift,
    query_weight,
    query_bias,
    key_weight,
    value_weight,
    value_bias,
    output_weight,
    output_bias,
    second_gain,
    second_shift,
    up_weight,
    up_bias,
    down_weight,
    down_bias,
):
    slots, half, width = frames.shape
    n = seq_size // slots
    groups = dp_size * slots
    ndev = dp_size * seq_size
    hd = width // n
    rs = query_weight.shape[0]
    hidden = up_weight.shape[1]
    chunk = hidden // ndev
    mine = hidden // n
    rows = 2 * half
    total = n * rows
    both = ("dp", "seq")

    dp_at = lax.axis_index("dp")
    seq_at = lax.axis_index("seq")
    h = seq_at // n
    j = seq_at % n
    length = lengths[order[h]]
    meta = jnp.stack([j, h, length, dp_at]).astype(jnp.int32)

    def xor(value, bit):
        return lax.ppermute(value, "seq", [(i, i ^ bit) for i in range(seq_size)])

    def xor_dp(value, bit):
        return lax.ppermute(value, "dp", [(i, i ^ bit) for i in range(dp_size)])

    def gather(value):
        got = [value] + [xor(value, r) for r in range(n - 2, 0, -2)]
        even = [got[0]] + got[1:][::-1]
        out = []
        for piece in even:
            out += [piece, xor(piece, 1)]
        return out

    def scatter(keep, send):
        recv = xor(send, 1)
        pieces = vmem_call(
            pair_kernel,
            meta,
            [keep, recv],
            [sds((rows, width), f32)] + [sds((rows, width), bf16)] * (n // 2 - 1),
            "pair",
            keep.size,
        )
        return [pieces[0]] + [xor(pieces[i], 2 * i) for i in range(n // 2 - 1, 0, -1)]

    def take_half(value, bit):
        keep = lax.dynamic_index_in_dim(value, bit, 0, keepdims=False)
        send = lax.dynamic_index_in_dim(value, 1 - bit, 0, keepdims=False)
        return keep, send.astype(bf16)

    bits = []
    step = dp_size // 2
    while step:
        bits.append(step)
        step //= 2

    def gather_groups(value):
        other = xor(value, n)
        value = jnp.where(h == 0, jnp.stack([value, other]), jnp.stack([other, value]))
        for bit in bits[::-1]:
            other = xor_dp(value, bit)
            low = (dp_at & bit) == 0
            value = jnp.where(low, jnp.concatenate([value, other]), jnp.concatenate([other, value]))
        return value

    def reduce_groups(value):
        for bit in bits:
            value = value.reshape((2, value.shape[0] // 2) + value.shape[1:])
            keep, send = take_half(value, (dp_at & bit) // bit)
            value = keep.astype(f32) + xor_dp(send, bit).astype(f32)
        keep, send = take_half(value, h)
        return keep.astype(f32) + xor(send, n).astype(f32)

    def members(value):
        index = [[s * n + i for i in range(n)] for s in range(slots)]
        return lax.all_to_all(value, "seq", 0, 0, tiled=True, axis_index_groups=index)

    x_own = lax.dynamic_index_in_dim(frames, h, 0, keepdims=False)
    x_recv = xor(lax.dynamic_index_in_dim(frames, 1 - h, 0, keepdims=False), n)
    xs = []
    for a, b in zip(gather(x_own), gather(x_recv)):
        xs += [a, b]

    block_rows = -(-(rs + 1) // 8) * 8
    small_in = [first_gain, first_shift, query_bias, value_bias, output_bias, second_gain, second_shift, down_bias]
    tail = jnp.concatenate(small_in + [up_bias])
    tail = jnp.pad(tail, (0, 3 * hd - tail.shape[0]))
    by_head = jnp.concatenate(
        [w.reshape(rs, n, hd).transpose(1, 0, 2) for w in (query_weight, key_weight, value_weight)], axis=2
    )
    by_head = jnp.concatenate(
        [
            by_head,
            jnp.broadcast_to(tail[None, None, :], (n, 1, 3 * hd)),
            jnp.zeros((n, block_rows - rs - 1, 3 * hd), bf16),
        ],
        axis=1,
    )
    everyone = jnp.broadcast_to(by_head[None], (groups,) + by_head.shape).reshape(ndev, block_rows, 3 * hd)
    got = lax.all_to_all(everyone, both, 0, 0, tiled=True)
    w_qkv = got[:, :rs, :].reshape(width, 3 * hd)
    vec = got[:, rs, : 8 * rs].reshape(ndev, 8, rs).transpose(1, 0, 2).reshape(8, width).astype(f32)
    bias_up = got[:, rs, 8 * rs : 8 * rs + chunk].reshape(groups, n, chunk)
    bias_up = lax.dynamic_index_in_dim(bias_up, j, 1, keepdims=False).reshape(1, mine).astype(f32)
    bias_q = lax.dynamic_slice(vec, (2, j * hd), (1, hd))
    bias_v = lax.dynamic_slice(vec, (3, j * hd), (1, hd))

    up_mine = up_weight.reshape(rs, groups, n, chunk).transpose(2, 0, 1, 3).reshape(n, rs, mine)
    up_mine = members(up_mine).reshape(n * rs, mine)
    w_up = gather_groups(up_mine).reshape(width, mine)
    w_down = gather_groups(down_weight).reshape(mine, width)

    out_mine = gather_groups(output_weight)
    out_all = gather(out_mine)
    (w_out,) = vmem_call(place_kernel, meta, out_all, [sds((groups, n, rs, width), bf16)], "place", width * width)
    w_out = w_out.reshape(width, width)

    x_all, h_first, q, k, v = vmem_call(
        functools.partial(qkv_kernel, n),
        meta,
        xs + [w_qkv, vec, bias_q, bias_v],
        [sds((total, width), bf16)] * 2 + [sds((total, hd), bf16)] * 3,
        "qkv",
        2 * total * width * 3 * hd,
    )
    qb = min(256, total)
    o_heads, lse = vmem_call(
        functools.partial(attend_kernel, n, half, qb),
        meta,
        [q, k, v],
        [sds((total, hd), bf16), sds((hd // HEAD, total), f32)],
        "attend",
        8 * total * total * hd,
        scratch=[pltpu.VMEM((total, 128), f32)],
    )
    o_rows = members(o_heads.reshape(n, rows, hd))
    y1, h2 = vmem_call(
        functools.partial(mid_kernel, n),
        meta,
        [o_rows, w_out, x_own, x_recv, vec],
        [sds((rows, width), f32), sds((rows, width), bf16)],
        "mid",
        2 * rows * width * width,
        scratch=[pltpu.VMEM((rows, width), bf16)],
    )

    dy_own = lax.dynamic_index_in_dim(out_grad, h, 0, keepdims=False)
    dy_recv = xor(lax.dynamic_index_in_dim(out_grad, 1 - h, 0, keepdims=False), n)
    dy = jnp.concatenate([dy_own, dy_recv])
    dy_all, dg = vmem_call(
        functools.partial(down_back_kernel, n),
        meta,
        gather(dy) + [w_down],
        [sds((total, width), bf16), sds((total, mine), f32)],
        "down_back",
        2 * total * width * mine,
    )

    part = [sds((total // 2, width), f32), sds((total // 2, width), bf16)]
    h2_all, g, du, keep, send, d_bias_up = vmem_call(
        functools.partial(ffn_kernel, n),
        meta,
        gather(h2) + [w_up, bias_up, dg],
        [sds((total, width), bf16)] + [sds((total, mine), bf16)] * 2 + part + [sds((1, mine), f32)],
        "ffn",
        4 * total * width * mine,
    )
    dh2 = scatter(keep, send)
    dy1, da, do_rows, small_two = vmem_call(
        functools.partial(mid_back_kernel, n, n // 2),
        meta,
        dh2 + [y1, dy, vec, w_out],
        [sds((rows, width), f32), sds((rows, width), bf16), sds((n, rows, hd), bf16), sds((4, width), f32)],
        "mid_back",
        2 * rows * width * width,
    )
    do_heads = members(do_rows).reshape(total, hd)

    keep, send = vmem_call(
        functools.partial(down_kernel, n), meta, [g, w_down], part, "down", 2 * total * width * mine
    )
    kept, sent = vmem_call(
        functools.partial(out_kernel, n // 2),
        meta,
        scatter(keep, send) + [y1, vec],
        [sds((half, width), bf16)] * 2,
        "out",
        rows * width,
    )
    other = xor(sent, n)
    output = jnp.where(h == 0, jnp.stack([kept, other]), jnp.stack([other, kept]))

    d_qkv, keep, send, d_bias_qkv = vmem_call(
        functools.partial(attend_back_kernel, n, half, qb),
        meta,
        [q, k, v, do_heads, lse, w_qkv],
        [sds((total, 3 * hd), bf16)] + part + [sds((1, 3 * hd), f32)],
        "attend_back",
        20 * total * total * hd,
        scratch=[pltpu.VMEM((total, 128), f32), pltpu.VMEM((total, HEAD), f32), pltpu.VMEM((total, HEAD), f32)],
    )
    dh1 = scatter(keep, send)
    (small_one,) = vmem_call(
        first_small_kernel, meta, [x_all, d_qkv, w_qkv], [sds((2, width), f32)], "first_small", 6 * total * width * hd
    )
    kept, sent = vmem_call(
        functools.partial(last_kernel, n // 2),
        meta,
        dh1 + [x_own, x_recv, dy1, vec],
        [sds((half, width), bf16)] * 2,
        "last",
        rows * width,
    )
    other = xor(sent, n)
    frames_grad = jnp.where(h == 0, jnp.stack([kept, other]), jnp.stack([other, kept]))

    d_down = jnp.einsum("rf,rd->fd", g, dy_all, preferred_element_type=f32)
    d_down = reduce_groups(d_down.reshape(groups, chunk, width))
    d_up = jnp.einsum("rd,rf->df", h2_all, du, preferred_element_type=f32)
    d_up = reduce_groups(d_up.reshape(groups, n * rs, mine))
    d_qkv_w = jnp.einsum("rd,rf->df", h_first, d_qkv, preferred_element_type=f32)
    d_qkv_w = reduce_groups(d_qkv_w.reshape(groups, n * rs, 3 * hd))
    da_all = gather(da)
    da_all = [piece[None] for piece in da_all]
    (da_all,) = vmem_call(place_kernel, meta, da_all, [sds((1, n, rows, width), bf16)], "place", width * total)
    da_all = da_all.reshape(total, width)
    d_out = jnp.einsum("rf,rd->fd", o_heads, da_all, preferred_element_type=f32)
    back = jnp.concatenate([d_up.reshape(n, rs, mine), d_qkv_w.reshape(n, rs, 3 * hd)], axis=2).astype(bf16)
    back = members(back).astype(f32)
    up_weight_grad = back[:, :, :mine].reshape(n, rs, groups, chunk).transpose(1, 2, 0, 3).reshape(rs, hidden)
    qkv_grad = back[:, :, mine:].transpose(1, 0, 2).reshape(rs, n, 3, hd)
    query_weight_grad, key_weight_grad, value_weight_grad = (
        qkv_grad[:, :, i, :].reshape(rs, width) for i in range(3)
    )

    group = dp_at * slots + h
    d_out = d_out.reshape(groups, rs, width)
    output_weight_grad = None
    for k_step in range(groups):
        pairs = []
        for d in range(ndev):
            g_of, j_of = (d // seq_size) * slots + (d % seq_size) // n, d % n
            pairs.append((d, j_of * groups + (g_of + k_step) % groups))
        piece = lax.dynamic_index_in_dim(d_out, (group + k_step) % groups, 0, keepdims=False)
        piece = lax.ppermute(piece.astype(bf16), both, pairs).astype(f32)
        output_weight_grad = piece if output_weight_grad is None else output_weight_grad + piece

    vectors = jnp.zeros((2, width), f32)
    vectors = lax.dynamic_update_slice(vectors, d_bias_qkv[:, :hd], (0, j * hd))
    vectors = lax.dynamic_update_slice(vectors, d_bias_qkv[:, 2 * hd :], (1, j * hd))
    vectors = jnp.concatenate([small_one, small_two, vectors])
    vectors = vectors.reshape(8, ndev, rs).transpose(1, 0, 2).reshape(ndev, 8 * rs)
    spread = jnp.zeros((groups, n, chunk), f32)
    spread = lax.dynamic_update_slice(spread, d_bias_up.reshape(groups, 1, chunk), (0, j, 0))
    vectors = jnp.concatenate([vectors, spread.reshape(ndev, chunk)], axis=1)
    vectors = lax.all_to_all(vectors[:, None, :], both, 0, 0, tiled=True)
    vectors = jnp.sum(vectors, axis=(0, 1))
    singles = vectors[: 8 * rs].reshape(8, rs)
    return (
        output,
        frames_grad,
        singles[0],
        singles[1],
        query_weight_grad,
        singles[6],
        key_weight_grad,
        value_weight_grad,
        singles[7],
        output_weight_grad,
        singles[4],
        singles[2],
        singles[3],
        up_weight_grad,
        vectors[8 * rs :],
        d_down,
        singles[5],
    )


def solution(mesh):
    vector = P(("dp", "seq"))
    matrix = P(("dp", "seq"), None)
    rows = P("dp", "seq", None)
    return jax.shard_map(
        functools.partial(on_device, mesh.shape["dp"], mesh.shape["seq"]),
        mesh=mesh,
        in_specs=(
            rows,
            rows,
            P("dp"),
            P(),
            vector,
            vector,
            matrix,
            vector,
            matrix,
            matrix,
            vector,
            matrix,
            vector,
            vector,
            vector,
            matrix,
            vector,
            matrix,
            vector,
        ),
        out_specs=(
            rows,
            rows,
            vector,
            vector,
            matrix,
            vector,
            matrix,
            matrix,
            vector,
            matrix,
            vector,
            vector,
            vector,
            matrix,
            vector,
            matrix,
            vector,
        ),
        check_vma=False,
    )
```

time: 1560 us -> 344 us (0.22)
  waiting for transfers between devices: 1120 us -> 82.1 us
  blocking collectives: 172 us -> 0 us
  matrix products: 117 us -> 4.33 us
  starting transfers between devices: 1.28 us -> 103 us
  Pallas kernels: 0 us -> 58.3 us
  local copies, waits for them, and re-layouts: 120 us -> 65.2 us
    reduce_scatter x6 -> x0, waiting for transfers between devices: 759 us -> none  [the longest x1 188 us: on_device(): lax.psum_scatter(down_weight_part, ('dp', 'seq'), scatter_dimension=0, ti...]
    all_gather x10 -> x0, waiting for transfers between devices: 353 us -> none  [the longest x1 76.9 us: on_device(): lax.all_gather(up_weight, ('dp', 'seq'), axis=0, tiled=True)]
    dot_general x50 -> x4, matrix products: 117 us -> 4.33 us  [the longest x1 1.3 us: on_device(): d_up = jnp.einsum('rd,rf->df', h2_all, du, preferred_element_type=f32)]
    all_gather x3 -> x0, blocking collectives: 90.7 us -> none  [the longest x1 39.2 us: on_device(): lax.all_gather(up_bias, ('dp', 'seq'), axis=0, tiled=True)]
    ppermute x0 -> x74, waiting for transfers between devices: none -> 81.8 us  [the longest x64 81.7 us: xor(): return lax.ppermute(value, 'seq', [(i, i ^ bit) for i in range(seq_size)])]
    unnamed x2 -> x0, blocking collectives: 81.1 us -> none
    ppermute x0 -> x74, starting transfers between devices: none -> 76.2 us  [the longest x64 56.7 us: xor(): return lax.ppermute(value, 'seq', [(i, i ^ bit) for i in range(seq_size)])]
    dynamic_slice x52 -> x3, local copies, waits for them, and re-layouts: 64.5 us -> 1.25 us  [the longest x2 1.18 us: on_device(): length = lengths[order[h]]]
  transfers between devices with their start and end apart: 16 -> 80, of which waited for: 13 -> 19; matrix products, arithmetic and copies ran while one was open for 16% -> 14% of each run, Pallas kernels for 0% -> 15%
where the time goes in v1:
time: 344 us; the launch traced here: 341 us
  starting transfers between devices  103 us (30%)
  waiting for transfers between devices  82.1 us (24%)
  local copies, waits for them, and re-layouts  65.2 us (19%)
  Pallas kernels  58.3 us (17%)
  other arithmetic  24.6 us (7%)
  matrix products  4.33 us (1%)
  between operations  3.71 us (1%)
    ppermute x64, waiting for transfers between devices, xor(): return lax.ppermute(value, 'seq', [(i, i ^ bit) for i in range(seq_size)])  81.7 us
    pallas_call x16, Pallas kernels, vmem_call(): pl.pallas_call(kernel, out_shape=tuple(outs), in_specs=[pl.BlockSpec(memo...  58.3 us
    ppermute x64, starting transfers between devices, xor(): return lax.ppermute(value, 'seq', [(i, i ^ bit) for i in range(seq_size)])  56.7 us
    unnamed x175, local copies, waits for them, and re-layouts  39.5 us
    all_to_all x4, starting transfers between devices, members(): lax.all_to_all(value, 'seq', 0, 0, tiled=True, axis_index_groups=index)  15.3 us
    ppermute x4, starting transfers between devices, on_device(): piece = lax.ppermute(piece.astype(bf16), both, pairs).astype(f32)  12.4 us
    all_to_all x1, starting transfers between devices, on_device(): got = lax.all_to_all(everyone, both, 0, 0, tiled=True)  7.41 us
    ppermute x6, starting transfers between devices, xor_dp(): return lax.ppermute(value, 'dp', [(i, i ^ bit) for i in range(dp_size)])  7.11 us
  transfers between devices with their start and end apart: 80, of which 19 were waited for; matrix products, arithmetic and copies ran while one was open for 14% of the time, Pallas kernels for 15%

profile of v1, /device:TPU:0, one launch (start us, length us, event | category | flops | bytes accessed | tf_op | source)
XLA Modules:
  0.0 341.1 jit_solution(17487398645777346384)
XLA Ops:
  3.3 6.1 %concatenate.41 = bf16[384]{0:T(512)(128)(2,1)S(1)} concatenate(bf16[32]{0:T(256)(128)(2,1)} %param.23, bf16[32]{0:T(256)(128)(2,1)} %param.24, bf16[32]{0:T(256)(128)(2,1)} %param.26, bf16[32]{0:T(256)(128)(2,1)} %param.29, bf16[32]{0:T(256)(128)(2,1)} %param.31, bf16[32]{0:T(256)(128)(2,1)} %param.32, bf16[32]{0:T(256)(128)(2,1)} %param.33, bf16[32]{0:T(256)(128)(2,1)} %param.37, ...), dimensions={0} | concatenate | bytes 1536 | tf_op jit(solution)/shard_map/concatenate | solution.py:413
  10.7 7.4 %all-to-all-start = ((bf16[32,40,384]{2,1,0:T(8,128)(2,1)}), bf16[32,40,384]{2,1,0:T(8,128)(2,1)}, u32[]{:S(2)}, u32[]{:S(2)}) async-start(bf16[32,40,384]{2,1,0:T(8,128)(2,1)} %bitcast.9), calls=%async_computation | async-start | bytes 1966080 | tf_op jit(solution)/shard_map/all_to_all | solution.py:427
  18.2 2.7 collective-permute-start.33
  21.2 2.7 collective-permute-start
  23.8 2.4 collective-permute-start.11
  26.8 33.4 %collective-permute-done.15 = bf16[32,1024]{1,0:T(8,128)(2,1)S(1)} collective-permute-done((bf16[32,1024]{1,0:T(8,128)(2,1)S(1)}, bf16[32,1024]{1,0:T(8,128)(2,1)S(1)}, u32[]{:S(2)}, u32[]{:S(2)}) %collective-permute-start.15) | collective-permute-done | bytes 65568 | tf_op jit(solution)/shard_map/ppermute | solution.py:348
  60.2 1.5 collective-permute-start.3
  63.0 1.5 collective-permute-start.16
  65.3 5.7 %collective-permute-done.7.refs_8_ = bf16[64,1024]{1,0:T(8,128)(2,1)S(1)} collective-permute-done((bf16[64,1024]{1,0:T(8,128)(2,1)S(1)}, bf16[64,1024]{1,0:T(8,128)(2,1)S(1)}, u32[]{:S(2)}, u32[]{:S(2)}) %collective-permute-start.7) | collective-permute-done | bytes 131104 | tf_op jit(solution)/shard_map/ppermute | solution.py:348
  82.2 4.0 %all-to-all-start.2 = ((bf16[8,32,512]{2,1,0:T(8,128)(2,1)}), bf16[8,32,512]{2,1,0:T(8,128)(2,1)}, u32[]{:S(2)}, u32[]{:S(2)}) async-start(bf16[8,32,512]{2,1,0:T(8,128)(2,1)} %reshape.171), calls=%async_computation.2 | async-start | bytes 524288 | tf_op jit(solution)/shard_map/all_to_all | solution.py:403
  89.2 2.5 collective-permute-start.39
  94.1 2.5 collective-permute-start.22
  105.3 3.2 qkv.1
  113.4 1.5 collective-permute-start.42
  119.1 9.0 %attend.1 = (bf16[1024,128]{1,0:T(8,128)(2,1)}, f32[2,1024]{1,0:T(2,128)S(1)}) custom-call(s32[4]{0:T(128)S(1)} %pad_add_fusion.meta, bf16[1024,128]{1,0:T(8,128)(2,1)S(1)} %copy-done.55, bf16[1024,128]{1,0:T(8,128)(2,1)S(1)} %copy-done.58, bf16[1024,128]{1,0:T(8,128)(2,1)S(1)} %copy-done.61), custom_call_target="tpu_custom_call" | custom-call | flops 1073741824 | bytes 1056768 | tf_op jit(solution)/shard_map/attend/pallas_call | solution.py:44
  128.1 3.6 %all-to-all-start.1 = ((bf16[8,128,128]{2,1,0:T(8,128)(2,1)}), bf16[8,128,128]{2,1,0:T(8,128)(2,1)S(1)}, u32[]{:S(2)}, u32[]{:S(2)}) async-start(bf16[8,128,128]{2,1,0:T(8,128)(2,1)} %bitcast.12), calls=%async_computation.1 | async-start | bytes 524288 | tf_op jit(solution)/shard_map/all_to_all | solution.py:403
  132.9 2.1 maximum_select_fusion.2
  145.3 1.9 mid.1
  147.3 1.8 collective-permute-start.25
  149.1 1.5 collective-permute-start.27
  150.8 1.8 maximum_select_fusion.1
  152.7 3.6 %collective-permute-done.25.refs_2_ = bf16[128,1024]{1,0:T(8,128)(2,1)} collective-permute-done((bf16[128,1024]{1,0:T(8,128)(2,1)}, bf16[128,1024]{1,0:T(8,128)(2,1)}, u32[]{:S(2)}, u32[]{:S(2)}) %collective-permute-start.25) | collective-permute-done | bytes 262176 | tf_op jit(solution)/shard_map/ppermute | solution.py:348
  156.3 2.2 collective-permute-done.27.refs_4_
  158.5 4.6 %collective-permute-done.29.refs_6_ = bf16[128,1024]{1,0:T(8,128)(2,1)} collective-permute-done((bf16[128,1024]{1,0:T(8,128)(2,1)}, bf16[128,1024]{1,0:T(8,128)(2,1)}, u32[]{:S(2)}, u32[]{:S(2)}) %collective-permute-start.29) | collective-permute-done | bytes 262176 | tf_op jit(solution)/shard_map/ppermute | solution.py:348
  163.2 4.4 %down_back.1 = (bf16[1024,1024]{1,0:T(8,128)(2,1)S(1)}, f32[1024,512]{1,0:T(8,128)S(1)}) custom-call(s32[4]{0:T(128)S(1)} %pad_add_fusion.meta, bf16[128,1024]{1,0:T(8,128)(2,1)} %pad_maximum_fusion.1.refs_0_.refs_5_, bf16[128,1024]{1,0:T(8,128)(2,1)} %collective-permute-done.34.refs_1_, bf16[128,1024]{1,0:T(8,128)(2,1)} %collective-permute-done.35.refs_2_, ...), custom_call_target="tpu_custom_call" | custom-call | flops 1073741824 | bytes 7340032 | tf_op jit(solution)/shard_map/down_back/pallas_call | solution.py:44
  167.6 1.7 maximum_select_fusion
  170.2 7.3 %ffn.1 = (bf16[1024,1024]{1,0:T(8,128)(2,1)S(1)}, bf16[1024,512]{1,0:T(8,128)(2,1)S(1)}, bf16[1024,512]{1,0:T(8,128)(2,1)S(1)}, f32[512,1024]{1,0:T(8,128)S(1)},...) custom-call(s32[4]{0:T(128)S(1)} %pad_add_fusion.meta, bf16[128,1024]{1,0:T(8,128)(2,1)} %get-tuple-element.64.refs_0_, ...), custom_call_target="tpu_custom_call" | custom-call | flops 2147483648 | bytes 12587008 | tf_op jit(solution)/shard_map/ffn/pallas_call | solution.py:44
  185.2 2.9 down.1
  189.5 1.8 copy.63
  193.3 1.6 copy-done.7
  194.9 1.6 pair.4
  196.5 2.6 collective-permute-start.49
  202.3 4.3 %collective-permute-done.49.refs_1_ = bf16[128,1024]{1,0:T(8,128)(2,1)S(1)} collective-permute-done((bf16[128,1024]{1,0:T(8,128)(2,1)S(1)}, bf16[128,1024]{1,0:T(8,128)(2,1)S(1)}, u32[]{:S(2)}, u32[]{:S(2)}) %collective-permute-start.49) | collective-permute-done | bytes 262176 | tf_op jit(solution)/shard_map/ppermute | solution.py:348
  206.6 2.1 collective-permute-start.73
  208.6 7.3 %collective-permute-done.50.refs_2_ = bf16[128,1024]{1,0:T(8,128)(2,1)S(1)} collective-permute-done((bf16[128,1024]{1,0:T(8,128)(2,1)S(1)}, bf16[128,1024]{1,0:T(8,128)(2,1)S(1)}, u32[]{:S(2)}, u32[]{:S(2)}) %collective-permute-start.50) | collective-permute-done | bytes 262176 | tf_op jit(solution)/shard_map/ppermute | solution.py:348
  216.0 2.3 mid_back.1
  220.4 3.5 %all-to-all-start.3 = ((bf16[8,128,128]{2,1,0:T(8,128)(2,1)}), bf16[8,128,128]{2,1,0:T(8,128)(2,1)S(1)}, u32[]{:S(2)}, u32[]{:S(2)}) async-start(bf16[8,128,128]{2,1,0:T(8,128)(2,1)} %copy-done.36), calls=%async_computation.3 | async-start | bytes 524288 | tf_op jit(solution)/shard_map/all_to_all | solution.py:403
  223.9 1.7 bitcast_add_fusion.1
  226.5 1.9 bitcast_add_fusion.3
  228.4 2.3 pair.3
  231.5 2.9 collective-permute-start.44
  235.0 2.0 collective-permute-start.62
  237.0 13.4 %attend_back.1 = (bf16[1024,384]{1,0:T(8,128)(2,1)S(1)}, f32[512,1024]{1,0:T(8,128)S(1)}, bf16[512,1024]{1,0:T(8,128)(2,1)}, f32[1,384]{1,0:T(1,128)S(1)}) custom-call(s32[4]{0:T(128)S(1)} %pad_add_fusion.meta, bf16[1024,128]{1,0:T(8,128)(2,1)S(1)} %copy-done.56, bf16[1024,128]{1,0:T(8,128)(2,1)S(1)} %copy-done.59, bf16[1024,128]{1,0:T(8,128)(2,1)S(1)} %copy-done.62, ...), custom_call_target="tpu_custom_call" | custom-call | flops 2684354560 | bytes 5776896 | tf_op jit(solution)/shard_map/attend_back/pallas_call | solution.py:44
  252.0 1.5 collective-permute-start.64
  255.8 1.7 fusion.2
  257.6 1.9 out.1
  261.6 3.3 collective-permute-done.66
  266.4 3.9 %first_small.1 = f32[2,1024]{1,0:T(2,128)S(1)} custom-call(s32[4]{0:T(128)S(1)} %pad_add_fusion.meta, bf16[1024,1024]{1,0:T(8,128)(2,1)S(1)} %copy-done.1, bf16[1024,384]{1,0:T(8,128)(2,1)S(1)} %copy-done.16, bf16[1024,384]{1,0:T(8,128)(2,1)S(1)} %bitcast.162), custom_call_target="tpu_custom_call" | custom-call | flops 805306368 | bytes 3678208 | tf_op jit(solution)/shard_map/first_small/pallas_call | solution.py:44
  273.6 2.5 collective-permute-start.60
  277.1 4.0 %all-to-all-start.4 = ((f32[32,1,384]{2,1,0:T(1,128)}), f32[32,1,384]{2,1,0:T(1,128)}, u32[]{:S(2)}, u32[]{:S(2)}) async-start(f32[32,1,384]{2,1,0:T(1,128)} %copy.61), calls=%async_computation.4 | async-start | bytes 98304 | tf_op jit(solution)/shard_map/all_to_all | solution.py:583
  281.1 2.7 collective-permute-start.47
  283.8 1.7 place.3
  285.5 4.6 %collective-permute-done.60 = bf16[256,384]{1,0:T(8,128)(2,1)} collective-permute-done((bf16[256,384]{1,0:T(8,128)(2,1)}, bf16[256,384]{1,0:T(8,128)(2,1)}, u32[]{:S(2)}, u32[]{:S(2)}) %collective-permute-start.60) | collective-permute-done | bytes 196640 | tf_op jit(solution)/shard_map/ppermute | solution.py:348
  292.2 4.1 %all-to-all-start.5 = ((bf16[8,32,896]{2,1,0:T(8,128)(2,1)}), bf16[8,32,896]{2,1,0:T(8,128)(2,1)}, u32[]{:S(2)}, u32[]{:S(2)}) async-start(bf16[8,32,896]{2,1,0:T(8,128)(2,1)} %pad_maximum_fusion), calls=%async_computation.5 | async-start | bytes 917504 | tf_op jit(solution)/shard_map/all_to_all | solution.py:403
  297.7 5.2 %collective-permute-start.69 = (bf16[32,1024]{1,0:T(8,128)(2,1)S(1)}, bf16[32,1024]{1,0:T(8,128)(2,1)S(1)}, u32[]{:S(2)}, u32[]{:S(2)}) collective-permute-start(bf16[32,1024]{1,0:T(8,128)(2,1)S(1)} %get-tuple-element.109), channel_id=1, source_target_pairs={{0,1},{1,5},{2,9},{3,13},{4,17},{5,21},{6,25},{7,29},{8,2},{9,6},{... | collective-permute-start | bytes 196616 | tf_op jit(solution)/shard_map/ppermute | solution.py:572
  302.9 1.8 maximum_select_fusion.5
  304.8 2.3 collective-permute-start.70
  307.0 4.2 %collective-permute-start.71 = (bf16[32,1024]{1,0:T(8,128)(2,1)S(1)}, bf16[32,1024]{1,0:T(8,128)(2,1)S(1)}, u32[]{:S(2)}, u32[]{:S(2)}) collective-permute-start(bf16[32,1024]{1,0:T(8,128)(2,1)S(1)} %get-tuple-element.107), channel_id=1, source_target_pairs={{0,3},{1,7},{2,11},{3,15},{4,19},{5,23},{6,27},{7,31},{8,0},{9,4},... | collective-permute-start | bytes 196616 | tf_op jit(solution)/shard_map/ppermute | solution.py:572
  312.1 1.6 copy-done.5
  314.4 2.5 collective-permute-start.53
  316.9 3.0 collective-permute-start.54
  324.3 5.3 %collective-permute-done.54.refs_2_ = bf16[128,1024]{1,0:T(8,128)(2,1)S(1)} collective-permute-done((bf16[128,1024]{1,0:T(8,128)(2,1)S(1)}, bf16[128,1024]{1,0:T(8,128)(2,1)S(1)}, u32[]{:S(2)}, u32[]{:S(2)}) %collective-permute-start.54) | collective-permute-done | bytes 262176 | tf_op jit(solution)/shard_map/ppermute | solution.py:348
  331.2 2.2 collective-permute-start.56
  338.8 1.6 collective-permute-done.56
  (361 shorter events, 98.9 us)
Async XLA Ops:
  10.7 71.5 %all-to-all-start = ((bf16[32,40,384]{2,1,0:T(8,128)(2,1)}), bf16[32,40,384]{2,1,0:T(8,128)(2,1)}, u32[]{:S(2)}, u32[]{:S(2)}) async-start(bf16[32,40,384]{2,1,0:T(8,128)(2,1)} %bitcast.9), calls=%async_computation | async-start | bytes 1966080 | tf_op jit(solution)/shard_map/all_to_all | solution.py:427
  18.2 43.5 %collective-permute-start.33 = (bf16[64,1024]{1,0:T(8,128)(2,1)S(1)}, bf16[64,1024]{1,0:T(8,128)(2,1)S(1)}, u32[]{:S(2)}, u32[]{:S(2)}) collective-permute-start(bf16[64,1024]{1,0:T(8,128)(2,1)S(1)} %get-tuple-element.111), channel_id=1, source_target_pairs={{0,8},{1,9},{2,10},{3,11},{4,12},{5,13},{6,14},{7,15},{8,0},{9,1},... | collective-permute-start | bytes 393224 | tf_op jit(solution)/shard_map/ppermute | solution.py:348
  20.8 39.3 %collective-permute-start.15 = (bf16[32,1024]{1,0:T(8,128)(2,1)S(1)}, bf16[32,1024]{1,0:T(8,128)(2,1)S(1)}, u32[]{:S(2)}, u32[]{:S(2)}) collective-permute-start(bf16[32,1024]{1,0:T(8,128)(2,1)S(1)} %copy-done.81), channel_id=1, source_target_pairs={{0,8},{1,9},{2,10},{3,11},{4,12},{5,13},{6,14},{7,15},{8,0},{9,1},... | collective-permute-start | bytes 196616 | tf_op jit(solution)/shard_map/ppermute | solution.py:348
  21.2 41.8 %collective-permute-start = (bf16[64,1024]{1,0:T(8,128)(2,1)S(1)}, bf16[64,1024]{1,0:T(8,128)(2,1)S(1)}, u32[]{:S(2)}, u32[]{:S(2)}) collective-permute-start(bf16[64,1024]{1,0:T(8,128)(2,1)S(1)} %get-tuple-element.112), channel_id=1, source_target_pairs={{0,8},{1,9},{2,10},{3,11},{4,12},{5,13},{6,14},{7,15},{8,0},{9,1},... | collective-permute-start | bytes 393224 | tf_op jit(solution)/shard_map/ppermute | solution.py:348
  23.8 39.1 %collective-permute-start.11 = (bf16[64,1024]{1,0:T(8,128)(2,1)S(1)}, bf16[64,1024]{1,0:T(8,128)(2,1)S(1)}, u32[]{:S(2)}, u32[]{:S(2)}) collective-permute-start(bf16[64,1024]{1,0:T(8,128)(2,1)S(1)} %get-tuple-element.113.refs_0_.x_own.refs_4_), channel_id=1, source_target_pairs={{0,6},{1,7},{2,4},{3,5},{4,2},{5,3},{6,0},{7,1},{8,14},{9,15},{10,... | collective-permute-start | bytes 393224 | tf_op jit(solution)/shard_map/ppermute | solution.py:348
  26.3 49.4 %collective-permute-start.41 = (bf16[128,1024]{1,0:T(8,128)(2,1)S(1)}, bf16[128,1024]{1,0:T(8,128)(2,1)S(1)}, u32[]{:S(2)}, u32[]{:S(2)}) collective-permute-start(bf16[128,1024]{1,0:T(8,128)(2,1)S(1)} %copy-done.79), channel_id=1, source_target_pairs={{0,8},{1,9},{2,10},{3,11},{4,12},{5,13},{6,14},{7,15},{8,0},{9,1},... | collective-permute-start | bytes 786440 | tf_op jit(solution)/shard_map/ppermute | solution.py:348
  65.1 11.0 %collective-permute-start.8 = (bf16[64,1024]{1,0:T(8,128)(2,1)S(1)}, bf16[64,1024]{1,0:T(8,128)(2,1)S(1)}, u32[]{:S(2)}, u32[]{:S(2)}) collective-permute-start(bf16[64,1024]{1,0:T(8,128)(2,1)S(1)} %collective-permute-done.refs_1_.x_recv.refs_5_), channel_id=1, source_target_pairs={{0,4},{1,5},{2,6},{3,7},{4,0},{5,1},{6,2},{7,3},{8,12},{9,13},{10,... | collective-permute-start | bytes 393224 | tf_op jit(solution)/shard_map/ppermute | solution.py:348
  75.7 10.5 %collective-permute-start.2 = (bf16[64,1024]{1,0:T(8,128)(2,1)S(1)}, bf16[64,1024]{1,0:T(8,128)(2,1)S(1)}, u32[]{:S(2)}, u32[]{:S(2)}) collective-permute-start(bf16[64,1024]{1,0:T(8,128)(2,1)S(1)} %collective-permute-done.refs_1_.x_recv.refs_5_), channel_id=1, source_target_pairs={{0,1},{1,0},{2,3},{3,2},{4,5},{5,4},{6,7},{7,6},{8,9},{9,8},{10,11... | collective-permute-start | bytes 393224 | tf_op jit(solution)/shard_map/ppermute | solution.py:348
  76.2 10.6 %collective-permute-start.5 = (bf16[64,1024]{1,0:T(8,128)(2,1)S(1)}, bf16[64,1024]{1,0:T(8,128)(2,1)S(1)}, u32[]{:S(2)}, u32[]{:S(2)}) collective-permute-start(bf16[64,1024]{1,0:T(8,128)(2,1)S(1)} %collective-permute-done.3.refs_4_), channel_id=1, source_target_pairs={{0,1},{1,0},{2,3},{3,2},{4,5},{5,4},{6,7},{7,6},{8,9},{9,8},{10,11... | collective-permute-start | bytes 393224 | tf_op jit(solution)/shard_map/ppermute | solution.py:348
  77.6 11.7 %collective-permute-start.35 = (bf16[128,1024]{1,0:T(8,128)(2,1)}, bf16[128,1024]{1,0:T(8,128)(2,1)}, u32[]{:S(2)}, u32[]{:S(2)}) collective-permute-start(bf16[128,1024]{1,0:T(8,128)(2,1)} %pad_maximum_fusion.1.refs_0_.refs_5_), channel_id=1, source_target_pairs={{0,2},{1,3},{2,0},{3,1},{4,6},{5,7},{6,4},{7,5},{8,10},{9,11},{10,... | collective-permute-start | bytes 786440 | tf_op jit(solution)/shard_map/ppermute | solution.py:348
  79.4 12.4 %collective-permute-start.37 = (bf16[128,1024]{1,0:T(8,128)(2,1)}, bf16[128,1024]{1,0:T(8,128)(2,1)}, u32[]{:S(2)}, u32[]{:S(2)}) collective-permute-start(bf16[128,1024]{1,0:T(8,128)(2,1)} %pad_maximum_fusion.1.refs_0_.refs_5_), channel_id=1, source_target_pairs={{0,4},{1,5},{2,6},{3,7},{4,0},{5,1},{6,2},{7,3},{8,12},{9,13},{10,... | collective-permute-start | bytes 786440 | tf_op jit(solution)/shard_map/ppermute | solution.py:348
  82.2 32.7 %all-to-all-start.2 = ((bf16[8,32,512]{2,1,0:T(8,128)(2,1)}), bf16[8,32,512]{2,1,0:T(8,128)(2,1)}, u32[]{:S(2)}, u32[]{:S(2)}) async-start(bf16[8,32,512]{2,1,0:T(8,128)(2,1)} %reshape.171), calls=%async_computation.2 | async-start | bytes 524288 | tf_op jit(solution)/shard_map/all_to_all | solution.py:403
  87.9 10.0 %collective-permute-start.6 = (bf16[64,1024]{1,0:T(8,128)(2,1)S(1)}, bf16[64,1024]{1,0:T(8,128)(2,1)S(1)}, u32[]{:S(2)}, u32[]{:S(2)}) collective-permute-start(bf16[64,1024]{1,0:T(8,128)(2,1)S(1)} %collective-permute-done.4.refs_5_), channel_id=1, source_target_pairs={{0,1},{1,0},{2,3},{3,2},{4,5},{5,4},{6,7},{7,6},{8,9},{9,8},{10,11... | collective-permute-start | bytes 393224 | tf_op jit(solution)/shard_map/ppermute | solution.py:348
  89.2 24.1 %collective-permute-start.39 = (bf16[128,1024]{1,0:T(8,128)(2,1)}, bf16[128,1024]{1,0:T(8,128)(2,1)}, u32[]{:S(2)}, u32[]{:S(2)}) collective-permute-start(bf16[128,1024]{1,0:T(8,128)(2,1)} %pad_maximum_fusion.1.refs_0_.refs_5_), channel_id=1, source_target_pairs={{0,6},{1,7},{2,4},{3,5},{4,2},{5,3},{6,0},{7,1},{8,14},{9,15},{10,... | collective-permute-start | bytes 786440 | tf_op jit(solution)/shard_map/ppermute | solution.py:348
  91.8 23.1 %collective-permute-start.18 = (bf16[4,32,1024]{2,1,0:T(8,128)(2,1)S(1)}, bf16[4,32,1024]{2,1,0:T(8,128)(2,1)S(1)}, u32[]{:S(2)}, u32[]{:S(2)}) collective-permute-start(bf16[4,32,1024]{2,1,0:T(8,128)(2,1)S(1)} %maximum_select_fusion.4.refs_0_), channel_id=1, source_target_pairs={{0,2},{1,3},{2,0},{3,1},{4,6},{5,7},{6,4},{7,5},{8,10},{9,11},{10,... | collective-permute-start | bytes 786440 | tf_op jit(solution)/shard_map/ppermute | solution.py:348
  93.1 22.7 %collective-permute-start.20 = (bf16[4,32,1024]{2,1,0:T(8,128)(2,1)S(1)}, bf16[4,32,1024]{2,1,0:T(8,128)(2,1)S(1)}, u32[]{:S(2)}, u32[]{:S(2)}) collective-permute-start(bf16[4,32,1024]{2,1,0:T(8,128)(2,1)S(1)} %maximum_select_fusion.4.refs_0_), channel_id=1, source_target_pairs={{0,4},{1,5},{2,6},{3,7},{4,0},{5,1},{6,2},{7,3},{8,12},{9,13},{10,... | collective-permute-start | bytes 786440 | tf_op jit(solution)/shard_map/ppermute | solution.py:348
  94.1 21.6 %collective-permute-start.22 = (bf16[4,32,1024]{2,1,0:T(8,128)(2,1)S(1)}, bf16[4,32,1024]{2,1,0:T(8,128)(2,1)S(1)}, u32[]{:S(2)}, u32[]{:S(2)}) collective-permute-start(bf16[4,32,1024]{2,1,0:T(8,128)(2,1)S(1)} %maximum_select_fusion.4.refs_0_), channel_id=1, source_target_pairs={{0,6},{1,7},{2,4},{3,5},{4,2},{5,3},{6,0},{7,1},{8,14},{9,15},{10,... | collective-permute-start | bytes 786440 | tf_op jit(solution)/shard_map/ppermute | solution.py:348
  98.6 33.2 %collective-permute-start.17 = (bf16[4,32,1024]{2,1,0:T(8,128)(2,1)S(1)}, bf16[4,32,1024]{2,1,0:T(8,128)(2,1)S(1)}, u32[]{:S(2)}, u32[]{:S(2)}) collective-permute-start(bf16[4,32,1024]{2,1,0:T(8,128)(2,1)S(1)} %maximum_select_fusion.4.refs_0_), channel_id=1, source_target_pairs={{0,1},{1,0},{2,3},{3,2},{4,5},{5,4},{6,7},{7,6},{8,9},{9,8},{10,11... | collective-permute-start | bytes 786440 | tf_op jit(solution)/shard_map/ppermute | solution.py:348
  113.4 37.2 %collective-permute-start.42 = (bf16[2,128,1024]{2,1,0:T(8,128)(2,1)}, bf16[2,128,1024]{2,1,0:T(8,128)(2,1)}, u32[]{:S(2)}, u32[]{:S(2)}) collective-permute-start(bf16[2,128,1024]{2,1,0:T(8,128)(2,1)} %maximum_select_fusion.3), channel_id=1, source_target_pairs={{0,16},{16,0},{1,17},{17,1},{2,18},{18,2},{3,19},{19,3},{4,20},{20... | collective-permute-start | bytes 1572872 | tf_op jit(solution)/shard_map/ppermute | solution.py:351
  114.9 17.7 %collective-permute-start.31 = (bf16[256,512]{1,0:T(8,128)(2,1)}, bf16[256,512]{1,0:T(8,128)(2,1)}, u32[]{:S(2)}, u32[]{:S(2)}) collective-permute-start(bf16[256,512]{1,0:T(8,128)(2,1)} %bitcast.18), channel_id=1, source_target_pairs={{0,8},{1,9},{2,10},{3,11},{4,12},{5,13},{6,14},{7,15},{8,0},{9,1},... | collective-permute-start | bytes 786440 | tf_op jit(solution)/shard_map/ppermute | solution.py:348
  115.8 16.3 %collective-permute-start.19 = (bf16[4,32,1024]{2,1,0:T(8,128)(2,1)S(1)}, bf16[4,32,1024]{2,1,0:T(8,128)(2,1)S(1)}, u32[]{:S(2)}, u32[]{:S(2)}) collective-permute-start(bf16[4,32,1024]{2,1,0:T(8,128)(2,1)S(1)} %collective-permute-done.18.refs_2_), channel_id=1, source_target_pairs={{0,1},{1,0},{2,3},{3,2},{4,5},{5,4},{6,7},{7,6},{8,9},{9,8},{10,11... | collective-permute-start | bytes 786440 | tf_op jit(solution)/shard_map/ppermute | solution.py:348
  115.8 16.5 %collective-permute-start.21 = (bf16[4,32,1024]{2,1,0:T(8,128)(2,1)S(1)}, bf16[4,32,1024]{2,1,0:T(8,128)(2,1)S(1)}, u32[]{:S(2)}, u32[]{:S(2)}) collective-permute-start(bf16[4,32,1024]{2,1,0:T(8,128)(2,1)S(1)} %collective-permute-done.20.refs_4_), channel_id=1, source_target_pairs={{0,1},{1,0},{2,3},{3,2},{4,5},{5,4},{6,7},{7,6},{8,9},{9,8},{10,11... | collective-permute-start | bytes 786440 | tf_op jit(solution)/shard_map/ppermute | solution.py:348
  128.1 13.9 %all-to-all-start.1 = ((bf16[8,128,128]{2,1,0:T(8,128)(2,1)}), bf16[8,128,128]{2,1,0:T(8,128)(2,1)S(1)}, u32[]{:S(2)}, u32[]{:S(2)}) async-start(bf16[8,128,128]{2,1,0:T(8,128)(2,1)} %bitcast.12), calls=%async_computation.1 | async-start | bytes 524288 | tf_op jit(solution)/shard_map/all_to_all | solution.py:403
  132.0 15.2 %collective-permute-start.34 = (bf16[128,1024]{1,0:T(8,128)(2,1)}, bf16[128,1024]{1,0:T(8,128)(2,1)}, u32[]{:S(2)}, u32[]{:S(2)}) collective-permute-start(bf16[128,1024]{1,0:T(8,128)(2,1)} %pad_maximum_fusion.1.refs_0_.refs_5_), channel_id=1, source_target_pairs={{0,1},{1,0},{2,3},{3,2},{4,5},{5,4},{6,7},{7,6},{8,9},{9,8},{10,11... | collective-permute-start | bytes 786440 | tf_op jit(solution)/shard_map/ppermute | solution.py:348
  132.3 14.9 %collective-permute-start.36 = (bf16[128,1024]{1,0:T(8,128)(2,1)}, bf16[128,1024]{1,0:T(8,128)(2,1)}, u32[]{:S(2)}, u32[]{:S(2)}) collective-permute-start(bf16[128,1024]{1,0:T(8,128)(2,1)} %collective-permute-done.35.refs_2_), channel_id=1, source_target_pairs={{0,1},{1,0},{2,3},{3,2},{4,5},{5,4},{6,7},{7,6},{8,9},{9,8},{10,11... | collective-permute-start | bytes 786440 | tf_op jit(solution)/shard_map/ppermute | solution.py:348
  132.6 16.5 %collective-permute-start.38 = (bf16[128,1024]{1,0:T(8,128)(2,1)}, bf16[128,1024]{1,0:T(8,128)(2,1)}, u32[]{:S(2)}, u32[]{:S(2)}) collective-permute-start(bf16[128,1024]{1,0:T(8,128)(2,1)} %collective-permute-done.37.refs_4_), channel_id=1, source_target_pairs={{0,1},{1,0},{2,3},{3,2},{4,5},{5,4},{6,7},{7,6},{8,9},{9,8},{10,11... | collective-permute-start | bytes 786440 | tf_op jit(solution)/shard_map/ppermute | solution.py:348
  135.0 32.6 %collective-permute-start.32 = (bf16[2,256,512]{2,1,0:T(8,128)(2,1)}, bf16[2,256,512]{2,1,0:T(8,128)(2,1)}, u32[]{:S(2)}, u32[]{:S(2)}) collective-permute-start(bf16[2,256,512]{2,1,0:T(8,128)(2,1)} %maximum_select_fusion.2), channel_id=1, source_target_pairs={{0,16},{16,0},{1,17},{17,1},{2,18},{18,2},{3,19},{19,3},{4,20},{20... | collective-permute-start | bytes 1572872 | tf_op jit(solution)/shard_map/ppermute | solution.py:351
  150.6 12.6 %collective-permute-start.29 = (bf16[128,1024]{1,0:T(8,128)(2,1)}, bf16[128,1024]{1,0:T(8,128)(2,1)}, u32[]{:S(2)}, u32[]{:S(2)}) collective-permute-start(bf16[128,1024]{1,0:T(8,128)(2,1)} %get-tuple-element.64.refs_0_), channel_id=1, source_target_pairs={{0,6},{1,7},{2,4},{3,5},{4,2},{5,3},{6,0},{7,1},{8,14},{9,15},{10,... | collective-permute-start | bytes 786440 | tf_op jit(solution)/shard_map/ppermute | solution.py:348
  152.7 17.5 %collective-permute-start.24 = (bf16[128,1024]{1,0:T(8,128)(2,1)}, bf16[128,1024]{1,0:T(8,128)(2,1)S(1)}, u32[]{:S(2)}, u32[]{:S(2)}) collective-permute-start(bf16[128,1024]{1,0:T(8,128)(2,1)} %get-tuple-element.64.refs_0_), channel_id=1, source_target_pairs={{0,1},{1,0},{2,3},{3,2},{4,5},{5,4},{6,7},{7,6},{8,9},{9,8},{10,11... | collective-permute-start | bytes 786440 | tf_op jit(solution)/shard_map/ppermute | solution.py:348
  156.3 13.9 %collective-permute-start.26 = (bf16[128,1024]{1,0:T(8,128)(2,1)}, bf16[128,1024]{1,0:T(8,128)(2,1)S(1)}, u32[]{:S(2)}, u32[]{:S(2)}) collective-permute-start(bf16[128,1024]{1,0:T(8,128)(2,1)} %collective-permute-done.25.refs_2_), channel_id=1, source_target_pairs={{0,1},{1,0},{2,3},{3,2},{4,5},{5,4},{6,7},{7,6},{8,9},{9,8},{10,11... | collective-permute-start | bytes 786440 | tf_op jit(solution)/shard_map/ppermute | solution.py:348
  158.5 11.7 %collective-permute-start.28 = (bf16[128,1024]{1,0:T(8,128)(2,1)}, bf16[128,1024]{1,0:T(8,128)(2,1)S(1)}, u32[]{:S(2)}, u32[]{:S(2)}) collective-permute-start(bf16[128,1024]{1,0:T(8,128)(2,1)} %collective-permute-done.27.refs_4_), channel_id=1, source_target_pairs={{0,1},{1,0},{2,3},{3,2},{4,5},{5,4},{6,7},{7,6},{8,9},{9,8},{10,11... | collective-permute-start | bytes 786440 | tf_op jit(solution)/shard_map/ppermute | solution.py:348
  177.6 15.7 %collective-permute-start.48 = (bf16[512,1024]{1,0:T(8,128)(2,1)}, bf16[512,1024]{1,0:T(8,128)(2,1)}, u32[]{:S(2)}, u32[]{:S(2)}) collective-permute-start(bf16[512,1024]{1,0:T(8,128)(2,1)} %get-tuple-element.77), channel_id=1, source_target_pairs={{0,1},{1,0},{2,3},{3,2},{4,5},{5,4},{6,7},{7,6},{8,9},{9,8},{10,11... | collective-permute-start | bytes 3145736 | tf_op jit(solution)/shard_map/ppermute | solution.py:348
  180.4 19.3 %collective-permute-start.72 = (bf16[2,128,1024]{2,1,0:T(8,128)(2,1)}, bf16[2,128,1024]{2,1,0:T(8,128)(2,1)}, u32[]{:S(2)}, u32[]{:S(2)}) collective-permute-start(bf16[2,128,1024]{2,1,0:T(8,128)(2,1)} %fusion.1), channel_id=1, source_target_pairs={{0,16},{16,0},{1,17},{17,1},{2,18},{18,2},{3,19},{19,3},{4,20},{20... | collective-permute-start | bytes 1572872 | tf_op jit(solution)/shard_map/ppermute | solution.py:351
  184.6 39.3 %collective-permute-start.57 = (bf16[2,256,512]{2,1,0:T(8,128)(2,1)}, bf16[2,256,512]{2,1,0:T(8,128)(2,1)}, u32[]{:S(2)}, u32[]{:S(2)}) collective-permute-start(bf16[2,256,512]{2,1,0:T(8,128)(2,1)} %fusion), channel_id=1, source_target_pairs={{0,16},{16,0},{1,17},{17,1},{2,18},{18,2},{3,19},{19,3},{4,20},{20... | collective-permute-start | bytes 1572872 | tf_op jit(solution)/shard_map/ppermute | solution.py:351
  189.5 38.9 %collective-permute-start.43 = (bf16[512,1024]{1,0:T(8,128)(2,1)}, bf16[512,1024]{1,0:T(8,128)(2,1)}, u32[]{:S(2)}, u32[]{:S(2)}) collective-permute-start(bf16[512,1024]{1,0:T(8,128)(2,1)} %get-tuple-element.68), channel_id=1, source_target_pairs={{0,1},{1,0},{2,3},{3,2},{4,5},{5,4},{6,7},{7,6},{8,9},{9,8},{10,11... | collective-permute-start | bytes 3145736 | tf_op jit(solution)/shard_map/ppermute | solution.py:348
  196.5 10.1 %collective-permute-start.49 = (bf16[128,1024]{1,0:T(8,128)(2,1)S(1)}, bf16[128,1024]{1,0:T(8,128)(2,1)S(1)}, u32[]{:S(2)}, u32[]{:S(2)}) collective-permute-start(bf16[128,1024]{1,0:T(8,128)(2,1)S(1)} %get-tuple-element.79), channel_id=1, source_target_pairs={{0,6},{1,7},{2,4},{3,5},{4,2},{5,3},{6,0},{7,1},{8,14},{9,15},{10,... | collective-permute-start | bytes 786440 | tf_op jit(solution)/shard_map/ppermute | solution.py:348
  199.1 16.8 %collective-permute-start.50 = (bf16[128,1024]{1,0:T(8,128)(2,1)S(1)}, bf16[128,1024]{1,0:T(8,128)(2,1)S(1)}, u32[]{:S(2)}, u32[]{:S(2)}) collective-permute-start(bf16[128,1024]{1,0:T(8,128)(2,1)S(1)} %get-tuple-element.80), channel_id=1, source_target_pairs={{0,4},{1,5},{2,6},{3,7},{4,0},{5,1},{6,2},{7,3},{8,12},{9,13},{10,... | collective-permute-start | bytes 786440 | tf_op jit(solution)/shard_map/ppermute | solution.py:348
  199.7 16.3 %collective-permute-start.51 = (bf16[128,1024]{1,0:T(8,128)(2,1)S(1)}, bf16[128,1024]{1,0:T(8,128)(2,1)S(1)}, u32[]{:S(2)}, u32[]{:S(2)}) collective-permute-start(bf16[128,1024]{1,0:T(8,128)(2,1)S(1)} %get-tuple-element.81), channel_id=1, source_target_pairs={{0,2},{1,3},{2,0},{3,1},{4,6},{5,7},{6,4},{7,5},{8,10},{9,11},{10,... | collective-permute-start | bytes 786440 | tf_op jit(solution)/shard_map/ppermute | solution.py:348
  206.6 19.9 %collective-permute-start.73 = (bf16[128,1024]{1,0:T(8,128)(2,1)}, bf16[128,1024]{1,0:T(8,128)(2,1)}, u32[]{:S(2)}, u32[]{:S(2)}) collective-permute-start(bf16[128,1024]{1,0:T(8,128)(2,1)} %fusion.6), channel_id=1, source_target_pairs={{0,8},{1,9},{2,10},{3,11},{4,12},{5,13},{6,14},{7,15},{8,0},{9,1},... | collective-permute-start | bytes 786440 | tf_op jit(solution)/shard_map/ppermute | solution.py:348
  220.4 16.6 %all-to-all-start.3 = ((bf16[8,128,128]{2,1,0:T(8,128)(2,1)}), bf16[8,128,128]{2,1,0:T(8,128)(2,1)S(1)}, u32[]{:S(2)}, u32[]{:S(2)}) async-start(bf16[8,128,128]{2,1,0:T(8,128)(2,1)} %copy-done.36), calls=%async_computation.3 | async-start | bytes 524288 | tf_op jit(solution)/shard_map/all_to_all | solution.py:403
  226.5 25.5 %collective-permute-start.58 = (bf16[256,512]{1,0:T(8,128)(2,1)}, bf16[256,512]{1,0:T(8,128)(2,1)}, u32[]{:S(2)}, u32[]{:S(2)}) collective-permute-start(bf16[256,512]{1,0:T(8,128)(2,1)} %fusion.5), channel_id=1, source_target_pairs={{0,8},{1,9},{2,10},{3,11},{4,12},{5,13},{6,14},{7,15},{8,0},{9,1},... | collective-permute-start | bytes 786440 | tf_op jit(solution)/shard_map/ppermute | solution.py:348
  231.5 22.0 %collective-permute-start.44 = (bf16[128,1024]{1,0:T(8,128)(2,1)}, bf16[128,1024]{1,0:T(8,128)(2,1)}, u32[]{:S(2)}, u32[]{:S(2)}) collective-permute-start(bf16[128,1024]{1,0:T(8,128)(2,1)} %get-tuple-element.70), channel_id=1, source_target_pairs={{0,6},{1,7},{2,4},{3,5},{4,2},{5,3},{6,0},{7,1},{8,14},{9,15},{10,... | collective-permute-start | bytes 786440 | tf_op jit(solution)/shard_map/ppermute | solution.py:348
  234.4 20.0 %collective-permute-start.45 = (bf16[128,1024]{1,0:T(8,128)(2,1)}, bf16[128,1024]{1,0:T(8,128)(2,1)}, u32[]{:S(2)}, u32[]{:S(2)}) collective-permute-start(bf16[128,1024]{1,0:T(8,128)(2,1)} %get-tuple-element.71), channel_id=1, source_target_pairs={{0,4},{1,5},{2,6},{3,7},{4,0},{5,1},{6,2},{7,3},{8,12},{9,13},{10,... | collective-permute-start | bytes 786440 | tf_op jit(solution)/shard_map/ppermute | solution.py:348
  234.9 22.6 %collective-permute-start.46 = (bf16[128,1024]{1,0:T(8,128)(2,1)}, bf16[128,1024]{1,0:T(8,128)(2,1)}, u32[]{:S(2)}, u32[]{:S(2)}) collective-permute-start(bf16[128,1024]{1,0:T(8,128)(2,1)} %get-tuple-element.72), channel_id=1, source_target_pairs={{0,2},{1,3},{2,0},{3,1},{4,6},{5,7},{6,4},{7,5},{8,10},{9,11},{10,... | collective-permute-start | bytes 786440 | tf_op jit(solution)/shard_map/ppermute | solution.py:348
  235.0 25.1 %collective-permute-start.62 = (bf16[128,1024]{1,0:T(8,128)(2,1)}, bf16[128,1024]{1,0:T(8,128)(2,1)}, u32[]{:S(2)}, u32[]{:S(2)}) collective-permute-start(bf16[128,1024]{1,0:T(8,128)(2,1)} %get-tuple-element.101), channel_id=1, source_target_pairs={{0,2},{1,3},{2,0},{3,1},{4,6},{5,7},{6,4},{7,5},{8,10},{9,11},{10,... | collective-permute-start | bytes 786440 | tf_op jit(solution)/shard_map/ppermute | solution.py:348
  252.0 9.6 %collective-permute-start.64 = (bf16[128,1024]{1,0:T(8,128)(2,1)}, bf16[128,1024]{1,0:T(8,128)(2,1)}, u32[]{:S(2)}, u32[]{:S(2)}) collective-permute-start(bf16[128,1024]{1,0:T(8,128)(2,1)} %get-tuple-element.101), channel_id=1, source_target_pairs={{0,4},{1,5},{2,6},{3,7},{4,0},{5,1},{6,2},{7,3},{8,12},{9,13},{10,... | collective-permute-start | bytes 786440 | tf_op jit(solution)/shard_map/ppermute | solution.py:348
  253.4 11.4 %collective-permute-start.66 = (bf16[128,1024]{1,0:T(8,128)(2,1)}, bf16[128,1024]{1,0:T(8,128)(2,1)}, u32[]{:S(2)}, u32[]{:S(2)}) collective-permute-start(bf16[128,1024]{1,0:T(8,128)(2,1)} %get-tuple-element.101), channel_id=1, source_target_pairs={{0,6},{1,7},{2,4},{3,5},{4,2},{5,3},{6,0},{7,1},{8,14},{9,15},{10,... | collective-permute-start | bytes 786440 | tf_op jit(solution)/shard_map/ppermute | solution.py:348
  254.4 15.9 %collective-permute-start.59 = (bf16[2,256,384]{2,1,0:T(8,128)(2,1)}, bf16[2,256,384]{2,1,0:T(8,128)(2,1)}, u32[]{:S(2)}, u32[]{:S(2)}) collective-permute-start(bf16[2,256,384]{2,1,0:T(8,128)(2,1)} %fusion.3), channel_id=1, source_target_pairs={{0,16},{16,0},{1,17},{17,1},{2,18},{18,2},{3,19},{19,3},{4,20},{20... | collective-permute-start | bytes 1179656 | tf_op jit(solution)/shard_map/ppermute | solution.py:351
  257.6 16.0 %collective-permute-start.61 = (bf16[128,1024]{1,0:T(8,128)(2,1)}, bf16[128,1024]{1,0:T(8,128)(2,1)}, u32[]{:S(2)}, u32[]{:S(2)}) collective-permute-start(bf16[128,1024]{1,0:T(8,128)(2,1)} %get-tuple-element.101), channel_id=1, source_target_pairs={{0,1},{1,0},{2,3},{3,2},{4,5},{5,4},{6,7},{7,6},{8,9},{9,8},{10,11... | collective-permute-start | bytes 786440 | tf_op jit(solution)/shard_map/ppermute | solution.py:348
  260.1 21.0 %collective-permute-start.63 = (bf16[128,1024]{1,0:T(8,128)(2,1)}, bf16[128,1024]{1,0:T(8,128)(2,1)S(1)}, u32[]{:S(2)}, u32[]{:S(2)}) collective-permute-start(bf16[128,1024]{1,0:T(8,128)(2,1)} %collective-permute-done.62), channel_id=1, source_target_pairs={{0,1},{1,0},{2,3},{3,2},{4,5},{5,4},{6,7},{7,6},{8,9},{9,8},{10,11... | collective-permute-start | bytes 786440 | tf_op jit(solution)/shard_map/ppermute | solution.py:348
  261.6 22.2 %collective-permute-start.65 = (bf16[128,1024]{1,0:T(8,128)(2,1)}, bf16[128,1024]{1,0:T(8,128)(2,1)}, u32[]{:S(2)}, u32[]{:S(2)}) collective-permute-start(bf16[128,1024]{1,0:T(8,128)(2,1)} %collective-permute-done.64), channel_id=1, source_target_pairs={{0,1},{1,0},{2,3},{3,2},{4,5},{5,4},{6,7},{7,6},{8,9},{9,8},{10,11... | collective-permute-start | bytes 786440 | tf_op jit(solution)/shard_map/ppermute | solution.py:348
  264.9 18.9 %collective-permute-start.67 = (bf16[128,1024]{1,0:T(8,128)(2,1)}, bf16[128,1024]{1,0:T(8,128)(2,1)}, u32[]{:S(2)}, u32[]{:S(2)}) collective-permute-start(bf16[128,1024]{1,0:T(8,128)(2,1)} %collective-permute-done.66), channel_id=1, source_target_pairs={{0,1},{1,0},{2,3},{3,2},{4,5},{5,4},{6,7},{7,6},{8,9},{9,8},{10,11... | collective-permute-start | bytes 786440 | tf_op jit(solution)/shard_map/ppermute | solution.py:348
  270.3 41.7 %collective-permute-start.52 = (bf16[512,1024]{1,0:T(8,128)(2,1)}, bf16[512,1024]{1,0:T(8,128)(2,1)S(1)}, u32[]{:S(2)}, u32[]{:S(2)}) collective-permute-start(bf16[512,1024]{1,0:T(8,128)(2,1)} %get-tuple-element.85), channel_id=1, source_target_pairs={{0,1},{1,0},{2,3},{3,2},{4,5},{5,4},{6,7},{7,6},{8,9},{9,8},{10,11... | collective-permute-start | bytes 3145736 | tf_op jit(solution)/shard_map/ppermute | solution.py:348
  273.6 16.5 %collective-permute-start.60 = (bf16[256,384]{1,0:T(8,128)(2,1)}, bf16[256,384]{1,0:T(8,128)(2,1)}, u32[]{:S(2)}, u32[]{:S(2)}) collective-permute-start(bf16[256,384]{1,0:T(8,128)(2,1)} %fusion.7), channel_id=1, source_target_pairs={{0,8},{1,9},{2,10},{3,11},{4,12},{5,13},{6,14},{7,15},{8,0},{9,1},... | collective-permute-start | bytes 589832 | tf_op jit(solution)/shard_map/ppermute | solution.py:348
  277.1 15.1 %all-to-all-start.4 = ((f32[32,1,384]{2,1,0:T(1,128)}), f32[32,1,384]{2,1,0:T(1,128)}, u32[]{:S(2)}, u32[]{:S(2)}) async-start(f32[32,1,384]{2,1,0:T(1,128)} %copy.61), calls=%async_computation.4 | async-start | bytes 98304 | tf_op jit(solution)/shard_map/all_to_all | solution.py:583
  281.1 21.8 %collective-permute-start.47 = (bf16[64,1024]{1,0:T(8,128)(2,1)}, bf16[64,1024]{1,0:T(8,128)(2,1)}, u32[]{:S(2)}, u32[]{:S(2)}) collective-permute-start(bf16[64,1024]{1,0:T(8,128)(2,1)} %get-tuple-element.75), channel_id=1, source_target_pairs={{0,8},{1,9},{2,10},{3,11},{4,12},{5,13},{6,14},{7,15},{8,0},{9,1},... | collective-permute-start | bytes 393224 | tf_op jit(solution)/shard_map/ppermute | solution.py:348
  292.2 41.1 %all-to-all-start.5 = ((bf16[8,32,896]{2,1,0:T(8,128)(2,1)}), bf16[8,32,896]{2,1,0:T(8,128)(2,1)}, u32[]{:S(2)}, u32[]{:S(2)}) async-start(bf16[8,32,896]{2,1,0:T(8,128)(2,1)} %pad_maximum_fusion), calls=%async_computation.5 | async-start | bytes 917504 | tf_op jit(solution)/shard_map/all_to_all | solution.py:403
  296.9 20.0 %collective-permute-start.68 = (bf16[32,1024]{1,0:T(8,128)(2,1)S(1)}, bf16[32,1024]{1,0:T(8,128)(2,1)S(1)}, u32[]{:S(2)}, u32[]{:S(2)}) collective-permute-start(bf16[32,1024]{1,0:T(8,128)(2,1)S(1)} %get-tuple-element.106), channel_id=1, source_target_pairs={{0,0},{1,4},{2,8},{3,12},{4,16},{5,20},{6,24},{7,28},{8,1},{9,5},{... | collective-permute-start | bytes 196616 | tf_op jit(solution)/shard_map/ppermute | solution.py:572
  297.7 22.2 %collective-permute-start.69 = (bf16[32,1024]{1,0:T(8,128)(2,1)S(1)}, bf16[32,1024]{1,0:T(8,128)(2,1)S(1)}, u32[]{:S(2)}, u32[]{:S(2)}) collective-permute-start(bf16[32,1024]{1,0:T(8,128)(2,1)S(1)} %get-tuple-element.109), channel_id=1, source_target_pairs={{0,1},{1,5},{2,9},{3,13},{4,17},{5,21},{6,25},{7,29},{8,2},{9,6},{... | collective-permute-start | bytes 196616 | tf_op jit(solution)/shard_map/ppermute | solution.py:572
  304.8 17.7 %collective-permute-start.70 = (bf16[32,1024]{1,0:T(8,128)(2,1)S(1)}, bf16[32,1024]{1,0:T(8,128)(2,1)S(1)}, u32[]{:S(2)}, u32[]{:S(2)}) collective-permute-start(bf16[32,1024]{1,0:T(8,128)(2,1)S(1)} %get-tuple-element.108), channel_id=1, source_target_pairs={{0,2},{1,6},{2,10},{3,14},{4,18},{5,22},{6,26},{7,30},{8,3},{9,7},... | collective-permute-start | bytes 196616 | tf_op jit(solution)/shard_map/ppermute | solution.py:572
  307.0 15.4 %collective-permute-start.71 = (bf16[32,1024]{1,0:T(8,128)(2,1)S(1)}, bf16[32,1024]{1,0:T(8,128)(2,1)S(1)}, u32[]{:S(2)}, u32[]{:S(2)}) collective-permute-start(bf16[32,1024]{1,0:T(8,128)(2,1)S(1)} %get-tuple-element.107), channel_id=1, source_target_pairs={{0,3},{1,7},{2,11},{3,15},{4,19},{5,23},{6,27},{7,31},{8,0},{9,4},... | collective-permute-start | bytes 196616 | tf_op jit(solution)/shard_map/ppermute | solution.py:572
  314.4 9.9 %collective-permute-start.53 = (bf16[128,1024]{1,0:T(8,128)(2,1)S(1)}, bf16[128,1024]{1,0:T(8,128)(2,1)S(1)}, u32[]{:S(2)}, u32[]{:S(2)}) collective-permute-start(bf16[128,1024]{1,0:T(8,128)(2,1)S(1)} %get-tuple-element.87), channel_id=1, source_target_pairs={{0,6},{1,7},{2,4},{3,5},{4,2},{5,3},{6,0},{7,1},{8,14},{9,15},{10,... | collective-permute-start | bytes 786440 | tf_op jit(solution)/shard_map/ppermute | solution.py:348
  316.9 12.8 %collective-permute-start.54 = (bf16[128,1024]{1,0:T(8,128)(2,1)S(1)}, bf16[128,1024]{1,0:T(8,128)(2,1)S(1)}, u32[]{:S(2)}, u32[]{:S(2)}) collective-permute-start(bf16[128,1024]{1,0:T(8,128)(2,1)S(1)} %get-tuple-element.88), channel_id=1, source_target_pairs={{0,4},{1,5},{2,6},{3,7},{4,0},{5,1},{6,2},{7,3},{8,12},{9,13},{10,... | collective-permute-start | bytes 786440 | tf_op jit(solution)/shard_map/ppermute | solution.py:348
  319.9 10.3 %collective-permute-start.55 = (bf16[128,1024]{1,0:T(8,128)(2,1)S(1)}, bf16[128,1024]{1,0:T(8,128)(2,1)S(1)}, u32[]{:S(2)}, u32[]{:S(2)}) collective-permute-start(bf16[128,1024]{1,0:T(8,128)(2,1)S(1)} %get-tuple-element.89), channel_id=1, source_target_pairs={{0,2},{1,3},{2,0},{3,1},{4,6},{5,7},{6,4},{7,5},{8,10},{9,11},{10,... | collective-permute-start | bytes 786440 | tf_op jit(solution)/shard_map/ppermute | solution.py:348
  (100 other events, 809.6 us)

commit v2 on v1

v2 whole, which is shorter than its diff:
```python
import functools

import jax
import jax.numpy as jnp
from jax import lax
from jax.experimental import pallas as pl
from jax.experimental.pallas import tpu as pltpu
from jax.sharding import PartitionSpec as P

HEAD = 64
f32 = jnp.float32
bf16 = jnp.bfloat16
norm_eps = 1e-05
inv_root_two = 0.7071067811865476
inv_root_tau = 0.3989422804014327
NN = (((1,), (0,)), ((), ()))
NT = (((1,), (1,)), ((), ()))
TN = (((0,), (0,)), ((), ()))
MIB = 1024 * 1024


def dot(a, b, dims=NN):
    return lax.dot_general(a, b, dims, preferred_element_type=f32)


def normalize(rows):
    average = jnp.mean(rows, axis=-1, keepdims=True)
    centered = rows - average
    inv_std = lax.rsqrt(jnp.mean(centered * centered, axis=-1, keepdims=True) + norm_eps)
    return centered * inv_std, inv_std


def norm_back(grad_rows, scaled, inv_std, gain):
    grad_hat = grad_rows * gain
    return inv_std * (
        grad_hat
        - jnp.mean(grad_hat, axis=-1, keepdims=True)
        - scaled * jnp.mean(grad_hat * scaled, axis=-1, keepdims=True)
    )


def sds(shape, dtype):
    return jax.ShapeDtypeStruct(shape, dtype)


def vmem(like):
    return pltpu.VMEM(like.shape, like.dtype)


class Near:
    def __init__(self, array):
        self.array = array
        self.shape, self.dtype = array.shape, array.dtype


def near(arrays):
    return [Near(a) for a in arrays]


class Place:
    def __init__(self, slots, n):
        seq_at = lax.axis_index("seq")
        self.h, self.j = seq_at // n, seq_at % n
        self.group = lax.axis_index("dp") * slots + self.h
        self.length = None


def call(grid, kernel, args, outs, name, flops=0, scratch=(), sems=1, limit=24, lengths=()):
    here = pl.BlockSpec(memory_space=pltpu.HBM)
    anywhere = pl.BlockSpec(memory_space=pl.ANY)
    scalars = pl.BlockSpec(memory_space=pltpu.SMEM)
    nbytes = sum(a.shape[0] * a.shape[1] * a.dtype.itemsize for a in list(args) + list(outs))

    def body(*refs):
        place = Place(*grid)
        if lengths:
            order_ref, lengths_ref = refs[:2]
            place.length = lengths_ref[order_ref[place.h]]
        kernel(place, *refs[len(lengths) :])

    return pl.pallas_call(
        body,
        out_shape=tuple(o.array if isinstance(o, Near) else pltpu.HBM(o.shape, o.dtype) for o in outs),
        in_specs=[scalars] * len(lengths) + [anywhere if isinstance(a, Near) else here for a in args],
        out_specs=tuple(anywhere if isinstance(o, Near) else here for o in outs),
        scratch_shapes=list(scratch) + [pltpu.SemaphoreType.DMA((sems,))],
        compiler_params=pltpu.CompilerParams(vmem_limit_bytes=limit * MIB),
        cost_estimate=pl.CostEstimate(flops=int(flops), bytes_accessed=int(nbytes), transcendentals=0),
        name=name,
    )(
        *lengths,
        *[a.array if isinstance(a, Near) else pltpu.with_memory_space_constraint(a, pltpu.HBM) for a in args],
    )


class Mover:
    def __init__(self, sems):
        self.sems, self.used, self.open = sems, 0, []

    def start(self, source, target):
        copy = pltpu.make_async_copy(source, target, self.sems.at[self.used])
        self.used += 1
        copy.start()
        return copy

    def put(self, source, target):
        self.open.append(self.start(source, target))

    def drain(self):
        for copy in self.open:
            copy.wait()
        self.open = []


def cost(microseconds):
    return microseconds * 1150 * 10**6


def after(value, *others):
    return lax.optimization_barrier((value,) + others)[0]


def rows_at(index, rows):
    return pl.ds(pl.multiple_of(index * rows, rows), rows)


def pack_kernel(n, groups, first_row, place, *refs):
    frames, out_grad, wq, wk, wv, up = refs[:6]
    small = refs[6:15]
    x_own, x_send, dy_own, dy_send, packed, q_s, k_s, v_s, up_s, *rest = refs[15:]
    small_s, packed_s, sems = rest[:9], rest[9], rest[10]
    move = Mover(sems)
    for rows, own, sent in ((frames, x_own, x_send), (out_grad, dy_own, dy_send)):
        move.put(rows.at[1 - place.h], sent)
        move.put(rows.at[place.h], own)
    loads = [move.start(a, b) for a, b in ((wq, q_s), (wk, k_s), (wv, v_s), (up, up_s))]
    loads += [move.start(a, b) for a, b in zip(small, small_s)]
    for copy in loads:
        copy.wait()
    rs = wq.shape[0]
    hd = wq.shape[1] // n
    chunk = small[8].shape[1]
    zeros = jnp.zeros((packed_s.shape[1] - rs, packed_s.shape[2]), bf16)
    for m in range(n):
        cols = slice(m * hd, (m + 1) * hd)
        packed_s[m, rs:, :] = zeros
        packed_s[m, :rs, :hd] = q_s[:, cols]
        packed_s[m, :rs, hd : 2 * hd] = k_s[:, cols]
        packed_s[m, :rs, 2 * hd : 3 * hd] = v_s[:, cols]
        for g in range(groups):
            at = (g * n + m) * chunk
            packed_s[m, :rs, 3 * hd + g * chunk : 3 * hd + (g + 1) * chunk] = up_s[:, at : at + chunk]
        for i in range(8):
            packed_s[m, first_row + i : first_row + i + 1, :rs] = small_s[i][...]
        packed_s[m, first_row : first_row + 1, hd : hd + chunk] = small_s[8][...]
    move.put(packed_s, packed)
    move.drain()


def join_kernel(n, place, got, out_w, down, attn, ffn, got_s, out_s, attn_s, up_s, sems):
    move = Mover(sems)
    load, more = move.start(got, got_s), move.start(out_w, out_s)
    width, mine = down.shape[1], ffn.shape[1]
    chunk = down.shape[0]
    feats = ffn.shape[0] - width // mine * chunk
    for c in range(width // mine):
        move.put(down.at[:, c * mine : (c + 1) * mine], ffn.at[feats + c * chunk : feats + (c + 1) * chunk, :])
    load.wait()
    more.wait()
    hd = width // n
    rs = feats // n
    attn_s[:, :, : 3 * hd] = got_s[:, :, : 3 * hd]
    attn_s[:, :, 3 * hd :] = jnp.zeros((n, attn_s.shape[1], hd), bf16)
    for m in range(n):
        attn_s[m, :rs, 3 * hd :] = out_s[:, m * hd : (m + 1) * hd]
    move.put(attn_s, attn)
    for m in range(n):
        up_s[m * rs : (m + 1) * rs, :] = got_s[m, :rs, 3 * hd :]
    move.put(up_s, ffn.at[:feats, :])
    move.drain()


def key_mask(place, rows, n, half, width):
    row = lax.broadcasted_iota(jnp.int32, (rows, width), 0)
    member = row // (2 * half)
    inside = row % (2 * half)
    own = (inside < half).astype(jnp.int32)
    h = place.h
    block_half = own * h + (1 - own) * (1 - h)
    frame = (block_half * n + member) * half + inside % half
    return frame < place.length


def first_kernel(n, groups, half, qb, first_row, place, *refs):
    xs, gots = refs[:n], refs[n : n + groups]
    outs = refs[n + groups : n + groups + 11]
    hat_out, h_out, qkv_out, o_out, lse_out, w_out, vec_out, bias_up_out, wo_out, keep, send = outs
    x_s, hat_s, h_s, qkv_s, o_s, lse_s, got_s, w_s, vec_s, bias_up_s, wo_s, keep_s, send_s, bias, sems = refs[
        n + groups + 11 :
    ]
    move = Mover(sems)
    j = place.j
    rows = 2 * half
    total = n * rows
    ndev = got_s.shape[0]
    hd = got_s.shape[2] // 4
    rs = x_s.shape[1] // ndev
    chunk = bias_up_s.shape[1] // groups
    load = [move.start(gots[i], got_s.at[pl.ds((place.group ^ i) * n, n)]) for i in range(groups)]
    copies = [move.start(xs[r], x_s.at[rows_at(j ^ r, rows), :]) for r in range(n)]
    bias[...] = jnp.where(key_mask(place, total, n, half, 128), 0.0, -1.0).astype(f32)
    for copy in load:
        copy.wait()
    for d in range(ndev):
        w_s[d * rs : (d + 1) * rs, :] = got_s[d, :rs, : 3 * hd]
        at = slice(d % n * hd, (d % n + 1) * hd)
        wo_s[d // n * rs : (d // n + 1) * rs, at] = got_s[d, :rs, 3 * hd :]
        vec_s[:, d * rs : (d + 1) * rs] = got_s[d, first_row : first_row + 8, :rs].astype(f32)
    bq, bv = [], []
    for t in range(groups):
        bias_up_s[:, t * chunk : (t + 1) * chunk] = got_s[
            t * n + j, first_row : first_row + 1, hd : hd + chunk
        ].astype(f32)
        bq.append(got_s[j * groups + t, first_row + 2 : first_row + 3, :rs].astype(f32))
        bv.append(got_s[j * groups + t, first_row + 3 : first_row + 4, :rs].astype(f32))
    bq = jnp.concatenate(bq, axis=1)
    bv = jnp.concatenate(bv, axis=1)
    move.put(w_s, w_out)
    move.put(vec_s, vec_out)
    move.put(bias_up_s, bias_up_out)
    for r in range(n):
        copies[r].wait()
        base = pl.multiple_of((j ^ r) * rows, rows)
        for part in range(2):
            at = pl.ds(base + part * half, half)
            scaled, _ = normalize(x_s[at, :].astype(f32))
            hat_s[at, :] = scaled.astype(bf16)
            h_s[at, :] = (scaled * vec_s[0:1, :] + vec_s[1:2, :]).astype(bf16)
        at = pl.ds(base, rows)
        qkv = dot(h_s[at, :], w_s[...])
        qkv_s[at, :hd] = ((qkv[:, :hd] + bq) * 0.125).astype(bf16)
        qkv_s[at, hd : 2 * hd] = qkv[:, hd : 2 * hd].astype(bf16)
        qkv_s[at, 2 * hd :] = (qkv[:, 2 * hd :] + bv).astype(bf16)
    move.put(hat_s, hat_out)
    move.put(h_s, h_out)
    move.put(qkv_s, qkv_out)
    heads = hd // HEAD
    for head in range(heads):
        cols = slice(head * HEAD, (head + 1) * HEAD)
        kh = qkv_s[:, hd + head * HEAD : hd + (head + 1) * HEAD]
        vt = qkv_s[:, 2 * hd + head * HEAD : 2 * hd + (head + 1) * HEAD].astype(f32).T.astype(bf16)

        def step(i, _, cols=cols, kh=kh, vt=vt, head=head):
            at = rows_at(i, qb)
            scores = dot(kh, qkv_s[at, cols], NT)
            scores = jnp.where(bias[:, 0:1] >= 0.0, scores, -1e30)
            row_max = jnp.max(scores, axis=0, keepdims=True)
            e = jnp.exp(scores - row_max)
            row_sum = jnp.sum(e, axis=0, keepdims=True)
            ot = dot(vt, e.astype(bf16)) / row_sum
            o_s[at, cols] = ot.T.astype(bf16)
            lse_s[pl.ds(head, 1), at] = row_max + jnp.log(row_sum)
            return 0

        lax.fori_loop(0, total // qb, step, 0)
    move.put(o_s, o_out)
    move.put(lse_s, lse_out)
    move.put(wo_s, wo_out)
    for r in list(range(1, n, 2)) + list(range(0, n, 2)):
        y = dot(o_s[rows_at(j ^ r, rows), :], wo_s[...])
        here = slice((r // 2) * rows, (r // 2 + 1) * rows)
        if r % 2 == 0:
            keep_s[here, :] = y
            move.put(keep_s.at[here, :], keep.at[here, :])
        else:
            send_s[here, :] = y.astype(bf16)
            move.put(send_s.at[here, :], send.at[here, :])
    move.drain()


def mid_kernel(count, place, *refs):
    ins, x, vec = refs[:count], refs[count], refs[count + 1]
    y_out, h_out = refs[count + 2 : count + 4]
    held = refs[count + 4 : 2 * count + 4]
    x_s, vec_s, y_s, h_s, sems = refs[2 * count + 4 :]
    move = Mover(sems)
    loads = [move.start(a, b) for a, b in zip(ins, held)]
    loads += [move.start(x, x_s), move.start(vec, vec_s)]
    for copy in loads:
        copy.wait()
    y = held[0][...]
    for i in range(1, count):
        y = y + held[i][...].astype(f32)
    y = x_s[...].astype(f32) + y + vec_s[4:5, :]
    y_s[...] = y
    scaled, _ = normalize(y)
    h_s[...] = (scaled * vec_s[5:6, :] + vec_s[6:7, :]).astype(bf16)
    move.put(h_s, h_out)
    move.put(y_s, y_out)
    move.drain()


def down_back_kernel(n, groups, place, *refs):
    dys, ws = refs[:n], refs[n : n + groups]
    dy_out, dg_out, w_up_out, w_down_out, dy_s, dg_s, w_up, w_down, sems = refs[n + groups :]
    move = Mover(sems)
    j, g = place.j, place.group
    rows = dys[0].shape[0]
    chunk = w_down.shape[0] // groups
    mine = w_up.shape[1]
    feats = w_up.shape[0] // groups
    first, last = [], []
    for i in range(groups):
        for c in range(w_down.shape[1] // mine):
            source = ws[i].at[feats + c * chunk : feats + (c + 1) * chunk, :]
            first.append(move.start(source, w_down.at[rows_at(g ^ i, chunk), c * mine : (c + 1) * mine]))
    copies = [move.start(dys[r], dy_s.at[rows_at(j ^ r, rows), :]) for r in range(n)]
    for i in range(groups):
        last.append(move.start(ws[i].at[:feats, :], w_up.at[rows_at(g ^ i, feats), :]))
    for copy in first:
        copy.wait()
    move.put(w_down, w_down_out)
    for r in range(n):
        copies[r].wait()
        at = rows_at(j ^ r, rows)
        dg_s[at, :] = dot(dy_s[at, :], w_down[...], NT)
        move.put(dg_s.at[at, :], dg_out.at[at, :])
    for copy in last:
        copy.wait()
    move.put(w_up, w_up_out)
    move.put(dy_s, dy_out)
    move.drain()


def ffn_kernel(n, place, *refs):
    hs = refs[:n]
    w_up_in, b_up_in, dg_in = refs[n : n + 3]
    h_out, g_out, du_out, keep, send, db_out = refs[n + 3 : n + 9]
    w_up, b_up, dg, h_s, g_s, du_s, keep_s, send_s, db, sems = refs[n + 9 :]
    move = Mover(sems)
    j = place.j
    rows = hs[0].shape[0]
    loads = [move.start(w_up_in, w_up), move.start(b_up_in, b_up)]
    copies = []
    for r in range(n):
        at = rows_at(j ^ r, rows)
        copies.append((move.start(hs[r], h_s.at[at, :]), move.start(dg_in.at[at, :], dg.at[at, :])))
    db[...] = jnp.zeros_like(db)
    for copy in loads:
        copy.wait()
    for r in range(n):
        for copy in copies[r]:
            copy.wait()
        at = rows_at(j ^ r, rows)
        u = dot(h_s[at, :], w_up[...]) + b_up[...]
        cdf = 0.5 * (1.0 + lax.erf(u * inv_root_two))
        g_s[at, :] = (u * cdf).astype(bf16)
        slope = cdf + u * jnp.exp(-0.5 * u * u) * inv_root_tau
        du = (dg[at, :] * slope).astype(bf16)
        du_s[at, :] = du
        db[...] += jnp.sum(du.astype(f32), axis=0, keepdims=True)
        dh = dot(du, w_up[...], NT)
        here = slice((r // 2) * rows, (r // 2 + 1) * rows)
        if r % 2 == 0:
            keep_s[here, :] = dh
            move.put(keep_s.at[here, :], keep.at[here, :])
        else:
            send_s[here, :] = dh.astype(bf16)
            move.put(send_s.at[here, :], send.at[here, :])
    move.put(h_s, h_out)
    move.put(g_s, g_out)
    move.put(du_s, du_out)
    move.put(db, db_out)
    move.drain()


def down_kernel(n, place, g_in, w_in, keep, send, g, w, keep_s, send_s, sems):
    move = Mover(sems)
    j = place.j
    rows = g.shape[0] // n
    load = move.start(w_in, w)
    copies = [move.start(g_in.at[rows_at(j ^ r, rows), :], g.at[rows_at(j ^ r, rows), :]) for r in range(n)]
    load.wait()
    for r in range(n):
        copies[r].wait()
        out = dot(g[rows_at(j ^ r, rows), :], w[...])
        here = slice((r // 2) * rows, (r // 2 + 1) * rows)
        if r % 2 == 0:
            keep_s[here, :] = out
            move.put(keep_s.at[here, :], keep.at[here, :])
        else:
            send_s[here, :] = out.astype(bf16)
            move.put(send_s.at[here, :], send.at[here, :])
    move.drain()


def ffn_grads_kernel(groups, place, h_in, du_in, dy_in, g_in, *refs):
    outs = refs[:groups]
    h, du, dy, g, grads, stage, sems = refs[groups:]
    move = Mover(sems)
    loads = [move.start(a, b) for a, b in ((h_in, h), (du_in, du), (dy_in, dy), (g_in, g))]
    feats = h.shape[1] // groups
    mine = du.shape[1]
    chunk = mine // groups
    loads[0].wait()
    loads[1].wait()
    for i in range(groups):
        grads[i, :feats, :] = dot(h[:, i * feats : (i + 1) * feats], du[...], TN)
    loads[2].wait()
    loads[3].wait()
    for c in range(dy.shape[1] // mine):
        part = dot(g[...], dy[:, c * mine : (c + 1) * mine], TN)
        for i in range(groups):
            grads[i, feats + c * chunk : feats + (c + 1) * chunk, :] = part[i * chunk : (i + 1) * chunk, :]
    for i in range(1, groups):
        stage[i - 1] = grads[place.group ^ i].astype(bf16)
        move.put(stage.at[i - 1], outs[i])
    move.put(grads.at[place.group], outs[0])
    move.drain()


def pair_kernel(place, keep, recv, *refs):
    count = (len(refs) - 3) // 2
    outs = refs[:count]
    keep_s, recv_s = refs[count : count + 2]
    stage, sems = refs[count + 2 : 2 * count + 2], refs[2 * count + 2]
    move = Mover(sems)
    rows = outs[0].shape[0]
    order = list(range(1, count)) + [0]
    loads = {}
    for i in order:
        here = slice(i * rows, (i + 1) * rows)
        loads[i] = (
            move.start(keep.at[here, :], keep_s.at[here, :]),
            move.start(recv.at[here, :], recv_s.at[here, :]),
        )
    for i in order:
        here = slice(i * rows, (i + 1) * rows)
        for copy in loads[i]:
            copy.wait()
        stage[i][...] = (keep_s[here, :] + recv_s[here, :].astype(f32)).astype(outs[i].dtype)
        move.put(stage[i], outs[i])
    move.drain()


def fold_kernel(count, place, *refs):
    ins, outs = refs[: 2 * count], refs[2 * count : 3 * count]
    held, stage, sems = refs[3 * count : 5 * count], refs[5 * count : 6 * count], refs[6 * count]
    move = Mover(sems)
    loads = [move.start(a, b) for a, b in zip(ins, held)]
    for i in range(count):
        loads[i].wait()
        loads[count + i].wait()
        stage[i][...] = (held[i][...].astype(f32) + held[count + i][...].astype(f32)).astype(bf16)
        move.put(stage[i], outs[i])
    move.drain()


def out_kernel(count, place, *refs):
    ins = refs[: count + 2]
    kept, sent = refs[count + 2 : count + 4]
    held = refs[count + 4 : 2 * count + 6]
    out_s, sems = refs[2 * count + 6 :]
    move = Mover(sems)
    for copy in [move.start(a, b) for a, b in zip(ins, held)]:
        copy.wait()
    total = held[0][...] + held[count][...]
    for i in range(1, count):
        total = total + held[i][...].astype(f32)
    out_s[...] = (total + held[count + 1][7:8, :]).astype(bf16)
    half = kept.shape[0]
    move.put(out_s.at[half:, :], sent)
    move.put(out_s.at[:half, :], kept)
    move.drain()


def mid_back_kernel(count, place, *refs):
    ins = refs[: count + 3]
    dy1_out, da_out, small_out = refs[count + 3 : count + 6]
    held = refs[count + 6 : 2 * count + 9]
    dy1_s, da_s, small, sems = refs[2 * count + 9 :]
    move = Mover(sems)
    for copy in [move.start(a, b) for a, b in zip(ins, held)]:
        copy.wait()
    dh = held[0][...]
    for i in range(1, count):
        dh = dh + held[i][...].astype(f32)
    y, vec, dy = held[count : count + 3]
    scaled, inv_std = normalize(y[...])
    dyf = dy[...].astype(f32)
    dy1 = dyf + norm_back(dh, scaled, inv_std, vec[5:6, :])
    da = dy1.astype(bf16)
    da_s[...] = da
    move.put(da_s, da_out)
    dy1_s[...] = dy1
    move.put(dy1_s, dy1_out)
    small[0:1, :] = jnp.sum(dh * scaled, axis=0, keepdims=True)
    small[1:2, :] = jnp.sum(dh, axis=0, keepdims=True)
    small[2:3, :] = jnp.sum(da.astype(f32), axis=0, keepdims=True)
    small[3:4, :] = jnp.sum(dyf, axis=0, keepdims=True)
    move.put(small, small_out)
    move.drain()


def attend_back_kernel(n, half, qb, place, *refs):
    das, ins = refs[:n], refs[n : n + 4]
    dqkv_out, keep, send, db_out = refs[n + 4 : n + 8]
    da, qkv, lse, wo, w, dqkv, keep_s, send_s, db, do, bias, acc_k, acc_v, sems = refs[n + 8 :]
    j = place.j
    rows = 2 * half
    move = Mover(sems)
    copies = [move.start(das[r], da.at[rows_at(j ^ r, rows), :]) for r in range(n)]
    loads = [move.start(a, b) for a, b in zip(ins, (wo, qkv, lse, w))]
    total = qkv.shape[0]
    hd = do.shape[1]
    heads = hd // HEAD
    bias[...] = jnp.where(key_mask(place, total, n, half, 128), 0.0, -1.0).astype(f32)
    for copy in loads:
        copy.wait()
    for r in range(n):
        copies[r].wait()
        at = rows_at(j ^ r, rows)
        do[at, :] = dot(da[at, :], wo[...], NT).astype(bf16)
    for head in range(heads):
        cols = slice(head * HEAD, (head + 1) * HEAD)
        kh = qkv[:, hd + head * HEAD : hd + (head + 1) * HEAD]
        vh = qkv[:, 2 * hd + head * HEAD : 2 * hd + (head + 1) * HEAD]
        kt = kh.astype(f32).T.astype(bf16)
        acc_k[...] = jnp.zeros_like(acc_k)
        acc_v[...] = jnp.zeros_like(acc_v)

        def step(i, _, cols=cols, kh=kh, vh=vh, kt=kt, head=head):
            at = rows_at(i, qb)
            qh = qkv[at, cols]
            doh = do[at, cols]
            scores = dot(kh, qh, NT)
            probs = jnp.where(bias[:, 0:1] >= 0.0, jnp.exp(scores - lse[pl.ds(head, 1), at]), 0.0)
            dp = dot(vh, doh, NT)
            centre = jnp.sum(probs * dp, axis=0, keepdims=True)
            ds = (probs * (dp - centre)).astype(bf16)
            acc_v[...] += dot(probs.astype(bf16), doh)
            acc_k[...] += dot(ds, qh)
            dq = dot(kt, ds)
            dqkv[at, cols] = (dq.T.astype(bf16).astype(f32) * 0.125).astype(bf16)
            return 0

        lax.fori_loop(0, total // qb, step, 0)
        dqkv[:, hd + head * HEAD : hd + (head + 1) * HEAD] = acc_k[...].astype(bf16)
        dqkv[:, 2 * hd + head * HEAD : 2 * hd + (head + 1) * HEAD] = acc_v[...].astype(bf16)
    move.put(dqkv, dqkv_out)
    db[...] = jnp.zeros_like(db)
    for r in list(range(1, n, 2)) + list(range(0, n, 2)):
        grads = dqkv[rows_at(j ^ r, rows), :]
        db[...] += jnp.sum(grads.astype(f32), axis=0, keepdims=True)
        dh = dot(grads, w[...], NT)
        here = slice((r // 2) * rows, (r // 2 + 1) * rows)
        if r % 2 == 0:
            keep_s[here, :] = dh
            move.put(keep_s.at[here, :], keep.at[here, :])
        else:
            send_s[here, :] = dh.astype(bf16)
            move.put(send_s.at[here, :], send.at[here, :])
    move.put(db, db_out)
    move.drain()


def attn_grads_kernel(n, groups, first_row, place, *refs):
    das, ins = refs[:n], refs[n : n + 8]
    outs = refs[n + 8 : n + 8 + groups]
    da, hat, h, dqkv, w, o, two, db, up, small, grads, packed_s, sems = refs[n + 8 + groups :]
    move = Mover(sems)
    j = place.j
    loads = [move.start(a, b) for a, b in zip(ins, (dqkv, h, w, hat, o, two, db, up))]
    rows = das[0].shape[0]
    copies = [move.start(das[r], da.at[rows_at(j ^ r, rows), :]) for r in range(n)]
    ndev = packed_s.shape[0]
    hd = dqkv.shape[1] // 3
    rs = h.shape[1] // ndev
    chunk = up.shape[1] // groups
    loads[0].wait()
    loads[1].wait()
    grads[...] = dot(h[...], dqkv[...], TN).astype(bf16)
    for copy in loads[2:]:
        copy.wait()
    small[...] = jnp.zeros_like(small)
    step_rows = 128

    def step(i, _):
        at = rows_at(i, step_rows)
        dh = dot(dqkv[at, :], w[...], NT)
        small[0:1, :] += jnp.sum(dh * hat[at, :].astype(f32), axis=0, keepdims=True)
        small[1:2, :] += jnp.sum(dh, axis=0, keepdims=True)
        return 0

    lax.fori_loop(0, hat.shape[0] // step_rows, step, 0)
    small[4:8, :] = two[...]
    for copy in copies:
        copy.wait()
    out_grad = dot(o[...], da[...], TN).astype(bf16)
    zeros = jnp.zeros((packed_s.shape[1] - rs, packed_s.shape[2]), bf16)
    for d in range(ndev):
        packed_s[d, rs:, :] = zeros
        packed_s[d, :rs, : 3 * hd] = grads[d * rs : (d + 1) * rs, :]
        packed_s[d, :rs, 3 * hd :] = out_grad[d // n * rs : (d // n + 1) * rs, d % n * hd : (d % n + 1) * hd]
        packed_s[d, first_row : first_row + 8, :rs] = small[:, d * rs : (d + 1) * rs].astype(bf16)
    for t in range(groups):
        cols = slice(t * rs, (t + 1) * rs)
        at = j * groups + t
        packed_s[at, first_row + 2 : first_row + 3, :rs] = db[:, :hd][:, cols].astype(bf16)
        packed_s[at, first_row + 3 : first_row + 4, :rs] = db[:, 2 * hd :][:, cols].astype(bf16)
        packed_s[t * n + j, first_row : first_row + 1, hd : hd + chunk] = up[
            :, t * chunk : (t + 1) * chunk
        ].astype(bf16)
    for i in list(range(2, groups)) + [1, 0]:
        move.put(packed_s.at[pl.ds((place.group ^ i) * n, n)], outs[i])
    move.drain()


def last_kernel(count, place, *refs):
    ins = refs[: count + 3]
    kept, sent = refs[count + 3 : count + 5]
    held = refs[count + 5 : 2 * count + 8]
    out_s, sems = refs[2 * count + 8 :]
    move = Mover(sems)
    for copy in [move.start(a, b) for a, b in zip(ins, held)]:
        copy.wait()
    x, dy1, vec = held[count:]
    dh = held[0][...]
    for i in range(1, count):
        dh = dh + held[i][...].astype(f32)
    scaled, inv_std = normalize(x[...].astype(f32))
    out_s[...] = (dy1[...] + norm_back(dh, scaled, inv_std, vec[0:1, :])).astype(bf16)
    half = kept.shape[0]
    move.put(out_s.at[half:, :], sent)
    move.put(out_s.at[:half, :], kept)
    move.drain()


def tail_sum_kernel(n, count, place, *refs):
    attns, ffns = refs[:count], refs[count : 2 * count]
    packed, down_out, out_w = refs[2 * count : 2 * count + 3]
    attn_s, ffn_s = refs[2 * count + 3 : 3 * count + 3], refs[3 * count + 3 : 4 * count + 3]
    packed_s, total, down_s, out_s, sems = refs[4 * count + 3 :]
    move = Mover(sems)
    loads = [move.start(a, b) for a, b in zip(attns + ffns, attn_s + ffn_s)]
    for copy in loads[:count]:
        copy.wait()
    attn = attn_s[0][...].astype(f32)
    for piece in attn_s[1:]:
        attn = attn + piece[...].astype(f32)
    attn = attn.astype(bf16)
    chunk, width = down_s.shape
    hd = width // n
    mine = total.shape[1]
    feats = total.shape[0] - width // mine * chunk
    rs = feats // n
    for m in range(n):
        out_s[:, m * hd : (m + 1) * hd] = attn[m, :rs, 3 * hd :]
    move.put(out_s, out_w)
    packed_s[:, :, : 3 * hd] = attn[:, :, : 3 * hd]
    packed_s[:, :, 3 * hd :] = jnp.zeros((n, packed_s.shape[1], mine), bf16)
    for copy in loads[count:]:
        copy.wait()
    ffn = ffn_s[0][...]
    for piece in ffn_s[1:]:
        ffn = ffn + piece[...].astype(f32)
    total[...] = ffn
    for m in range(n):
        packed_s[m, :rs, 3 * hd :] = total[m * rs : (m + 1) * rs, :].astype(bf16)
    move.put(packed_s, packed)
    for c in range(width // mine):
        down_s[:, c * mine : (c + 1) * mine] = total[feats + c * chunk : feats + (c + 1) * chunk, :]
    move.put(down_s, down_out)
    move.drain()


def unpack_kernel(n, groups, first_row, place, *refs):
    back, out_w = refs[:2]
    halves = refs[2:6]
    output, frames_grad, out_w_grad, up, wq, wk, wv = refs[6:13]
    vectors = refs[13:22]
    back_s, in_s, out_s, up_s, q_s, k_s, v_s = refs[22:29]
    vectors_s, sems = refs[29:38], refs[38]
    move = Mover(sems)
    for i, target in enumerate((output, frames_grad)):
        move.put(halves[2 * i], target.at[place.h])
        move.put(halves[2 * i + 1], target.at[1 - place.h])
    load, more = move.start(back, back_s), move.start(out_w, in_s)
    more.wait()
    out_s[...] = in_s[...].astype(f32)
    move.put(out_s, out_w_grad)
    load.wait()
    rs = wq.shape[0]
    hd = wq.shape[1] // n
    chunk = up.shape[1] // (n * groups)
    sums = jnp.zeros((8, 3 * hd), f32)
    for m in range(n):
        cols = slice(m * hd, (m + 1) * hd)
        for i, target in enumerate((q_s, k_s, v_s)):
            target[:, cols] = back_s[m, :rs, i * hd : (i + 1) * hd].astype(f32)
        for g in range(groups):
            at = (g * n + m) * chunk
            here = 3 * hd + g * chunk
            up_s[:, at : at + chunk] = back_s[m, :rs, here : here + chunk].astype(f32)
        sums = sums + back_s[m, first_row:, : 3 * hd].astype(f32)
    for a, b in ((q_s, wq), (k_s, wk), (v_s, wv), (up_s, up)):
        move.put(a, b)
    for i in range(8):
        vectors_s[i][...] = sums[i : i + 1, :rs]
    vectors_s[8][...] = sums[0:1, hd : hd + chunk]
    for a, b in zip(vectors_s, vectors):
        move.put(a, b)
    move.drain()


def on_device(
    dp_size,
    seq_size,
    frames,
    out_grad,
    order,
    lengths,
    first_gain,
    first_shift,
    query_weight,
    query_bias,
    key_weight,
    value_weight,
    value_bias,
    output_weight,
    output_bias,
    second_gain,
    second_shift,
    up_weight,
    up_bias,
    down_weight,
    down_bias,
):
    slots, half, width = frames.shape
    n = seq_size // slots
    groups = dp_size * slots
    ndev = dp_size * seq_size
    hd = width // n
    heads = hd // HEAD
    rs = query_weight.shape[0]
    hidden = up_weight.shape[1]
    chunk = hidden // ndev
    mine = hidden // n
    parts = width // mine
    feats = n * rs
    rows = 2 * half
    total = n * rows
    qb = min(256, total)
    count = n // 2
    both = ("dp", "seq")
    first_row = -(-rs // 8) * 8
    block_rows = first_row + 8

    grid = (slots, n)

    def xor(value, bit):
        return lax.ppermute(value, "seq", [(i, i ^ bit) for i in range(seq_size)])

    def gather_direct(value):
        got = [xor(value, r) for r in range(n - 2, 0, -2)]
        return [value] + got[::-1]

    def gather_pair(even):
        out = []
        for piece in even:
            out += [piece, xor(piece, 1)]
        return out

    def pair(keep, recv):
        outs = [sds((rows, width), f32)] + [sds((rows, width), bf16)] * (count - 1)
        return call(
        grid,
            pair_kernel,
            [keep, Near(recv)],
            near(outs),
            "pair",
            cost(1),
            scratch=[vmem(keep), vmem(recv)] + [vmem(o) for o in outs],
            sems=3 * count,
        )

    def scatter(pieces):
        return [pieces[0]] + [xor(pieces[i], 2 * i) for i in range(count - 1, 0, -1)][::-1]

    def to_group(value, i):
        pairs = []
        for d in range(ndev):
            dp_of, seq_of = d // seq_size, d % seq_size
            g_of = (dp_of * slots + seq_of // n) ^ i
            pairs.append((d, g_of // slots * seq_size + g_of % slots * n + seq_of % n))
        return lax.ppermute(value, both, pairs)

    def members(value):
        index = [[s * n + i for i in range(n)] for s in range(slots)]
        return lax.all_to_all(value, "seq", 0, 0, tiled=True, axis_index_groups=index)

    def fold(kept, got):
        outs = [sds(a.shape, bf16) for a in kept]
        return call(
            grid,
            functools.partial(fold_kernel, len(kept)),
            near(list(kept) + list(got)),
            near(outs),
            "fold",
            cost(2),
            scratch=[vmem(a) for a in list(kept) + list(got) + outs],
            sems=3 * len(kept),
        )

    def spread(pieces):
        bit = len(pieces)
        while bit < groups:
            pieces = pieces + [to_group(piece, bit) for piece in pieces]
            bit *= 2
        return pieces

    owners = [(d, (d % groups) // slots * seq_size + (d % groups) % slots * n + d // groups) for d in range(ndev)]
    out_w = lax.ppermute(output_weight, both, owners)

    small_in = [first_gain, first_shift, query_bias, value_bias, output_bias, second_gain, second_shift, down_bias]
    small_in = [v.reshape(1, -1) for v in small_in + [up_bias]]
    weights_in = [query_weight, key_weight, value_weight, up_weight]
    half_sds, row_sds = sds((half, width), bf16), sds((rows, width), bf16)
    packed_sds = sds((n, block_rows, 3 * hd + mine), bf16)
    x_own, x_send, dy_own, dy_send, packed = call(
        grid,
        functools.partial(pack_kernel, n, groups, first_row),
        [frames, out_grad] + weights_in + small_in,
        near([half_sds] * 4 + [packed_sds]),
        "pack",
        cost(2),
        scratch=[vmem(w) for w in weights_in] + [vmem(v) for v in small_in] + [vmem(packed_sds)],
        sems=18,
    )
    x_recv = xor(x_send, n)
    got = members(packed)
    x = jnp.concatenate([x_own, after(x_recv, got, out_w)])
    x_even = gather_direct(x)
    attn_sds = sds((n, block_rows, 4 * hd), bf16)
    ffn_sds = sds((feats + parts * chunk, mine), bf16)
    attn_w, ffn_w = call(
        grid,
        functools.partial(join_kernel, n),
        near([got, out_w]) + [down_weight],
        near([attn_sds, ffn_sds]),
        "join",
        cost(2),
        scratch=[vmem(packed_sds), pltpu.VMEM((rs, width), bf16), vmem(attn_sds)]
        + [pltpu.VMEM((feats, mine), bf16)],
        sems=4 + parts,
    )
    attn_ws = spread([attn_w, to_group(attn_w, 1)])
    dy = jnp.concatenate([dy_own, xor(after(dy_send, attn_w), n)])
    xs = gather_pair([x_even[0]] + [after(piece, dy, *attn_ws) for piece in x_even[1:]])

    ffn_w, dy_go, attn_last = lax.optimization_barrier((ffn_w, dy, tuple(attn_ws + xs)))
    ffn_ws = [ffn_w, to_group(ffn_w, 1), to_group(ffn_w, 2)]
    dy_even = gather_direct(dy_go)
    x_sds = sds((total, width), bf16)
    keep_sds, send_sds = sds((total // 2, width), f32), sds((total // 2, width), bf16)
    outs = [
        x_sds,
        x_sds,
        sds((total, 3 * hd), bf16),
        sds((total, hd), bf16),
        sds((heads, total), f32),
        sds((width, 3 * hd), bf16),
        sds((8, width), f32),
        sds((1, mine), f32),
        sds((hd, width), bf16),
        keep_sds,
        send_sds,
    ]
    s_hat, s_h, s_qkv, s_o, s_lse, s_w, s_vec, s_bias, s_wo, s_keep, s_send = [vmem(o) for o in outs]
    s_got = pltpu.VMEM((ndev, block_rows, 4 * hd), bf16)
    hat, h_first, qkv, o_heads, lse, w_qkv, vec, bias_up, wo, keep, send = call(
        grid,
        functools.partial(first_kernel, n, groups, half, qb, first_row),
        near(xs + attn_ws),
        outs[:-1] + near(outs[-1:]),
        "first",
        cost(17),
        scratch=[vmem(x_sds), s_hat, s_h, s_qkv, s_o, s_lse, s_got, s_w, s_vec, s_bias, s_wo, s_keep, s_send]
        + [pltpu.VMEM((total, 128), f32)],
        sems=2 * n + groups + 10,
        limit=32,
        lengths=(order, lengths),
    )
    send = after(send, *ffn_ws[1:], *dy_even[1:])

    y_sds = sds((rows, width), f32)
    y_pieces = pair(keep, xor(send, 1))
    ys = scatter(y_pieces)
    dys = gather_pair([dy_even[0]] + [after(piece, y_pieces[0]) for piece in dy_even[1:]])
    ffn_ws = spread(ffn_ws + [to_group(after(ffn_ws[1], y_pieces[0]), 2)])
    y1, h2 = call(
        grid,
        functools.partial(mid_kernel, count),
        near(ys + [x]) + [vec],
        [y_sds, Near(row_sds)],
        "mid",
        cost(2),
        scratch=[vmem(a) for a in ys + [row_sds, vec, y_sds, row_sds]],
        sems=count + 4,
    )
    h2_even = gather_direct(h2)

    outs = [x_sds, sds((total, mine), f32), sds((width, mine), bf16), sds((mine, width), bf16)]
    dy_all, dg, w_up, w_down = call(
        grid,
        functools.partial(down_back_kernel, n, groups),
        near(dys + ffn_ws),
        outs,
        "down_back",
        cost(5),
        scratch=[vmem(o) for o in outs],
        sems=2 * n + groups * (parts + 1) + 3,
    )
    h2s = gather_pair(h2_even[:1] + [after(piece, dg) for piece in h2_even[1:]])

    act_sds = sds((total, mine), bf16)
    outs = [x_sds, act_sds, act_sds, keep_sds, send_sds, sds((1, mine), f32)]
    h2_all, g, du, keep, send, d_bias_up = call(
        grid,
        functools.partial(ffn_kernel, n),
        near(h2s) + [w_up, bias_up, dg],
        outs[:4] + near(outs[4:5]) + outs[5:],
        "ffn",
        cost(9),
        scratch=[vmem(a) for a in [w_up, bias_up, dg] + outs],
        sems=3 * n + 6,
    )
    dh2 = scatter(pair(keep, xor(send, 1)))

    g_then = after(g, dh2[0])
    out_keep, out_send = call(
        grid,
        functools.partial(down_kernel, n),
        [g_then, w_down],
        [keep_sds, Near(send_sds)],
        "down",
        cost(4),
        scratch=[vmem(a) for a in (g, w_down, keep_sds, send_sds)],
        sems=2 * n + 1,
    )
    ffn_parts = call(
        grid,
        functools.partial(ffn_grads_kernel, groups),
        [h2_all, du, dy_all, g_then],
        [sds(ffn_sds.shape, f32)] + near([ffn_sds] * (groups - 1)),
        "ffn_grads",
        cost(5),
        scratch=[vmem(a) for a in (x_sds, act_sds, x_sds, act_sds)]
        + [pltpu.VMEM((groups,) + ffn_sds.shape, f32), pltpu.VMEM((groups - 1,) + ffn_sds.shape, bf16)],
        sems=4 + groups,
    )

    small_sds = sds((4, width), f32)
    outs = [y_sds, row_sds, small_sds]
    dy1, da, small_two = call(
        grid,
        functools.partial(mid_back_kernel, count),
        near(dh2) + [after(y1, ffn_parts[0], out_keep), vec, Near(dy)],
        outs[:1] + near(outs[1:2]) + outs[2:],
        "mid_back",
        cost(3),
        scratch=[vmem(a) for a in dh2 + [y1, vec, row_sds] + outs],
        sems=count + 6,
    )
    da_even = gather_direct(da)
    ffn_parts = [after(piece, da) for piece in ffn_parts]
    bit = groups // 2
    while bit > 2:
        ffn_parts = fold(ffn_parts[:bit], [to_group(piece, bit) for piece in ffn_parts[bit:]])
        bit //= 2
    ffn_got = [to_group(piece, 2) for piece in ffn_parts[2:4]]
    out_kept = pair(out_keep, xor(after(out_send, da), 1))
    das = gather_pair([da_even[0]] + [after(piece, out_kept[0]) for piece in da_even[1:]])

    out_kept, das = lax.optimization_barrier((tuple(out_kept), tuple(das)))
    out_kept, das = list(out_kept), list(das)
    out_pieces = scatter(out_kept)
    ins = [wo, qkv, lse, w_qkv]
    outs = [sds((total, 3 * hd), bf16), keep_sds, send_sds, sds((1, 3 * hd), f32)]
    d_qkv, keep, send, d_bias_qkv = call(
        grid,
        functools.partial(attend_back_kernel, n, half, qb),
        near(das) + ins,
        outs[:2] + near(outs[2:3]) + outs[3:],
        "attend_back",
        cost(15),
        scratch=[vmem(x_sds)]
        + [vmem(a) for a in (qkv, lse, wo, w_qkv)]
        + [vmem(a) for a in outs]
        + [
            pltpu.VMEM((total, hd), bf16),
            pltpu.VMEM((total, 128), f32),
            pltpu.VMEM((total, HEAD), f32),
            pltpu.VMEM((total, HEAD), f32),
        ],
        sems=2 * n + 6,
        limit=32,
        lengths=(order, lengths),
    )
    recv = xor(after(send, *out_pieces[1:], *ffn_got), 1)

    ins = [d_qkv, h_first, w_qkv, hat, o_heads, small_two, d_bias_qkv, d_bias_up]
    attn_parts = call(
        grid,
        functools.partial(attn_grads_kernel, n, groups, first_row),
        near(das) + ins,
        near([attn_sds] * groups),
        "attn_grads",
        cost(7),
        scratch=[vmem(a) for a in (x_sds, hat, h_first, d_qkv, w_qkv, o_heads, small_two, d_bias_qkv, d_bias_up)]
        + [
            pltpu.VMEM((8, width), f32),
            pltpu.VMEM((width, 3 * hd), bf16),
            pltpu.VMEM((ndev, block_rows, 4 * hd), bf16),
        ],
        sems=n + 8 + groups,
        limit=32,
    )
    dh1_pieces = pair(after(keep, attn_parts[0]), recv)
    dh1 = scatter(dh1_pieces)
    bit = groups // 2
    while bit > 2:
        attn_parts = fold(attn_parts[:bit], [to_group(piece, bit) for piece in attn_parts[bit:]])
        bit //= 2
    attn_got = [to_group(piece, 2) for piece in attn_parts[2:4]]

    (ffn_next,) = fold([after(ffn_parts[1], dh1_pieces[0])], ffn_got[1:])
    ffn_got = [ffn_got[0], to_group(ffn_next, 1)]
    ins = out_pieces + [y1, vec]
    out_own, out_sent = call(
        grid,
        functools.partial(out_kernel, count),
        near([after(ins[0], dh1_pieces[0])] + ins[1:count]) + ins[count:],
        near([half_sds] * 2),
        "out",
        cost(2),
        scratch=[vmem(a) for a in ins + [row_sds]],
        sems=len(ins) + 2,
    )
    out_other = xor(out_sent, n)
    (attn_next,) = fold([after(attn_parts[1], ffn_next, out_own)], attn_got[1:])
    attn_got = [attn_got[0], to_group(attn_next, 1)]

    ins = dh1 + [x, after(dy1, attn_next), vec]
    kept, sent = call(
        grid,
        functools.partial(last_kernel, count),
        near(ins[: count + 1]) + ins[count + 1 :],
        near([half_sds] * 2),
        "last",
        cost(2),
        scratch=[vmem(a) for a in ins + [row_sds]],
        sems=len(ins) + 2,
    )
    other = xor(sent, n)

    down_sds, out_w_sds = sds((chunk, width), f32), sds((rs, width), bf16)
    attn_sums, ffn_sums = [after(attn_parts[0], kept, out_other)] + attn_got, [ffn_parts[0]] + ffn_got
    back, down_weight_grad, out_w = call(
        grid,
        functools.partial(tail_sum_kernel, n, 3),
        near(attn_sums) + ffn_sums[:1] + near(ffn_sums[1:]),
        [Near(packed_sds), down_sds, Near(out_w_sds)],
        "tail_sum",
        cost(2),
        scratch=[vmem(a) for a in attn_sums + ffn_sums]
        + [vmem(packed_sds), pltpu.VMEM(ffn_sds.shape, f32), vmem(down_sds), vmem(out_w_sds)],
        sems=9,
    )
    back = members(back)
    out_w = lax.ppermute(out_w, both, [(b, a) for a, b in owners])
    frames_sds = sds(frames.shape, bf16)
    weight_sds = sds((rs, width), f32)
    outs = [weight_sds, sds((rs, hidden), f32)] + [weight_sds] * 3
    vectors = [sds((1, rs), f32)] * 8 + [sds((1, chunk), f32)]
    output, frames_grad, output_weight_grad, up_weight_grad, d_query, d_key, d_value, *vectors = call(
        grid,
        functools.partial(unpack_kernel, n, groups, first_row),
        near([back, out_w, out_own, out_other, kept, other]),
        [frames_sds] * 2 + outs + vectors,
        "unpack",
        cost(2),
        scratch=[vmem(a) for a in [back, out_w] + outs + vectors],
        sems=20,
    )
    vectors = [v.reshape(-1) for v in vectors]
    return (
        output,
        frames_grad,
        vectors[0],
        vectors[1],
        d_query,
        vectors[2],
        d_key,
        d_value,
        vectors[3],
        output_weight_grad,
        vectors[6],
        vectors[4],
        vectors[5],
        up_weight_grad,
        vectors[8],
        down_weight_grad,
        vectors[7],
    )


def solution(mesh):
    vector = P(("dp", "seq"))
    matrix = P(("dp", "seq"), None)
    rows = P("dp", "seq", None)
    return jax.shard_map(
        functools.partial(on_device, mesh.shape["dp"], mesh.shape["seq"]),
        mesh=mesh,
        in_specs=(
            rows,
            rows,
            P("dp"),
            P(),
            vector,
            vector,
            matrix,
            vector,
            matrix,
            matrix,
            vector,
            matrix,
            vector,
            vector,
            vector,
            matrix,
            vector,
            matrix,
            vector,
        ),
        out_specs=(
            rows,
            rows,
            vector,
            vector,
            matrix,
            vector,
            matrix,
            matrix,
            vector,
            matrix,
            vector,
            vector,
            vector,
            matrix,
            vector,
            matrix,
            vector,
        ),
        check_vma=False,
    )
```

time: 344 us -> 288 us (0.84)
  local copies, waits for them, and re-layouts: 65.2 us -> 0.06 us
  waiting for transfers between devices: 82.1 us -> 129 us
  starting transfers between devices: 103 us -> 64.2 us
  Pallas kernels: 58.3 us -> 91.9 us
  other arithmetic: 24.6 us -> 0 us
  matrix products: 4.33 us -> 0 us
    unnamed x175 -> x8, local copies, waits for them, and re-layouts: 39.5 us -> 0.04 us
    pallas_call x16 -> x21, Pallas kernels: 58.3 us -> 91.9 us  [call(): pl.pallas_call(body, out_shape=tuple((o.array if isinstance(o, Near) else...]
    ppermute x64 -> x48, waiting for transfers between devices: 81.7 us -> 106 us  [xor(): return lax.ppermute(value, 'seq', [(i, i ^ bit) for i in range(seq_size)])]
    ppermute x64 -> x48, starting transfers between devices: 56.7 us -> 37 us  [xor(): return lax.ppermute(value, 'seq', [(i, i ^ bit) for i in range(seq_size)])]
    all_to_all x4 -> x2, waiting for transfers between devices: 0.01 us -> 13.3 us  [members(): lax.all_to_all(value, 'seq', 0, 0, tiled=True, axis_index_groups=index)]
    all_to_all x2 -> x0, starting transfers between devices: 11.4 us -> none  [the longest x1 7.41 us: on_device(): got = lax.all_to_all(everyone, both, 0, 0, tiled=True)]
    select_n x8 -> x0, other arithmetic: 10.1 us -> none  [the longest x3 4.54 us: gather_groups(): jnp.where(low, jnp.concatenate([value, other]), jnp.concatenate([other, v...]
    ppermute x10 -> x14, waiting for transfers between devices: 0.03 us -> 9.9 us  [the longest x12 9.89 us: to_group(): return lax.ppermute(value, both, pairs)]
  transfers between devices with their start and end apart: 80 -> 64, of which waited for: 19 -> 32; matrix products, arithmetic and copies ran while one was open for 14% -> 0% of each run, Pallas kernels for 15% -> 24%
where the time goes in v2:
time: 288 us; the launch traced here: 287 us
  waiting for transfers between devices  129 us (45%)
  Pallas kernels  91.9 us (32%)
  starting transfers between devices  64.2 us (22%)
    ppermute x48, waiting for transfers between devices, xor(): return lax.ppermute(value, 'seq', [(i, i ^ bit) for i in range(seq_size)])  106 us
    pallas_call x21, Pallas kernels, call(): pl.pallas_call(body, out_shape=tuple((o.array if isinstance(o, Near) else...  91.9 us
    ppermute x48, starting transfers between devices, xor(): return lax.ppermute(value, 'seq', [(i, i ^ bit) for i in range(seq_size)])  37 us
    ppermute x12, starting transfers between devices, to_group(): return lax.ppermute(value, both, pairs)  17.1 us
    all_to_all x2, waiting for transfers between devices, members(): lax.all_to_all(value, 'seq', 0, 0, tiled=True, axis_index_groups=index)  13.3 us
    ppermute x12, waiting for transfers between devices, to_group(): return lax.ppermute(value, both, pairs)  9.89 us
    all_to_all x2, starting transfers between devices, members(): lax.all_to_all(value, 'seq', 0, 0, tiled=True, axis_index_groups=index)  8.82 us
  transfers between devices with their start and end apart: 64, of which 32 were waited for; matrix products, arithmetic and copies ran while one was open for 0% of the time, Pallas kernels for 24%

profile of v2, /device:TPU:0, one launch (start us, length us, event | category | flops | bytes accessed | tf_op | source)
XLA Modules:
  0.0 286.9 jit_solution(8179092912790399026)
XLA Ops:
  0.7 2.5 pack.1
  3.1 5.3 %all-to-all-start = ((bf16[8,40,896]{2,1,0:T(8,128)(2,1)}), bf16[8,40,896]{2,1,0:T(8,128)(2,1)S(1)}, u32[]{:S(2)}, u32[]{:S(2)}) async-start(bf16[8,40,896]{2,1,0:T(8,128)(2,1)} %get-tuple-element.149), calls=%async_computation | async-start | bytes 1146880 | tf_op jit(solution)/shard_map/all_to_all | solution.py:800
  9.1 9.4 %all-to-all-done.refs_0_ = bf16[8,40,896]{2,1,0:T(8,128)(2,1)S(1)} async-done(((bf16[8,40,896]{2,1,0:T(8,128)(2,1)}), bf16[8,40,896]{2,1,0:T(8,128)(2,1)S(1)}, u32[]{:S(2)}, u32[]{:S(2)}) %all-to-all-start) | async-done | bytes 573472 | tf_op jit(solution)/shard_map/all_to_all | solution.py:800
  18.5 1.2 join.1
  19.7 2.4 collective-permute-start.5
  22.7 2.4 collective-permute-start.4
  25.0 2.5 collective-permute-start.6
  27.5 17.5 %collective-permute-done = bf16[64,1024]{1,0:T(8,128)(2,1)S(1)} collective-permute-done((bf16[64,1024]{1,0:T(8,128)(2,1)S(1)}, bf16[64,1024]{1,0:T(8,128)(2,1)S(1)}, u32[]{:S(2)}, u32[]{:S(2)}) %collective-permute-start) | collective-permute-done | bytes 131104 | tf_op jit(solution)/shard_map/ppermute | solution.py:762
  45.0 3.4 %collective-permute-start.7 = (bf16[8,40,512]{2,1,0:T(8,128)(2,1)S(1)}, bf16[8,40,512]{2,1,0:T(8,128)(2,1)S(1)}, u32[]{:S(2)}, u32[]{:S(2)}) collective-permute-start(bf16[8,40,512]{2,1,0:T(8,128)(2,1)S(1)} %collective-permute-done.5.refs_11_), channel_id=1, source_target_pairs={{0,16},{1,17},{2,18},{3,19},{4,20},{5,21},{6,22},{7,23},{8,24},{9,... | collective-permute-start | bytes 983048 | tf_op jit(solution)/shard_map/ppermute | solution.py:796
  49.4 2.6 collective-permute-start.3
  52.0 6.6 %collective-permute-done.11.refs_8_ = bf16[128,1024]{1,0:T(8,128)(2,1)S(1)} collective-permute-done((bf16[128,1024]{1,0:T(8,128)(2,1)S(1)}, bf16[128,1024]{1,0:T(8,128)(2,1)S(1)}, u32[]{:S(2)}, u32[]{:S(2)}) %collective-permute-start.11) | collective-permute-done | bytes 262176 | tf_op jit(solution)/shard_map/ppermute | solution.py:762
  58.7 1.8 collective-permute-done.9.refs_6_
  60.5 2.6 collective-permute-done.3.refs_4_
  65.7 1.8 collective-permute-start.16
  67.4 1.4 collective-permute-start.15
  69.4 16.3 %first.1 = (bf16[1024,1024]{1,0:T(8,128)(2,1)}, bf16[1024,1024]{1,0:T(8,128)(2,1)}, bf16[1024,384]{1,0:T(8,128)(2,1)}, bf16[1024,128]{1,0:T(8,128)(2,1)}, f32[2,...) custom-call(s32[2]{0:T(128)S(1)} %copy-done, ...), custom_call_target="tpu_custom_call" | custom-call | flops 19549999104 | bytes 11579904 | tf_op jit(solution)/shard_map/first/pallas_call | solution.py:81
  85.7 2.2 collective-permute-done.16.refs_4_
  87.9 6.3 %collective-permute-done.13.refs_9_ = bf16[512,512]{1,0:T(8,128)(2,1)S(1)} collective-permute-done((bf16[512,512]{1,0:T(8,128)(2,1)S(1)}, bf16[512,512]{1,0:T(8,128)(2,1)S(1)}, u32[]{:S(2)}, u32[]{:S(2)}) %collective-permute-start.13) | collective-permute-done | bytes 524320 | tf_op jit(solution)/shard_map/ppermute | solution.py:796
  94.2 2.7 collective-permute-done.18.refs_1_
  96.8 1.7 pair.4
  99.6 2.6 collective-permute-start.21
  102.1 1.7 collective-permute-start.28
  103.8 3.2 %collective-permute-done.19.refs_1_ = bf16[128,1024]{1,0:T(8,128)(2,1)S(1)} collective-permute-done((bf16[128,1024]{1,0:T(8,128)(2,1)S(1)}, bf16[128,1024]{1,0:T(8,128)(2,1)S(1)}, u32[]{:S(2)}, u32[]{:S(2)}) %collective-permute-start.19) | collective-permute-done | bytes 262176 | tf_op jit(solution)/shard_map/ppermute | solution.py:762
  107.0 1.8 collective-permute-done.20.refs_2_
  108.8 5.0 %collective-permute-done.21.refs_3_ = bf16[128,1024]{1,0:T(8,128)(2,1)S(1)} collective-permute-done((bf16[128,1024]{1,0:T(8,128)(2,1)S(1)}, bf16[128,1024]{1,0:T(8,128)(2,1)S(1)}, u32[]{:S(2)}, u32[]{:S(2)}) %collective-permute-start.21) | collective-permute-done | bytes 262176 | tf_op jit(solution)/shard_map/ppermute | solution.py:762
  113.8 2.1 mid.1
  116.6 1.7 collective-permute-start.30
  118.4 1.1 collective-permute-start.23
  119.5 6.5 %down_back.1 = (bf16[1024,1024]{1,0:T(8,128)(2,1)}, f32[1024,512]{1,0:T(8,128)}, bf16[1024,512]{1,0:T(8,128)(2,1)}, bf16[512,1024]{1,0:T(8,128)(2,1)}) custom-call(bf16[128,1024]{1,0:T(8,128)(2,1)S(1)} %constant_dynamic-update-slice_fusion.2.refs_0_.refs_6_, bf16[128,1024]{1,0:T(8,128)(2,1)S(1)} %collective-permute-done.24.refs_1_, ...), custom_call_target="tpu_custom_call" | custom-call | flops 5750000128 | bytes 10485760 | tf_op jit(solution)/shard_map/down_back/pallas_call | solution.py:81
  126.0 4.7 %collective-permute-done.30.refs_4_ = bf16[128,1024]{1,0:T(8,128)(2,1)S(1)} collective-permute-done((bf16[128,1024]{1,0:T(8,128)(2,1)S(1)}, bf16[128,1024]{1,0:T(8,128)(2,1)S(1)}, u32[]{:S(2)}, u32[]{:S(2)}) %collective-permute-start.30) | collective-permute-done | bytes 262176 | tf_op jit(solution)/shard_map/ppermute | solution.py:762
  133.5 9.7 %ffn.1 = (bf16[1024,1024]{1,0:T(8,128)(2,1)}, bf16[1024,512]{1,0:T(8,128)(2,1)}, bf16[1024,512]{1,0:T(8,128)(2,1)}, f32[512,1024]{1,0:T(8,128)}, bf16[512,1024]{1,0:T(8,128)(2,1)S(1)}, /*index=5*/f32[1,512]{1,0:T(1,128)}) custom-call(bf16[128,1024]{1,0:T(8,128)(2,1)S(1)} %get-tuple-element.169.refs_0_, ...), custom_call_target="tpu_custom_call" | custom-call | flops 10350000128 | bytes 12587008 | tf_op jit(solution)/shard_map/ffn/pallas_call | solution.py:81
  143.3 2.5 collective-permute-done.34.refs_1_
  145.9 1.7 pair.5
  148.9 2.3 collective-permute-start.37
  151.2 5.8 %ffn_grads.1 = (f32[512,512]{1,0:T(8,128)}, bf16[512,512]{1,0:T(8,128)(2,1)S(1)}, bf16[512,512]{1,0:T(8,128)(2,1)S(1)}, bf16[512,512]{1,0:T(8,128)(2,1)S(1)}) custom-call(bf16[1024,1024]{1,0:T(8,128)(2,1)} %get-tuple-element.192.refs_0_, bf16[1024,512]{1,0:T(8,128)(2,1)} %get-tuple-element.193.refs_1_, bf16[1024,1024]{1,0:T(8,128)(2,1)} %get-tuple-element.194.refs_2_, ...), custom_call_target="tpu_custom_call" | custom-call | flops 5750000128 | bytes 8912896 | tf_op jit(solution)/shard_map/ffn_grads/pallas_call | solution.py:81
  157.0 4.4 %down.1 = (f32[512,1024]{1,0:T(8,128)}, bf16[512,1024]{1,0:T(8,128)(2,1)S(1)}) custom-call(bf16[1024,512]{1,0:T(8,128)(2,1)} %get-tuple-element.184.refs_0_.refs_3_, bf16[512,1024]{1,0:T(8,128)(2,1)} %get-tuple-element.185.refs_1_), custom_call_target="tpu_custom_call" | custom-call | flops 4600000000 | bytes 5242880 | tf_op jit(solution)/shard_map/down/pallas_call | solution.py:81
  161.5 1.3 collective-permute-done.37.refs_3_
  162.8 2.8 mid_back.1
  166.4 1.7 collective-permute-start.42
  168.2 1.1 collective-permute-start.40
  169.3 1.7 pair.6
  171.0 4.8 %collective-permute-done.44.refs_8_.refs_6_ = bf16[128,1024]{1,0:T(8,128)(2,1)S(1)} collective-permute-done((bf16[128,1024]{1,0:T(8,128)(2,1)S(1)}, bf16[128,1024]{1,0:T(8,128)(2,1)S(1)}, u32[]{:S(2)}, u32[]{:S(2)}) %collective-permute-start.44) | collective-permute-done | bytes 262176 | tf_op jit(solution)/shard_map/ppermute | solution.py:762
  175.8 4.7 %collective-permute-done.42.refs_6_.refs_4_ = bf16[128,1024]{1,0:T(8,128)(2,1)S(1)} collective-permute-done((bf16[128,1024]{1,0:T(8,128)(2,1)S(1)}, bf16[128,1024]{1,0:T(8,128)(2,1)S(1)}, u32[]{:S(2)}, u32[]{:S(2)}) %collective-permute-start.42) | collective-permute-done | bytes 262176 | tf_op jit(solution)/shard_map/ppermute | solution.py:762
  181.5 1.7 collective-permute-start.49
  184.8 2.3 collective-permute-start.48
  187.1 17.7 %attend_back.1 = (bf16[1024,384]{1,0:T(8,128)(2,1)}, f32[512,1024]{1,0:T(8,128)}, bf16[512,1024]{1,0:T(8,128)(2,1)S(1)}, f32[1,384]{1,0:T(1,128)}) custom-call(s32[2]{0:T(128)S(1)} %copy-done, s32[4]{0:T(128)S(1)} %copy-done.1, bf16[128,1024]{1,0:T(8,128)(2,1)S(1)} %get-tuple-element.206.refs_2_.refs_0_, ...), custom_call_target="tpu_custom_call" | custom-call | flops 17250000896 | bytes 7874048 | tf_op jit(solution)/shard_map/attend_back/pallas_call | solution.py:81
  204.8 2.3 collective-permute-done.50.refs_1_
  207.1 7.6 %attn_grads.1 = (bf16[8,40,512]{2,1,0:T(8,128)(2,1)S(1)}, bf16[8,40,512]{2,1,0:T(8,128)(2,1)S(1)}, bf16[8,40,512]{2,1,0:T(8,128)(2,1)S(1)}, bf16[8,40,512]{2,1,0:T(8,128)(2,1)S(1)}) custom-call(bf16[128,1024]{1,0:T(8,128)(2,1)S(1)} %get-tuple-element.206.refs_2_.refs_0_, bf16[128,1024]{1,0:T(8,128)(2,1)S(1)} %collective-permute-done.39.refs_3_.refs_1_, ...), custom_call_target="tpu_custom_call" | custom-call | flops 8049999872 | bytes 8148992 | tf_op jit(solution)/shard_map/attn_grads/pallas_call | solution.py:81
  214.7 1.8 collective-permute-start.55
  216.8 1.7 pair.7
  220.4 1.7 out.1
  222.1 1.9 collective-permute-start.53
  224.0 1.3 collective-permute-done.55.refs_1_
  226.8 1.7 collective-permute-start.58
  228.5 9.9 %collective-permute-done.53.refs_2_ = bf16[128,1024]{1,0:T(8,128)(2,1)S(1)} collective-permute-done((bf16[128,1024]{1,0:T(8,128)(2,1)S(1)}, bf16[128,1024]{1,0:T(8,128)(2,1)S(1)}, u32[]{:S(2)}, u32[]{:S(2)}) %collective-permute-start.53) | collective-permute-done | bytes 262176 | tf_op jit(solution)/shard_map/ppermute | solution.py:762
  238.4 3.1 %collective-permute-start.56 = (bf16[64,1024]{1,0:T(8,128)(2,1)S(1)}, bf16[64,1024]{1,0:T(8,128)(2,1)S(1)}, u32[]{:S(2)}, u32[]{:S(2)}) collective-permute-start(bf16[64,1024]{1,0:T(8,128)(2,1)S(1)} %get-tuple-element.253), channel_id=1, source_target_pairs={{0,8},{1,9},{2,10},{3,11},{4,12},{5,13},{6,14},{7,15},{8,0},{9,1},... | collective-permute-start | bytes 393224 | tf_op jit(solution)/shard_map/ppermute | solution.py:762
  241.6 5.4 %collective-permute-done.54.refs_3_ = bf16[128,1024]{1,0:T(8,128)(2,1)S(1)} collective-permute-done((bf16[128,1024]{1,0:T(8,128)(2,1)S(1)}, bf16[128,1024]{1,0:T(8,128)(2,1)S(1)}, u32[]{:S(2)}, u32[]{:S(2)}) %collective-permute-start.54) | collective-permute-done | bytes 262176 | tf_op jit(solution)/shard_map/ppermute | solution.py:762
  246.9 2.0 last.1
  249.0 16.0 %collective-permute-done.56.refs_3_ = bf16[64,1024]{1,0:T(8,128)(2,1)S(1)} collective-permute-done((bf16[64,1024]{1,0:T(8,128)(2,1)S(1)}, bf16[64,1024]{1,0:T(8,128)(2,1)S(1)}, u32[]{:S(2)}, u32[]{:S(2)}) %collective-permute-start.56) | collective-permute-done | bytes 131104 | tf_op jit(solution)/shard_map/ppermute | solution.py:762
  265.0 2.7 tail_sum.1
  267.6 3.5 %all-to-all-start.1 = ((bf16[8,40,896]{2,1,0:T(8,128)(2,1)}), bf16[8,40,896]{2,1,0:T(8,128)(2,1)S(1)}, u32[]{:S(2)}, u32[]{:S(2)}) async-start(bf16[8,40,896]{2,1,0:T(8,128)(2,1)} %get-tuple-element.257), calls=%async_computation.1 | async-start | bytes 1146880 | tf_op jit(solution)/shard_map/all_to_all | solution.py:800
  272.4 9.0 %collective-permute-done.61.refs_5_ = bf16[64,1024]{1,0:T(8,128)(2,1)S(1)} collective-permute-done((bf16[64,1024]{1,0:T(8,128)(2,1)S(1)}, bf16[64,1024]{1,0:T(8,128)(2,1)S(1)}, u32[]{:S(2)}, u32[]{:S(2)}) %collective-permute-start.61) | collective-permute-done | bytes 131104 | tf_op jit(solution)/shard_map/ppermute | solution.py:762
  281.4 3.9 %all-to-all-done.1.refs_0_ = bf16[8,40,896]{2,1,0:T(8,128)(2,1)S(1)} async-done(((bf16[8,40,896]{2,1,0:T(8,128)(2,1)}), bf16[8,40,896]{2,1,0:T(8,128)(2,1)S(1)}, u32[]{:S(2)}, u32[]{:S(2)}) %all-to-all-start.1) | async-done | bytes 573472 | tf_op jit(solution)/shard_map/all_to_all | solution.py:800
  285.3 1.4 unpack.1
  (95 shorter events, 19.8 us)
Async XLA Ops:
  3.1 15.3 %all-to-all-start = ((bf16[8,40,896]{2,1,0:T(8,128)(2,1)}), bf16[8,40,896]{2,1,0:T(8,128)(2,1)S(1)}, u32[]{:S(2)}, u32[]{:S(2)}) async-start(bf16[8,40,896]{2,1,0:T(8,128)(2,1)} %get-tuple-element.149), calls=%async_computation | async-start | bytes 1146880 | tf_op jit(solution)/shard_map/all_to_all | solution.py:800
  8.4 0.7 collective-permute-start.1
  19.7 25.3 %collective-permute-start.5 = (bf16[8,40,512]{2,1,0:T(8,128)(2,1)S(1)}, bf16[8,40,512]{2,1,0:T(8,128)(2,1)S(1)}, u32[]{:S(2)}, u32[]{:S(2)}) collective-permute-start(bf16[8,40,512]{2,1,0:T(8,128)(2,1)S(1)} %get-tuple-element.153.refs_10_), channel_id=1, source_target_pairs={{0,8},{1,9},{2,10},{3,11},{4,12},{5,13},{6,14},{7,15},{8,0},{9,1},... | collective-permute-start | bytes 983048 | tf_op jit(solution)/shard_map/ppermute | solution.py:796
  22.1 22.9 %collective-permute-start = (bf16[64,1024]{1,0:T(8,128)(2,1)S(1)}, bf16[64,1024]{1,0:T(8,128)(2,1)S(1)}, u32[]{:S(2)}, u32[]{:S(2)}) collective-permute-start(bf16[64,1024]{1,0:T(8,128)(2,1)S(1)} %get-tuple-element.148), channel_id=1, source_target_pairs={{0,8},{1,9},{2,10},{3,11},{4,12},{5,13},{6,14},{7,15},{8,0},{9,1},... | collective-permute-start | bytes 393224 | tf_op jit(solution)/shard_map/ppermute | solution.py:762
  22.7 26.7 %collective-permute-start.4 = (bf16[64,1024]{1,0:T(8,128)(2,1)S(1)}, bf16[64,1024]{1,0:T(8,128)(2,1)S(1)}, u32[]{:S(2)}, u32[]{:S(2)}) collective-permute-start(bf16[64,1024]{1,0:T(8,128)(2,1)S(1)} %get-tuple-element.154), channel_id=1, source_target_pairs={{0,8},{1,9},{2,10},{3,11},{4,12},{5,13},{6,14},{7,15},{8,0},{9,1},... | collective-permute-start | bytes 393224 | tf_op jit(solution)/shard_map/ppermute | solution.py:762
  25.0 33.6 %collective-permute-start.6 = (bf16[8,40,512]{2,1,0:T(8,128)(2,1)S(1)}, bf16[8,40,512]{2,1,0:T(8,128)(2,1)S(1)}, u32[]{:S(2)}, u32[]{:S(2)}) collective-permute-start(bf16[8,40,512]{2,1,0:T(8,128)(2,1)S(1)} %get-tuple-element.153.refs_10_), channel_id=1, source_target_pairs={{0,16},{1,17},{2,18},{3,19},{4,20},{5,21},{6,22},{7,23},{8,24},{9,... | collective-permute-start | bytes 983048 | tf_op jit(solution)/shard_map/ppermute | solution.py:796
  45.0 13.6 %collective-permute-start.7 = (bf16[8,40,512]{2,1,0:T(8,128)(2,1)S(1)}, bf16[8,40,512]{2,1,0:T(8,128)(2,1)S(1)}, u32[]{:S(2)}, u32[]{:S(2)}) collective-permute-start(bf16[8,40,512]{2,1,0:T(8,128)(2,1)S(1)} %collective-permute-done.5.refs_11_), channel_id=1, source_target_pairs={{0,16},{1,17},{2,18},{3,19},{4,20},{5,21},{6,22},{7,23},{8,24},{9,... | collective-permute-start | bytes 983048 | tf_op jit(solution)/shard_map/ppermute | solution.py:796
  48.5 10.2 %collective-permute-start.11 = (bf16[128,1024]{1,0:T(8,128)(2,1)S(1)}, bf16[128,1024]{1,0:T(8,128)(2,1)S(1)}, u32[]{:S(2)}, u32[]{:S(2)}) collective-permute-start(bf16[128,1024]{1,0:T(8,128)(2,1)S(1)} %constant_dynamic-update-slice_fusion.refs_2_.refs_4_), channel_id=1, source_target_pairs={{0,6},{1,7},{2,4},{3,5},{4,2},{5,3},{6,0},{7,1},{8,14},{9,15},{10,... | collective-permute-start | bytes 786440 | tf_op jit(solution)/shard_map/ppermute | solution.py:762
  49.2 11.2 %collective-permute-start.9 = (bf16[128,1024]{1,0:T(8,128)(2,1)S(1)}, bf16[128,1024]{1,0:T(8,128)(2,1)S(1)}, u32[]{:S(2)}, u32[]{:S(2)}) collective-permute-start(bf16[128,1024]{1,0:T(8,128)(2,1)S(1)} %constant_dynamic-update-slice_fusion.refs_2_.refs_4_), channel_id=1, source_target_pairs={{0,4},{1,5},{2,6},{3,7},{4,0},{5,1},{6,2},{7,3},{8,12},{9,13},{10,... | collective-permute-start | bytes 786440 | tf_op jit(solution)/shard_map/ppermute | solution.py:762
  49.4 13.6 %collective-permute-start.3 = (bf16[128,1024]{1,0:T(8,128)(2,1)S(1)}, bf16[128,1024]{1,0:T(8,128)(2,1)S(1)}, u32[]{:S(2)}, u32[]{:S(2)}) collective-permute-start(bf16[128,1024]{1,0:T(8,128)(2,1)S(1)} %constant_dynamic-update-slice_fusion.refs_2_.refs_4_), channel_id=1, source_target_pairs={{0,2},{1,3},{2,0},{3,1},{4,6},{5,7},{6,4},{7,5},{8,10},{9,11},{10,... | collective-permute-start | bytes 786440 | tf_op jit(solution)/shard_map/ppermute | solution.py:762
  58.7 5.0 %collective-permute-start.2 = (bf16[128,1024]{1,0:T(8,128)(2,1)S(1)}, bf16[128,1024]{1,0:T(8,128)(2,1)S(1)}, u32[]{:S(2)}, u32[]{:S(2)}) collective-permute-start(bf16[128,1024]{1,0:T(8,128)(2,1)S(1)} %constant_dynamic-update-slice_fusion.refs_2_.refs_4_), channel_id=1, source_target_pairs={{0,1},{1,0},{2,3},{3,2},{4,5},{5,4},{6,7},{7,6},{8,9},{9,8},{10,11... | collective-permute-start | bytes 786440 | tf_op jit(solution)/shard_map/ppermute | solution.py:762
  63.0 1.5 collective-permute-start.8
  63.2 1.8 collective-permute-start.10
  63.5 1.8 collective-permute-start.12
  65.3 20.4 %collective-permute-start.17 = (bf16[128,1024]{1,0:T(8,128)(2,1)S(1)}, bf16[128,1024]{1,0:T(8,128)(2,1)S(1)}, u32[]{:S(2)}, u32[]{:S(2)}) collective-permute-start(bf16[128,1024]{1,0:T(8,128)(2,1)S(1)} %constant_dynamic-update-slice_fusion.2.refs_0_.refs_6_), channel_id=1, source_target_pairs={{0,6},{1,7},{2,4},{3,5},{4,2},{5,3},{6,0},{7,1},{8,14},{9,15},{10,... | collective-permute-start | bytes 786440 | tf_op jit(solution)/shard_map/ppermute | solution.py:762
  65.7 22.2 %collective-permute-start.16 = (bf16[128,1024]{1,0:T(8,128)(2,1)S(1)}, bf16[128,1024]{1,0:T(8,128)(2,1)S(1)}, u32[]{:S(2)}, u32[]{:S(2)}) collective-permute-start(bf16[128,1024]{1,0:T(8,128)(2,1)S(1)} %constant_dynamic-update-slice_fusion.2.refs_0_.refs_6_), channel_id=1, source_target_pairs={{0,4},{1,5},{2,6},{3,7},{4,0},{5,1},{6,2},{7,3},{8,12},{9,13},{10,... | collective-permute-start | bytes 786440 | tf_op jit(solution)/shard_map/ppermute | solution.py:762
  67.4 20.4 %collective-permute-start.15 = (bf16[128,1024]{1,0:T(8,128)(2,1)S(1)}, bf16[128,1024]{1,0:T(8,128)(2,1)S(1)}, u32[]{:S(2)}, u32[]{:S(2)}) collective-permute-start(bf16[128,1024]{1,0:T(8,128)(2,1)S(1)} %constant_dynamic-update-slice_fusion.2.refs_0_.refs_6_), channel_id=1, source_target_pairs={{0,2},{1,3},{2,0},{3,1},{4,6},{5,7},{6,4},{7,5},{8,10},{9,11},{10,... | collective-permute-start | bytes 786440 | tf_op jit(solution)/shard_map/ppermute | solution.py:762
  68.8 19.1 %collective-permute-start.14 = (bf16[512,512]{1,0:T(8,128)(2,1)S(1)}, bf16[512,512]{1,0:T(8,128)(2,1)S(1)}, u32[]{:S(2)}, u32[]{:S(2)}) collective-permute-start(bf16[512,512]{1,0:T(8,128)(2,1)S(1)} %get-tuple-element.161.refs_8_), channel_id=1, source_target_pairs={{0,16},{1,17},{2,18},{3,19},{4,20},{5,21},{6,22},{7,23},{8,24},{9,... | collective-permute-start | bytes 1572872 | tf_op jit(solution)/shard_map/ppermute | solution.py:796
  69.1 25.0 %collective-permute-start.13 = (bf16[512,512]{1,0:T(8,128)(2,1)S(1)}, bf16[512,512]{1,0:T(8,128)(2,1)S(1)}, u32[]{:S(2)}, u32[]{:S(2)}) collective-permute-start(bf16[512,512]{1,0:T(8,128)(2,1)S(1)} %get-tuple-element.161.refs_8_), channel_id=1, source_target_pairs={{0,8},{1,9},{2,10},{3,11},{4,12},{5,13},{6,14},{7,15},{8,0},{9,1},... | collective-permute-start | bytes 1572872 | tf_op jit(solution)/shard_map/ppermute | solution.py:796
  94.2 2.7 collective-permute-start.18
  98.6 8.4 %collective-permute-start.19 = (bf16[128,1024]{1,0:T(8,128)(2,1)S(1)}, bf16[128,1024]{1,0:T(8,128)(2,1)S(1)}, u32[]{:S(2)}, u32[]{:S(2)}) collective-permute-start(bf16[128,1024]{1,0:T(8,128)(2,1)S(1)} %get-tuple-element.165), channel_id=1, source_target_pairs={{0,2},{1,3},{2,0},{3,1},{4,6},{5,7},{6,4},{7,5},{8,10},{9,11},{10,... | collective-permute-start | bytes 786440 | tf_op jit(solution)/shard_map/ppermute | solution.py:762
  99.6 9.2 %collective-permute-start.20 = (bf16[128,1024]{1,0:T(8,128)(2,1)S(1)}, bf16[128,1024]{1,0:T(8,128)(2,1)S(1)}, u32[]{:S(2)}, u32[]{:S(2)}) collective-permute-start(bf16[128,1024]{1,0:T(8,128)(2,1)S(1)} %get-tuple-element.166), channel_id=1, source_target_pairs={{0,4},{1,5},{2,6},{3,7},{4,0},{5,1},{6,2},{7,3},{8,12},{9,13},{10,... | collective-permute-start | bytes 786440 | tf_op jit(solution)/shard_map/ppermute | solution.py:762
  99.6 14.2 %collective-permute-start.21 = (bf16[128,1024]{1,0:T(8,128)(2,1)S(1)}, bf16[128,1024]{1,0:T(8,128)(2,1)S(1)}, u32[]{:S(2)}, u32[]{:S(2)}) collective-permute-start(bf16[128,1024]{1,0:T(8,128)(2,1)S(1)} %get-tuple-element.167), channel_id=1, source_target_pairs={{0,6},{1,7},{2,4},{3,5},{4,2},{5,3},{6,0},{7,1},{8,14},{9,15},{10,... | collective-permute-start | bytes 786440 | tf_op jit(solution)/shard_map/ppermute | solution.py:762
  102.1 17.3 %collective-permute-start.28 = (bf16[512,512]{1,0:T(8,128)(2,1)S(1)}, bf16[512,512]{1,0:T(8,128)(2,1)S(1)}, u32[]{:S(2)}, u32[]{:S(2)}) collective-permute-start(bf16[512,512]{1,0:T(8,128)(2,1)S(1)} %collective-permute-done.13.refs_9_), channel_id=1, source_target_pairs={{0,16},{1,17},{2,18},{3,19},{4,20},{5,21},{6,22},{7,23},{8,24},{9,... | collective-permute-start | bytes 1572872 | tf_op jit(solution)/shard_map/ppermute | solution.py:796
  103.8 12.1 %collective-permute-start.24 = (bf16[128,1024]{1,0:T(8,128)(2,1)S(1)}, bf16[128,1024]{1,0:T(8,128)(2,1)S(1)}, u32[]{:S(2)}, u32[]{:S(2)}) collective-permute-start(bf16[128,1024]{1,0:T(8,128)(2,1)S(1)} %constant_dynamic-update-slice_fusion.2.refs_0_.refs_6_), channel_id=1, source_target_pairs={{0,1},{1,0},{2,3},{3,2},{4,5},{5,4},{6,7},{7,6},{8,9},{9,8},{10,11... | collective-permute-start | bytes 786440 | tf_op jit(solution)/shard_map/ppermute | solution.py:762
  107.0 9.6 %collective-permute-start.25 = (bf16[128,1024]{1,0:T(8,128)(2,1)S(1)}, bf16[128,1024]{1,0:T(8,128)(2,1)S(1)}, u32[]{:S(2)}, u32[]{:S(2)}) collective-permute-start(bf16[128,1024]{1,0:T(8,128)(2,1)S(1)} %collective-permute-done.15.refs_2_), channel_id=1, source_target_pairs={{0,1},{1,0},{2,3},{3,2},{4,5},{5,4},{6,7},{7,6},{8,9},{9,8},{10,11... | collective-permute-start | bytes 786440 | tf_op jit(solution)/shard_map/ppermute | solution.py:762
  108.8 9.6 %collective-permute-start.26 = (bf16[128,1024]{1,0:T(8,128)(2,1)S(1)}, bf16[128,1024]{1,0:T(8,128)(2,1)S(1)}, u32[]{:S(2)}, u32[]{:S(2)}) collective-permute-start(bf16[128,1024]{1,0:T(8,128)(2,1)S(1)} %collective-permute-done.16.refs_4_), channel_id=1, source_target_pairs={{0,1},{1,0},{2,3},{3,2},{4,5},{5,4},{6,7},{7,6},{8,9},{9,8},{10,11... | collective-permute-start | bytes 786440 | tf_op jit(solution)/shard_map/ppermute | solution.py:762
  113.8 5.7 %collective-permute-start.27 = (bf16[128,1024]{1,0:T(8,128)(2,1)S(1)}, bf16[128,1024]{1,0:T(8,128)(2,1)S(1)}, u32[]{:S(2)}, u32[]{:S(2)}) collective-permute-start(bf16[128,1024]{1,0:T(8,128)(2,1)S(1)} %collective-permute-done.17.refs_6_), channel_id=1, source_target_pairs={{0,1},{1,0},{2,3},{3,2},{4,5},{5,4},{6,7},{7,6},{8,9},{9,8},{10,11... | collective-permute-start | bytes 786440 | tf_op jit(solution)/shard_map/ppermute | solution.py:762
  115.9 10.1 %collective-permute-start.32 = (bf16[128,1024]{1,0:T(8,128)(2,1)S(1)}, bf16[128,1024]{1,0:T(8,128)(2,1)S(1)}, u32[]{:S(2)}, u32[]{:S(2)}) collective-permute-start(bf16[128,1024]{1,0:T(8,128)(2,1)S(1)} %get-tuple-element.169.refs_0_), channel_id=1, source_target_pairs={{0,6},{1,7},{2,4},{3,5},{4,2},{5,3},{6,0},{7,1},{8,14},{9,15},{10,... | collective-permute-start | bytes 786440 | tf_op jit(solution)/shard_map/ppermute | solution.py:762
  116.6 14.1 %collective-permute-start.30 = (bf16[128,1024]{1,0:T(8,128)(2,1)S(1)}, bf16[128,1024]{1,0:T(8,128)(2,1)S(1)}, u32[]{:S(2)}, u32[]{:S(2)}) collective-permute-start(bf16[128,1024]{1,0:T(8,128)(2,1)S(1)} %get-tuple-element.169.refs_0_), channel_id=1, source_target_pairs={{0,4},{1,5},{2,6},{3,7},{4,0},{5,1},{6,2},{7,3},{8,12},{9,13},{10,... | collective-permute-start | bytes 786440 | tf_op jit(solution)/shard_map/ppermute | solution.py:762
  118.4 12.8 %collective-permute-start.23 = (bf16[128,1024]{1,0:T(8,128)(2,1)S(1)}, bf16[128,1024]{1,0:T(8,128)(2,1)S(1)}, u32[]{:S(2)}, u32[]{:S(2)}) collective-permute-start(bf16[128,1024]{1,0:T(8,128)(2,1)S(1)} %get-tuple-element.169.refs_0_), channel_id=1, source_target_pairs={{0,2},{1,3},{2,0},{3,1},{4,6},{5,7},{6,4},{7,5},{8,10},{9,11},{10,... | collective-permute-start | bytes 786440 | tf_op jit(solution)/shard_map/ppermute | solution.py:762
  119.5 12.3 %collective-permute-start.22 = (bf16[128,1024]{1,0:T(8,128)(2,1)S(1)}, bf16[128,1024]{1,0:T(8,128)(2,1)S(1)}, u32[]{:S(2)}, u32[]{:S(2)}) collective-permute-start(bf16[128,1024]{1,0:T(8,128)(2,1)S(1)} %get-tuple-element.169.refs_0_), channel_id=1, source_target_pairs={{0,1},{1,0},{2,3},{3,2},{4,5},{5,4},{6,7},{7,6},{8,9},{9,8},{10,11... | collective-permute-start | bytes 786440 | tf_op jit(solution)/shard_map/ppermute | solution.py:762
  131.2 1.5 collective-permute-start.29
  131.2 1.9 collective-permute-start.31
  131.7 1.8 collective-permute-start.33
  143.1 2.7 collective-permute-start.34
  147.6 13.9 %collective-permute-start.35 = (bf16[128,1024]{1,0:T(8,128)(2,1)S(1)}, bf16[128,1024]{1,0:T(8,128)(2,1)S(1)}, u32[]{:S(2)}, u32[]{:S(2)}) collective-permute-start(bf16[128,1024]{1,0:T(8,128)(2,1)S(1)} %get-tuple-element.188), channel_id=1, source_target_pairs={{0,2},{1,3},{2,0},{3,1},{4,6},{5,7},{6,4},{7,5},{8,10},{9,11},{10,... | collective-permute-start | bytes 786440 | tf_op jit(solution)/shard_map/ppermute | solution.py:762
  148.6 12.9 %collective-permute-start.36 = (bf16[128,1024]{1,0:T(8,128)(2,1)S(1)}, bf16[128,1024]{1,0:T(8,128)(2,1)S(1)}, u32[]{:S(2)}, u32[]{:S(2)}) collective-permute-start(bf16[128,1024]{1,0:T(8,128)(2,1)S(1)} %get-tuple-element.189), channel_id=1, source_target_pairs={{0,4},{1,5},{2,6},{3,7},{4,0},{5,1},{6,2},{7,3},{8,12},{9,13},{10,... | collective-permute-start | bytes 786440 | tf_op jit(solution)/shard_map/ppermute | solution.py:762
  148.9 14.0 %collective-permute-start.37 = (bf16[128,1024]{1,0:T(8,128)(2,1)S(1)}, bf16[128,1024]{1,0:T(8,128)(2,1)S(1)}, u32[]{:S(2)}, u32[]{:S(2)}) collective-permute-start(bf16[128,1024]{1,0:T(8,128)(2,1)S(1)} %get-tuple-element.190), channel_id=1, source_target_pairs={{0,6},{1,7},{2,4},{3,5},{4,2},{5,3},{6,0},{7,1},{8,14},{9,15},{10,... | collective-permute-start | bytes 786440 | tf_op jit(solution)/shard_map/ppermute | solution.py:762
  165.6 3.6 %collective-permute-start.38 = (bf16[512,1024]{1,0:T(8,128)(2,1)S(1)}, bf16[512,1024]{1,0:T(8,128)(2,1)S(1)}, u32[]{:S(2)}, u32[]{:S(2)}) collective-permute-start(bf16[512,1024]{1,0:T(8,128)(2,1)S(1)} %get-tuple-element.198), channel_id=1, source_target_pairs={{0,1},{1,0},{2,3},{3,2},{4,5},{5,4},{6,7},{7,6},{8,9},{9,8},{10,11... | collective-permute-start | bytes 3145736 | tf_op jit(solution)/shard_map/ppermute | solution.py:762
  165.7 10.1 %collective-permute-start.44 = (bf16[128,1024]{1,0:T(8,128)(2,1)S(1)}, bf16[128,1024]{1,0:T(8,128)(2,1)S(1)}, u32[]{:S(2)}, u32[]{:S(2)}) collective-permute-start(bf16[128,1024]{1,0:T(8,128)(2,1)S(1)} %get-tuple-element.206.refs_2_.refs_0_), channel_id=1, source_target_pairs={{0,6},{1,7},{2,4},{3,5},{4,2},{5,3},{6,0},{7,1},{8,14},{9,15},{10,... | collective-permute-start | bytes 786440 | tf_op jit(solution)/shard_map/ppermute | solution.py:762
  166.4 14.0 %collective-permute-start.42 = (bf16[128,1024]{1,0:T(8,128)(2,1)S(1)}, bf16[128,1024]{1,0:T(8,128)(2,1)S(1)}, u32[]{:S(2)}, u32[]{:S(2)}) collective-permute-start(bf16[128,1024]{1,0:T(8,128)(2,1)S(1)} %get-tuple-element.206.refs_2_.refs_0_), channel_id=1, source_target_pairs={{0,4},{1,5},{2,6},{3,7},{4,0},{5,1},{6,2},{7,3},{8,12},{9,13},{10,... | collective-permute-start | bytes 786440 | tf_op jit(solution)/shard_map/ppermute | solution.py:762
  168.2 12.8 %collective-permute-start.40 = (bf16[128,1024]{1,0:T(8,128)(2,1)S(1)}, bf16[128,1024]{1,0:T(8,128)(2,1)S(1)}, u32[]{:S(2)}, u32[]{:S(2)}) collective-permute-start(bf16[128,1024]{1,0:T(8,128)(2,1)S(1)} %get-tuple-element.206.refs_2_.refs_0_), channel_id=1, source_target_pairs={{0,2},{1,3},{2,0},{3,1},{4,6},{5,7},{6,4},{7,5},{8,10},{9,11},{10,... | collective-permute-start | bytes 786440 | tf_op jit(solution)/shard_map/ppermute | solution.py:762
  169.3 13.9 %collective-permute-start.39 = (bf16[128,1024]{1,0:T(8,128)(2,1)S(1)}, bf16[128,1024]{1,0:T(8,128)(2,1)S(1)}, u32[]{:S(2)}, u32[]{:S(2)}) collective-permute-start(bf16[128,1024]{1,0:T(8,128)(2,1)S(1)} %get-tuple-element.206.refs_2_.refs_0_), channel_id=1, source_target_pairs={{0,1},{1,0},{2,3},{3,2},{4,5},{5,4},{6,7},{7,6},{8,9},{9,8},{10,11... | collective-permute-start | bytes 786440 | tf_op jit(solution)/shard_map/ppermute | solution.py:762
  180.9 2.6 collective-permute-start.41
  181.0 2.5 collective-permute-start.43
  181.5 2.1 collective-permute-start.45
  181.5 23.3 %collective-permute-start.49 = (bf16[512,512]{1,0:T(8,128)(2,1)S(1)}, bf16[512,512]{1,0:T(8,128)(2,1)S(1)}, u32[]{:S(2)}, u32[]{:S(2)}) collective-permute-start(bf16[512,512]{1,0:T(8,128)(2,1)S(1)} %get-tuple-element.233), channel_id=1, source_target_pairs={{0,16},{1,17},{2,18},{3,19},{4,20},{5,21},{6,22},{7,23},{8,24},{9,... | collective-permute-start | bytes 1572872 | tf_op jit(solution)/shard_map/ppermute | solution.py:796
  183.2 23.9 %collective-permute-start.50 = (bf16[512,512]{1,0:T(8,128)(2,1)S(1)}, bf16[512,512]{1,0:T(8,128)(2,1)S(1)}, u32[]{:S(2)}, u32[]{:S(2)}) collective-permute-start(bf16[512,512]{1,0:T(8,128)(2,1)S(1)} %get-tuple-element.235), channel_id=1, source_target_pairs={{0,16},{1,17},{2,18},{3,19},{4,20},{5,21},{6,22},{7,23},{8,24},{9,... | collective-permute-start | bytes 1572872 | tf_op jit(solution)/shard_map/ppermute | solution.py:796
  183.5 23.5 %collective-permute-start.46 = (bf16[128,1024]{1,0:T(8,128)(2,1)S(1)}, bf16[128,1024]{1,0:T(8,128)(2,1)S(1)}, u32[]{:S(2)}, u32[]{:S(2)}) collective-permute-start(bf16[128,1024]{1,0:T(8,128)(2,1)S(1)} %get-tuple-element.229), channel_id=1, source_target_pairs={{0,2},{1,3},{2,0},{3,1},{4,6},{5,7},{6,4},{7,5},{8,10},{9,11},{10,... | collective-permute-start | bytes 786440 | tf_op jit(solution)/shard_map/ppermute | solution.py:762
  184.5 22.5 %collective-permute-start.47 = (bf16[128,1024]{1,0:T(8,128)(2,1)S(1)}, bf16[128,1024]{1,0:T(8,128)(2,1)S(1)}, u32[]{:S(2)}, u32[]{:S(2)}) collective-permute-start(bf16[128,1024]{1,0:T(8,128)(2,1)S(1)} %get-tuple-element.230), channel_id=1, source_target_pairs={{0,4},{1,5},{2,6},{3,7},{4,0},{5,1},{6,2},{7,3},{8,12},{9,13},{10,... | collective-permute-start | bytes 786440 | tf_op jit(solution)/shard_map/ppermute | solution.py:762
  184.8 22.2 %collective-permute-start.48 = (bf16[128,1024]{1,0:T(8,128)(2,1)S(1)}, bf16[128,1024]{1,0:T(8,128)(2,1)S(1)}, u32[]{:S(2)}, u32[]{:S(2)}) collective-permute-start(bf16[128,1024]{1,0:T(8,128)(2,1)S(1)} %get-tuple-element.231), channel_id=1, source_target_pairs={{0,6},{1,7},{2,4},{3,5},{4,2},{5,3},{6,0},{7,1},{8,14},{9,15},{10,... | collective-permute-start | bytes 786440 | tf_op jit(solution)/shard_map/ppermute | solution.py:762
  207.0 9.8 %collective-permute-start.51 = (bf16[512,1024]{1,0:T(8,128)(2,1)S(1)}, bf16[512,1024]{1,0:T(8,128)(2,1)S(1)}, u32[]{:S(2)}, u32[]{:S(2)}) collective-permute-start(bf16[512,1024]{1,0:T(8,128)(2,1)S(1)} %get-tuple-element.236), channel_id=1, source_target_pairs={{0,1},{1,0},{2,3},{3,2},{4,5},{5,4},{6,7},{7,6},{8,9},{9,8},{10,11... | collective-permute-start | bytes 3145736 | tf_op jit(solution)/shard_map/ppermute | solution.py:762
  214.7 10.6 %collective-permute-start.55 = (bf16[8,40,512]{2,1,0:T(8,128)(2,1)S(1)}, bf16[8,40,512]{2,1,0:T(8,128)(2,1)S(1)}, u32[]{:S(2)}, u32[]{:S(2)}) collective-permute-start(bf16[8,40,512]{2,1,0:T(8,128)(2,1)S(1)} %get-tuple-element.250), channel_id=1, source_target_pairs={{0,16},{1,17},{2,18},{3,19},{4,20},{5,21},{6,22},{7,23},{8,24},{9,... | collective-permute-start | bytes 983048 | tf_op jit(solution)/shard_map/ppermute | solution.py:796
  216.5 48.4 %collective-permute-start.57 = (bf16[8,40,512]{2,1,0:T(8,128)(2,1)S(1)}, bf16[8,40,512]{2,1,0:T(8,128)(2,1)S(1)}, u32[]{:S(2)}, u32[]{:S(2)}) collective-permute-start(bf16[8,40,512]{2,1,0:T(8,128)(2,1)S(1)} %get-tuple-element.255), channel_id=1, source_target_pairs={{0,16},{1,17},{2,18},{3,19},{4,20},{5,21},{6,22},{7,23},{8,24},{9,... | collective-permute-start | bytes 983048 | tf_op jit(solution)/shard_map/ppermute | solution.py:796
  218.6 8.2 %collective-permute-start.52 = (bf16[128,1024]{1,0:T(8,128)(2,1)S(1)}, bf16[128,1024]{1,0:T(8,128)(2,1)S(1)}, u32[]{:S(2)}, u32[]{:S(2)}) collective-permute-start(bf16[128,1024]{1,0:T(8,128)(2,1)S(1)} %get-tuple-element.238), channel_id=1, source_target_pairs={{0,2},{1,3},{2,0},{3,1},{4,6},{5,7},{6,4},{7,5},{8,10},{9,11},{10,... | collective-permute-start | bytes 786440 | tf_op jit(solution)/shard_map/ppermute | solution.py:762
  219.8 45.1 %collective-permute-start.59 = (bf16[512,512]{1,0:T(8,128)(2,1)S(1)}, bf16[512,512]{1,0:T(8,128)(2,1)S(1)}, u32[]{:S(2)}, u32[]{:S(2)}) collective-permute-start(bf16[512,512]{1,0:T(8,128)(2,1)S(1)} %fold.2), channel_id=1, source_target_pairs={{0,8},{1,9},{2,10},{3,11},{4,12},{5,13},{6,14},{7,15},{8,0},{9,1},... | collective-permute-start | bytes 1572872 | tf_op jit(solution)/shard_map/ppermute | solution.py:796
  222.1 16.3 %collective-permute-start.53 = (bf16[128,1024]{1,0:T(8,128)(2,1)S(1)}, bf16[128,1024]{1,0:T(8,128)(2,1)S(1)}, u32[]{:S(2)}, u32[]{:S(2)}) collective-permute-start(bf16[128,1024]{1,0:T(8,128)(2,1)S(1)} %get-tuple-element.239), channel_id=1, source_target_pairs={{0,4},{1,5},{2,6},{3,7},{4,0},{5,1},{6,2},{7,3},{8,12},{9,13},{10,... | collective-permute-start | bytes 786440 | tf_op jit(solution)/shard_map/ppermute | solution.py:762
  225.3 21.6 %collective-permute-start.54 = (bf16[128,1024]{1,0:T(8,128)(2,1)S(1)}, bf16[128,1024]{1,0:T(8,128)(2,1)S(1)}, u32[]{:S(2)}, u32[]{:S(2)}) collective-permute-start(bf16[128,1024]{1,0:T(8,128)(2,1)S(1)} %get-tuple-element.240), channel_id=1, source_target_pairs={{0,6},{1,7},{2,4},{3,5},{4,2},{5,3},{6,0},{7,1},{8,14},{9,15},{10,... | collective-permute-start | bytes 786440 | tf_op jit(solution)/shard_map/ppermute | solution.py:762
  226.8 38.2 %collective-permute-start.58 = (bf16[8,40,512]{2,1,0:T(8,128)(2,1)S(1)}, bf16[8,40,512]{2,1,0:T(8,128)(2,1)S(1)}, u32[]{:S(2)}, u32[]{:S(2)}) collective-permute-start(bf16[8,40,512]{2,1,0:T(8,128)(2,1)S(1)} %fold.3), channel_id=1, source_target_pairs={{0,8},{1,9},{2,10},{3,11},{4,12},{5,13},{6,14},{7,15},{8,0},{9,1},... | collective-permute-start | bytes 983048 | tf_op jit(solution)/shard_map/ppermute | solution.py:796
  238.4 26.5 %collective-permute-start.56 = (bf16[64,1024]{1,0:T(8,128)(2,1)S(1)}, bf16[64,1024]{1,0:T(8,128)(2,1)S(1)}, u32[]{:S(2)}, u32[]{:S(2)}) collective-permute-start(bf16[64,1024]{1,0:T(8,128)(2,1)S(1)} %get-tuple-element.253), channel_id=1, source_target_pairs={{0,8},{1,9},{2,10},{3,11},{4,12},{5,13},{6,14},{7,15},{8,0},{9,1},... | collective-permute-start | bytes 393224 | tf_op jit(solution)/shard_map/ppermute | solution.py:762
  267.6 17.7 %all-to-all-start.1 = ((bf16[8,40,896]{2,1,0:T(8,128)(2,1)}), bf16[8,40,896]{2,1,0:T(8,128)(2,1)S(1)}, u32[]{:S(2)}, u32[]{:S(2)}) async-start(bf16[8,40,896]{2,1,0:T(8,128)(2,1)} %get-tuple-element.257), calls=%async_computation.1 | async-start | bytes 1146880 | tf_op jit(solution)/shard_map/all_to_all | solution.py:800
  271.2 10.2 %collective-permute-start.61 = (bf16[64,1024]{1,0:T(8,128)(2,1)S(1)}, bf16[64,1024]{1,0:T(8,128)(2,1)S(1)}, u32[]{:S(2)}, u32[]{:S(2)}) collective-permute-start(bf16[64,1024]{1,0:T(8,128)(2,1)S(1)} %get-tuple-element.259), channel_id=1, source_target_pairs={{0,8},{1,9},{2,10},{3,11},{4,12},{5,13},{6,14},{7,15},{8,0},{9,1},... | collective-permute-start | bytes 393224 | tf_op jit(solution)/shard_map/ppermute | solution.py:762
  271.7 9.7 %collective-permute-start.60 = (bf16[32,1024]{1,0:T(8,128)(2,1)S(1)}, bf16[32,1024]{1,0:T(8,128)(2,1)S(1)}, u32[]{:S(2)}, u32[]{:S(2)}) collective-permute-start(bf16[32,1024]{1,0:T(8,128)(2,1)S(1)} %get-tuple-element.258), channel_id=1, source_target_pairs={{0,0},{8,1},{16,2},{24,3},{1,4},{9,5},{17,6},{25,7},{2,8},{10,9},{... | collective-permute-start | bytes 196616 | tf_op jit(solution)/shard_map/ppermute | solution.py:1081
  (3 other events, 129.7 us)
